TPU v7x, 128 devices: a whole 4x4x4 slice. The times are simulated.
128 devices in a mesh: gx: 32 (over x_hi, z, y), gy: 4 (over x_lo, core).
Axes of the slice: x: 4 (x_hi: 2, x_lo: 2; x = x_hi * 2 + x_lo), y: 4, z: 4, core: 2. Of those that a mesh axis runs over, the one named last changes fastest.
Arguments:
- populations: float32 [27, 256, 128, 128], P(None, 'gx', 'gy'), may hold values from 0.49 to 1.69
- precursor: float32 [27, 64, 128, 128], P(None, 'gx', 'gy'), may hold values from 0.49 to 1.69
- pairing: int32 [32], replicated, may hold values from 0 to 31, each once
- rates: float32 [27], replicated, may hold values from 0.5 to 1.9
- loading: float32 [32], replicated, may hold values from 4 to 32
- disc_cols: int32 [512], replicated, may hold values from 0 to 32767, as said below
- disc_turb: int32 [512], replicated, may hold values from -1 to 31, as said below
Outputs:
- read: float32 [27, 256, 128, 128], P(None, 'gx', 'gy')
- disc_speed: float32 [32], replicated
Inputs may be any that keep to these rules, and one draw needn't show every extreme that they name: `disc_cols`: each turbine's used slots name 8 to 16 spanwise-adjacent columns (periodic in y) of one streamwise plane; unused slots hold column 0. `disc_turb`: every turbine id 0..31 has 8 to 16 used slots, both counts reached; -1 marks an unused slot; slots are in no particular order.
All inputs are finite; a program needn't handle non-finite values.
Results may differ from a plain program's by a relative error of at most 0.00009.
Values sent between devices are 32-bit elements; how exact they have to be, the bound alone decides.
No kernel may reach another device: no remote copies, remote signals or barrier semaphores. Data moves between devices by JAX's collectives and lax.ppermute only.
A program may use at most 128 MiB of HBM per device.

v0:
```python
import jax
import jax.numpy as jnp
import numpy as np
from jax import lax
from jax.sharding import PartitionSpec as P

FULL_PRECISION = lax.Precision.HIGHEST


def extended(cells, sides, width):
    for axis, dim in sides:
        count = lax.axis_size(axis)
        head = lax.slice_in_dim(cells, 0, width, axis=dim)
        tail = lax.slice_in_dim(cells, cells.shape[dim] - width, cells.shape[dim], axis=dim)
        cells = jnp.concatenate(
            [
                lax.ppermute(tail, axis, [(i, (i + 1) % count) for i in range(count)]),
                cells,
                lax.ppermute(head, axis, [((i + 1) % count, i) for i in range(count)]),
            ],
            axis=dim,
        )
    return cells


def lattice_tables():
    steps_one = np.array([-1.0, 0.0, 1.0])
    weight_one = np.array([1.0 / 6.0, 2.0 / 3.0, 1.0 / 6.0])
    grid_x, grid_y, grid_z = np.meshgrid(np.arange(3), np.arange(3), np.arange(3), indexing="ij")
    grid_x = grid_x.ravel()
    grid_y = grid_y.ravel()
    grid_z = grid_z.ravel()
    shift_x = steps_one[grid_x]
    shift_y = steps_one[grid_y]
    shift_z = steps_one[grid_z]
    weights = weight_one[grid_x] * weight_one[grid_y] * weight_one[grid_z]
    vander = np.array([[1.0, 1.0, 1.0], [-1.0, 0.0, 1.0], [1.0, 0.0, 1.0]])
    inverse = np.array([[0.0, -0.5, 0.5], [1.0, 0.0, -1.0], [0.0, 0.5, 0.5]])
    moment_map = np.kron(np.kron(vander, vander), vander) * weights[None, :]
    back_map = np.kron(np.kron(inverse, inverse), inverse) / weights[:, None]
    third = 1.0 / 3.0
    fringe_map = np.stack(
        [
            weights,
            weights * shift_x,
            weights * shift_y,
            weights * shift_z,
            weights * shift_x * shift_x,
            weights * shift_y * shift_y,
            weights * shift_z * shift_z,
            weights * shift_x * shift_y,
            weights * shift_x * shift_z,
            weights * shift_y * shift_z,
        ]
    )
    quad_x = shift_x * shift_x - third
    quad_y = shift_y * shift_y - third
    quad_z = shift_z * shift_z - third
    rebuild_map = np.stack(
        [
            1.0 - 1.5 * (quad_x + quad_y + quad_z),
            3.0 * shift_x,
            3.0 * shift_y,
            3.0 * shift_z,
            4.5 * quad_x,
            4.5 * quad_y,
            4.5 * quad_z,
            9.0 * shift_x * shift_y,
            9.0 * shift_x * shift_z,
            9.0 * shift_y * shift_z,
        ],
        axis=1,
    )
    tables = (shift_x, shift_y, shift_z, moment_map, back_map, fringe_map, rebuild_map)
    return tuple((jnp.asarray(table, dtype=jnp.float32) for table in tables))


def disc_profile(depth):
    heights = jnp.arange(depth).astype(jnp.float32)
    return jnp.exp(-jnp.square((heights - depth / 3.0) / (depth / 6.0)))


def relax_cells(tables, moments, rates, force):
    shift_x, shift_y, shift_z, moment_map, back_map = tables[:5]
    density = moments[0]
    velocity_x = moments[9] / density
    velocity_y = moments[3] / density
    velocity_z = moments[1] / density
    projected = (
        shift_x[:, None] * velocity_x[None, :]
        + shift_y[:, None] * velocity_y[None, :]
        + shift_z[:, None] * velocity_z[None, :]
    )
    speed_sq = velocity_x * velocity_x + velocity_y * velocity_y + velocity_z * velocity_z
    balance = density[None, :] * (
        1.0 + 3.0 * projected + 4.5 * projected * projected - 1.5 * speed_sq[None, :]
    )
    balance_moments = jnp.dot(moment_map, balance, precision=FULL_PRECISION)
    relaxed = moments - rates[:, None] * (moments - balance_moments)
    return (
        jnp.dot(back_map, relaxed, precision=FULL_PRECISION)
        + 3.0 * shift_x[:, None] * force[None, :]
    )


def body(populations, precursor, pairing, rates, loading, disc_cols, disc_turb):
    tables = lattice_tables()
    comps, width_x, width_y, depth = populations.shape
    fringe_width = precursor.shape[1]
    turbines = loading.shape[0]
    flat = populations.reshape(comps, width_x * width_y * depth)
    moments = jnp.dot(tables[3], flat, precision=FULL_PRECISION)
    velocity_x = moments[9] / moments[0]
    profile = disc_profile(depth)
    along_y = width_y * lax.axis_size("gy")
    tile_x = lax.axis_index("gx")
    tile_y = lax.axis_index("gy")
    local_x = disc_cols // along_y - tile_x * width_x
    local_y = disc_cols % along_y - tile_y * width_y
    owned = (
        (disc_turb >= 0)
        & (local_x >= 0)
        & (local_x < width_x)
        & (local_y >= 0)
        & (local_y < width_y)
    )
    local_cell = jnp.where(owned, local_x * width_y + local_y, 0)
    columns = velocity_x.reshape(width_x * width_y, depth)[local_cell]
    row_values = jnp.where(owned, jnp.dot(columns, profile, precision=FULL_PRECISION), 0.0)
    owner_table = (disc_turb[None, :] == jnp.arange(turbines, dtype=jnp.int32)[:, None]).astype(
        jnp.float32
    )
    partial_totals = jnp.dot(owner_table, row_values, precision=FULL_PRECISION)
    totals = lax.psum(partial_totals, ("gx", "gy"))
    counts = jnp.sum(owner_table, axis=1)
    disc_speed = totals / (counts * jnp.sum(profile))
    thrust = 0.5 * loading * disc_speed * jnp.abs(disc_speed)
    row_thrust = jnp.dot(thrust, owner_table, precision=FULL_PRECISION)
    placed = (
        (jnp.arange(width_x * width_y, dtype=jnp.int32)[:, None] == local_cell[None, :])
        & owned[None, :]
    ).astype(jnp.float32)
    column_force = jnp.dot(placed, row_thrust, precision=FULL_PRECISION)
    force = -(column_force[:, None] * profile[None, :]).reshape(width_x * width_y * depth)
    post = relax_cells(tables, moments, rates, force).reshape(comps, width_x, width_y, depth)
    source_tile = pairing[tile_x]
    wanted = source_tile * fringe_width + jnp.arange(fringe_width, dtype=jnp.int32)
    piece = lax.all_gather(precursor, "gx", axis=1, tiled=True)
    have = jnp.arange(piece.shape[1], dtype=jnp.int32)
    chosen = (wanted[:, None] == have[None, :]).astype(jnp.float32)
    chosen_pops = jnp.einsum("pr,kryz->kpyz", chosen, piece, precision=FULL_PRECISION)
    selected = jnp.dot(
        tables[5],
        chosen_pops.reshape(comps, fringe_width * width_y * depth),
        precision=FULL_PRECISION,
    )
    rebuilt = jnp.dot(
        tables[6], selected.reshape(10, fringe_width * width_y * depth), precision=FULL_PRECISION
    )
    rebuilt = rebuilt.reshape(comps, fringe_width, width_y, depth)
    blend = (0.5 / (jnp.arange(fringe_width).astype(jnp.float32) + 1.0))[None, :, None, None]
    head = (1.0 - blend) * post[:, :fringe_width] + blend * rebuilt
    post = jnp.concatenate([head, post[:, fringe_width:]], axis=1)
    pieces = []
    padded = extended(post, (("gx", 1), ("gy", 2)), 1)
    for slot in range(27):
        step_x = slot // 9 - 1
        step_y = slot // 3 % 3 - 1
        pieces.append(
            padded[slot, 1 - step_x : 1 - step_x + width_x, 1 - step_y : 1 - step_y + width_y]
        )
    finished = []
    for slot in range(27):
        step_z = slot % 3 - 1
        moved = pieces[slot]
        if step_z == 1:
            moved = jnp.concatenate([post[26 - slot][:, :, :1], moved[:, :, :-1]], axis=2)
        elif step_z == -1:
            moved = jnp.concatenate([moved[:, :, 1:], post[26 - slot][:, :, -1:]], axis=2)
        finished.append(moved)
    return (jnp.stack(finished), disc_speed)


def solution(mesh):
    in_specs = (P(None, "gx", "gy", None), P(None, "gx", "gy", None), P(), P(), P(), P(), P())
    out_specs = (P(None, "gx", "gy", None), P())
    return jax.shard_map(body, mesh=mesh, in_specs=in_specs, out_specs=out_specs, check_vma=False)
```

profile of v0, /device:TPU:1, one launch (start us, length us, event | category | flops | bytes accessed | tf_op | source)
XLA Modules:
  0.0 319.0 jit_solution(4355309923791451909)
XLA Ops:
  7.2 2.2 copy.22
  9.4 2.4 pad.213
  11.9 4.4 %copy.26 = f32[4,8,256,128]{3,1,2,0:T(8,128)} copy(f32[4,8,256,128]{3,2,1,0:T(8,128)S(1)} %bitcast.220) | data formatting | bytes 8388608
  16.4 5.4 %fusion.80 = f32[27,32768]{1,0:T(8,128)S(1)} fusion(f32[27,27]{1,0:T(8,128)S(1)} %copy-done.5, f32[27,32768]{1,0:T(8,128)} %bitcast.218), kind=kOutput, calls=%fused_computation.182 | convolution fusion | flops 286654464 | bytes 7080804 | tf_op jit(solution)/shard_map/dot_general | solution.py:112
  21.8 2.0 copy-done.2
  23.7 0.5 add_multiply_fusion
  24.3 1.0 gather_fusion
  25.3 0.3 fusion.66
  25.8 75.3 %psum.7 = f32[32]{0:T(128)S(1)} all-reduce(f32[32]{0:T(128)S(1)} %convolution_bitcast_fusion.1), channel_id=1, replica_groups=mesh['gx'=32,'gy'=4] {'gx','gy'}, use_global_device_ids=true, to_apply=%region_0.1 | all-reduce | flops 32 | bytes 256 | tf_op jit(solution)/shard_map/psum | solution.py:134
  101.1 0.6 fusion.73
  101.9 0.7 multiply_divide_fusion
  102.7 0.3 fusion.31
  103.1 7.7 %fusion.1 = f32[27,32768]{1,0:T(8,128)S(1)} fusion(f32[27,32768]{1,0:T(8,128)} %copy-done.2, f32[27,27]{1,0:T(8,128)S(1)} %copy-done.5, f32[32768]{0:T(1024)S(1)} %bitcast.250, f32[32768]{0:T(1024)S(1)} %bitcast.252, f32[27]{0:T(128)S(1)} %copy-done.15, f32[32768]{0:T(1024)S(1)} %bitcast.251, f32[27]{0:T(128)S(1)} %copy-done.16, f32[32768]{0:T(1024)S(1)} %bitcast.217, ...), kind=kOutput, calls=%fused_computation.4 | convolution fusion | flops 299925504 | bytes 7736596 | tf_op jit(solution)/shard_map/dot_general | solution.py:98
  111.0 4.1 %convolution_add_fusion = f32[27,32768]{1,0:T(8,128)S(1)} fusion(f32[27,27]{1,0:T(8,128)S(1)} %copy-done.4, f32[27,32768]{1,0:T(8,128)S(1)} %fusion.1, f32[32768]{0:T(1024)S(1)} %negate_bitcast_fusion, f32[27]{0:T(128)S(1)} %copy-done.10), kind=kOutput, calls=%fused_computation.1 | convolution fusion | flops 288423936 | bytes 7211984 | tf_op jit(solution)/shard_map/dot_general | solution.py:101
  115.1 0.7 copy.27
  115.9 0.4 slice.431
  116.3 1.8 copy-done
  118.1 0.3 collective-permute-start
  118.4 0.7 dynamic_slice.3
  119.8 124.4 %all-gather.2.cloned.1.call-done = f32[27,64,32,128]{3,2,0,1:T(8,128)} async-done(((f32[27,2,32,128]{3,2,0,1:T(8,128)}), f32[27,64,32,128]{3,2,0,1:T(8,128)}) %all-gather.2.cloned.1.call-update) | async-done | bytes 28311568 | tf_op jit(solution)/shard_map/all_gather | solution.py:148
  244.2 31.6 %fusion.26 = f32[27,2,32,128]{3,1,2,0:T(2,128)S(1)} fusion(f32[27,64,32,128]{3,2,0,1:T(8,128)} %all-gather.2.cloned.1.call-done, s32[2]{0:T(128)S(1)} %iota_add_fusion), kind=kOutput, calls=%fused_computation.29 | convolution fusion | flops 169869440 | bytes 29196296 | tf_op jit(solution)/shard_map/pr,kryz->kpyz/dot_general | solution.py:151
  276.1 0.6 copy.28
  276.7 0.7 fusion.81
  277.4 1.0 fusion.82
  278.7 0.3 fusion.29
  279.0 10.8 %collective-permute-start.1 = (f32[27,1,32,128]{3,2,1,0:T(8,128)S(1)}, f32[27,1,32,128]{3,2,1,0:T(8,128)S(1)}, u32[]{:S(2)}, u32[]{:S(2)}) collective-permute-start(f32[27,1,32,128]{3,2,1,0:T(8,128)S(1)} %slice.394), channel_id=1, source_target_pairs={{4,0},{8,4},{12,8},{16,12},{20,16},{24,20},{28,24},{32,28},{36,32}... | collective-permute-start | bytes 1327112 | tf_op jit(solution)/shard_map/ppermute | solution.py:19
  289.8 0.4 slice.393
  290.2 8.0 %collective-permute-done.1 = f32[27,1,32,128]{3,2,1,0:T(8,128)S(1)} collective-permute-done((f32[27,1,32,128]{3,2,1,0:T(8,128)S(1)}, f32[27,1,32,128]{3,2,1,0:T(8,128)S(1)}, u32[]{:S(2)}, u32[]{:S(2)}) %collective-permute-start.1) | collective-permute-done | bytes 442400 | tf_op jit(solution)/shard_map/ppermute | solution.py:19
  298.4 3.1 collective-permute-start.3
  301.5 2.6 collective-permute-done.3
  304.1 1.8 collective-permute-done.2
  310.4 1.8 copy-done.8
  (100 shorter events, 5.6 us)
Async XLA Ops:
  7.2 237.0 %all-gather.2.cloned.1.call-start = ((), (), s32[]{:S(2)}) async-start(), calls=%async_computation | async-start | bytes 29196288 | tf_op jit(solution)/shard_map/all_gather | solution.py:148
  11.9 4.4 %copy-start.7 = (s32[512]{0:T(512)S(1)}, s32[512]{0:T(512)}, u32[]{:S(2)}) copy-start(s32[512]{0:T(512)} %param.20) | copy-start | bytes 6148
  11.9 4.4 %copy-start.9 = (s32[512]{0:T(512)S(1)}, s32[512]{0:T(512)}, u32[]{:S(2)}) copy-start(s32[512]{0:T(512)} %param.19) | copy-start | bytes 6148
  11.9 4.5 %copy-start.5 = (f32[27,27]{1,0:T(8,128)S(1)}, f32[27,27]{1,0:T(8,128)}, u32[]{:S(2)}) copy-start(f32[27,27]{1,0:T(8,128)} %constant.89.clone) | copy-start | bytes 8752
  21.7 2.0 copy-start.2
  23.7 78.8 %copy-start.12 = (f32[32]{0:T(128)S(1)}, f32[32]{0:T(128)}, u32[]{:S(2)}) copy-start(f32[32]{0:T(128)} %param.18) | copy-start | bytes 388
  23.7 79.3 %copy-start.13 = (f32[27]{0:T(128)S(1)}, f32[27]{0:T(128)}, u32[]{:S(2)}) copy-start(f32[27]{0:T(128)} %param.17) | copy-start | bytes 328
  23.7 79.3 %copy-start.15 = (f32[27]{0:T(128)S(1)}, f32[27]{0:T(128)}, u32[]{:S(2)}) copy-start(f32[27]{0:T(128)} %constant.88.clone) | copy-start | bytes 328
  23.7 79.4 %copy-start.16 = (f32[27]{0:T(128)S(1)}, f32[27]{0:T(128)}, u32[]{:S(2)}) copy-start(f32[27]{0:T(128)} %constant.87.clone) | copy-start | bytes 328
  23.7 79.4 %copy-start.17 = (f32[27]{0:T(128)S(1)}, f32[27]{0:T(128)}, u32[]{:S(2)}) copy-start(f32[27]{0:T(128)} %constant.86.clone) | copy-start | bytes 328
  102.6 8.3 %copy-start.11 = (f32[32]{0:T(128)}, f32[32]{0:T(128)S(1)}, u32[]{:S(2)}) copy-start(f32[32]{0:T(128)S(1)} %multiply_divide_fusion) | copy-start | bytes 388
  103.1 7.9 %copy-start.4 = (f32[27,27]{1,0:T(8,128)S(1)}, f32[27,27]{1,0:T(8,128)}, u32[]{:S(2)}) copy-start(f32[27,27]{1,0:T(8,128)} %constant.90.clone) | copy-start | bytes 8752
  103.1 7.9 %copy-start.10 = (f32[27]{0:T(128)S(1)}, f32[27]{0:T(128)}, u32[]{:S(2)}) copy-start(f32[27]{0:T(128)} %constant.95) | copy-start | bytes 328
  115.9 2.5 copy-start.14
  116.3 1.8 copy-start
  118.1 172.1 %collective-permute-start = (f32[27,1,32,128]{3,2,1,0:T(8,128)S(1)}, f32[27,1,32,128]{3,2,1,0:T(8,128)S(1)}, u32[]{:S(2)}, u32[]{:S(2)}) collective-permute-start(f32[27,1,32,128]{3,2,1,0:T(8,128)S(1)} %slice.391), channel_id=1, source_target_pairs={{0,4},{4,8},{8,12},{12,16},{16,20},{20,24},{24,28},{28,32},{32,36}... | collective-permute-start | bytes 1327112 | tf_op jit(solution)/shard_map/ppermute | solution.py:17
  275.8 0.9 copy-start.6
  275.8 1.6 copy-start.3
  276.7 2.0 copy-start.1
  279.0 19.2 %collective-permute-start.1 = (f32[27,1,32,128]{3,2,1,0:T(8,128)S(1)}, f32[27,1,32,128]{3,2,1,0:T(8,128)S(1)}, u32[]{:S(2)}, u32[]{:S(2)}) collective-permute-start(f32[27,1,32,128]{3,2,1,0:T(8,128)S(1)} %slice.394), channel_id=1, source_target_pairs={{4,0},{8,4},{12,8},{16,12},{20,16},{24,20},{28,24},{32,28},{36,32}... | collective-permute-start | bytes 1327112 | tf_op jit(solution)/shard_map/ppermute | solution.py:19
  298.4 5.8 %collective-permute-start.3 = (f32[27,10,1,128]{3,2,1,0:T(1,128)S(1)}, f32[27,10,1,128]{3,2,1,0:T(1,128)S(1)}, u32[]{:S(2)}, u32[]{:S(2)}) collective-permute-start(f32[27,10,1,128]{3,2,1,0:T(1,128)S(1)} %get-tuple-element.27), channel_id=1, source_target_pairs={{0,1},{1,2},{2,3},{3,0},{4,5},{5,6},{6,7},{7,4},{8,9},{9,10},{10,1... | collective-permute-start | bytes 414728 | tf_op jit(solution)/shard_map/ppermute | solution.py:17
  301.5 4.5 %collective-permute-start.2 = (f32[27,10,1,128]{3,2,1,0:T(1,128)S(1)}, f32[27,10,1,128]{3,2,1,0:T(1,128)S(1)}, u32[]{:S(2)}, u32[]{:S(2)}) collective-permute-start(f32[27,10,1,128]{3,2,1,0:T(1,128)S(1)} %get-tuple-element.28), channel_id=1, source_target_pairs={{1,0},{2,1},{3,2},{0,3},{5,4},{6,5},{7,6},{4,7},{9,8},{10,9},{11,1... | collective-permute-start | bytes 414728 | tf_op jit(solution)/shard_map/ppermute | solution.py:19
  310.4 1.8 copy-start.8
Sparse Core Ops, SparseCore 0:
  11.0 233.1 all-gather.1
where the time goes:
time: 320 us; the launch traced here: 319 us
  waiting for transfers between devices  137 us (43%)
  blocking collectives  75.3 us (24%)
  matrix products  51.5 us (16%)
  local copies, waits for them, and re-layouts  20.7 us (6%)
  between operations  15.5 us (5%)
  starting transfers between devices  14.2 us (4%)
  other arithmetic  4.99 us (2%)
    all_gather x1, waiting for transfers between devices, body(): piece = lax.all_gather(precursor, 'gx', axis=1, tiled=True)  124 us
    psum x1, blocking collectives, body(): totals = lax.psum(partial_totals, ('gx', 'gy'))  75.3 us
    dot_general x1, matrix products, body(): jnp.einsum('pr,kryz->kpyz', chosen, piece, precision=FULL_PRECISION)  31.6 us
    unnamed x45, local copies, waits for them, and re-layouts  16.8 us
    ppermute x2, starting transfers between devices, extended(): lax.ppermute(head, axis, [((i + 1) % count, i) for i in range(count)])  10.8 us
    ppermute x2, waiting for transfers between devices, extended(): lax.ppermute(head, axis, [((i + 1) % count, i) for i in range(count)])  9.82 us
    dot_general x1, matrix products, relax_cells(): balance_moments = jnp.dot(moment_map, balance, precision=FULL_PRECISION)  7.71 us
  transfers between devices with their start and end apart: 5, of which 4 were waited for; matrix products, arithmetic and copies ran while one was open for 20% of the time, Pallas kernels for 0%

commit v1 on v0

v1 whole, which is shorter than its diff:
```python
import jax
import jax.numpy as jnp
import numpy as np
from jax import lax
from jax.experimental import pallas as pl
from jax.experimental.pallas import tpu as pltpu
from jax.sharding import PartitionSpec as P

GX, GY = 32, 4
NDEV = GX * GY
XW, YW, Z = 8, 32, 128
NY_ALL, NX_ALL = 128, 256
SLOTS = 512
TURBINES = 32
F32 = jnp.float32

OWN, NEXT, LO_OWN, HI_OWN, LO_NEXT, HI_NEXT, DISC, CORNER = 0, 80, 104, 107, 110, 111, 112, 113
CORNERS = ((-1, -1), (-1, 1), (1, -1), (1, 1))
W_ROWS = 360
BLEND = (0.5, 0.25)

HEIGHTS = np.arange(Z).astype(np.float32)
PROFILE_SUM = float(np.sum(np.exp(-np.square((np.arange(Z) - Z / 3.0) / (Z / 6.0)))))


def slot(cx, cy, cz):
    return 9 * (cx + 1) + 3 * (cy + 1) + (cz + 1)


def profile_row():
    heights = lax.broadcasted_iota(jnp.int32, (8, Z), 1).astype(F32)
    return jnp.exp(-jnp.square((heights - Z / 3.0) * (6.0 / Z)))


def forward(g):
    for stride in (1, 3, 9):
        out = list(g)
        for i in range(27):
            if (i // stride) % 3 == 0:
                a, b, c = g[i], g[i + stride], g[i + 2 * stride]
                s = c + a
                out[i] = s + 4.0 * b
                out[i + stride] = c - a
                out[i + 2 * stride] = s
        g = out
    return g


def backward(m):
    for stride in (9, 3, 1):
        out = list(m)
        for i in range(27):
            if (i // stride) % 3 == 0:
                a, b, c = m[i], m[i + stride], m[i + 2 * stride]
                out[i] = c - b
                out[i + stride] = 0.5 * (a - c)
                out[i + 2 * stride] = c + b
        m = out
    return m


def collide(g, rates):
    m = forward(g)
    density = m[0] * (1.0 / 216.0)
    inv = 1.0 / m[0]
    u = (m[9] * inv, m[3] * inv, m[1] * inv)
    j = (m[9] * (1.0 / 216.0), m[3] * (1.0 / 216.0), m[1] * (1.0 / 216.0))
    ju = {}
    for a in range(3):
        for b in range(a, 3):
            ju[(a, b)] = j[a] * u[b]
    out = []
    for i in range(27):
        order = (i // 9, i // 3 % 3, i % 3)
        ones = [d for d in range(3) if order[d] == 1]
        twos = [d for d in range(3) if order[d] == 2]
        if i in (0, 1, 3, 9):
            out.append(m[i] * 0.125)
            continue
        r = rates(i)
        keep = m[i] * ((1.0 - r) * 0.125)
        if len(ones) == 3:
            out.append(keep)
            continue
        scale = r * (27.0 / 3.0 ** len(twos))
        if len(ones) == 0:
            eq = ju[(twos[0], twos[0])]
            for d in twos[1:]:
                eq = eq + ju[(d, d)]
            eq = density + 3.0 * eq
        elif len(ones) == 1:
            eq = j[ones[0]]
        else:
            eq = ju[(ones[0], ones[1])]
        out.append(keep + eq * scale)
    return backward(out)


def z_stream(p, lane):
    out = []
    for i in range(27):
        cz = i % 3 - 1
        if cz == 0:
            out.append(p[i])
        elif cz == 1:
            out.append(jnp.where(lane == 0, p[26 - i], pltpu.roll(p[i], 1, 1)))
        else:
            out.append(jnp.where(lane == Z - 1, p[26 - i], pltpu.roll(p[i], Z - 1, 1)))
    return out


def precursor_coefficients(g):
    m = forward(g)
    rho, jx, jy, jz = m[0], m[9], m[3], m[1]
    xx, yy, zz, xy, xz, yz = m[18], m[6], m[2], m[12], m[10], m[4]
    third = rho * (1.0 / 3.0)
    pxx, pyy, pzz = xx - third, yy - third, zz - third
    s = 1.0 / 216.0
    k0 = (rho - 1.5 * (pxx + pyy + pzz)) * s
    return [k0, jx * (3 * s), jy * (3 * s), jz * (3 * s), pxx * (4.5 * s), pyy * (4.5 * s), pzz * (4.5 * s),
            xy * (9 * s), xz * (9 * s), yz * (9 * s)]


def next_coefficients(c):
    return [c[0] - c[1] + c[4], c[2] - c[7], c[3] - c[8], c[5], c[6], c[9]]


def rebuild_next(c):
    out = []
    for cy in (-1, 0, 1):
        base = c[0] + (cy * c[1] + c[3] if cy else 0.0)
        lin = c[2] + cy * c[5] if cy else c[2]
        for cz in (-1, 0, 1):
            out.append(base + cz * lin + c[4] if cz else base)
    return out


def rebuild(c):
    out = []
    for cx in (-1, 0, 1):
        base = c[0] + cx * c[1] + c[4] if cx else c[0]
        liny = c[2] + cx * c[7] if cx else c[2]
        linz = c[3] + cx * c[8] if cx else c[3]
        out += rebuild_next([base, liny, linz, c[5], c[6], c[9]])
    return out


K1_PLANES = 2


def first_kernel(rates_ref, pop_ref, pre_ref, cols_ref, turb_ref, send_ref, w_ref, corner_scr, acc_scr):
    step = pl.program_id(0)
    gx = lax.axis_index("gx")
    gy = lax.axis_index("gy")

    @pl.when(step == 0)
    def _():
        rows = lax.broadcasted_iota(jnp.int32, (W_ROWS, SLOTS), 0)
        lo = rows - 320
        main = rows < 320
        xx = jnp.where(main, rows >> 5, jnp.where(lo < 16, lo, lo - 16))
        yy = jnp.where(main, rows & 31, jnp.where(lo < 16, -1, YW))
        col = ((gx * XW + xx - 1) & (NX_ALL - 1)) * NY_ALL + ((gy * YW + yy) & (NY_ALL - 1))
        valid = main | ((lo & 15) < 10)
        hit = ((col == cols_ref[...]) & valid & (lo < 32)) | (lo >= 32)
        owner = lax.broadcasted_iota(jnp.int32, (128, SLOTS), 0) == turb_ref[...]
        w_ref[...] = lax.dot_general(
            jnp.where(hit, 1.0, 0.0).astype(jnp.bfloat16),
            jnp.where(owner, 1.0, 0.0).astype(jnp.bfloat16),
            (((1,), (1,)), ((), ())), preferred_element_type=F32)
        acc_scr[...] = jnp.zeros_like(acc_scr)
        send_ref[LO_OWN:, :, :] = jnp.zeros((NDEV - LO_OWN, 8, Z), F32)
        for p in range(2):
            for q in range(4):
                g = [pre_ref[i, p, 8 * q:8 * q + 8, :] for i in range(27)]
                c = precursor_coefficients(g)
                for k in range(10):
                    send_ref[OWN + (2 * k + p) * 4 + q, :, :] = c[k]
                    row = 2 * k + p
                    if q == 3:
                        send_ref[LO_OWN + row // 8, row % 8:row % 8 + 1, :] = c[k][7:8, :]
                    if q == 0:
                        send_ref[HI_OWN + row // 8, row % 8:row % 8 + 1, :] = c[k][0:1, :]
                if p == 0:
                    n = next_coefficients(c)
                    for k in range(6):
                        send_ref[NEXT + 4 * k + q, :, :] = n[k]
                        if q == 3:
                            send_ref[LO_NEXT, k:k + 1, :] = n[k][7:8, :]
                        if q == 0:
                            send_ref[HI_NEXT, k:k + 1, :] = n[k][0:1, :]
        corner_scr[...] = jnp.ones_like(corner_scr)
        for i in range(27):
            corner_scr[i, 0:1, :] = pop_ref[i, 0, 0:1, :]
            corner_scr[i, 1:2, :] = pop_ref[i, 0, YW - 1:YW, :]

    profile = profile_row()
    for a in range(K1_PLANES):
        for q in range(4):
            rows = slice(8 * q, 8 * q + 8)
            part = []
            for cx in range(3):
                total = None
                for cy in range(3):
                    b = 9 * cx + 3 * cy
                    t = pop_ref[b, a, rows, :] + pop_ref[b + 2, a, rows, :] + 4.0 * pop_ref[b + 1, a, rows, :]
                    t = 4.0 * t if cy == 1 else t
                    total = t if total is None else total + t
                part.append(total)
            ends = part[0] + part[2]
            ux = (part[2] - part[0]) / (ends + 4.0 * part[1])
            sums = jnp.sum(ux * profile, axis=1, keepdims=True)
            base = pl.multiple_of((step * K1_PLANES + a + 1) * YW, YW) + 8 * q
            acc_scr[...] += sums * w_ref[pl.ds(base, 8), :]

    @pl.when(step == XW // K1_PLANES - 1)
    def _():
        a = K1_PLANES - 1
        for i in range(27):
            corner_scr[i, 2:3, :] = pop_ref[i, a, 0:1, :]
            corner_scr[i, 3:4, :] = pop_ref[i, a, YW - 1:YW, :]
        lane = lax.broadcasted_iota(jnp.int32, (8, Z), 1)
        post = z_stream(collide([corner_scr[i] for i in range(27)], lambda i: rates_ref[i]), lane)
        for n, (cx, cy) in enumerate(CORNERS):
            row = 2 * (cx > 0) + (cy > 0)
            for cz in (-1, 0, 1):
                send_ref[CORNER + n, cz + 1:cz + 2, :] = post[slot(cx, cy, cz)][row:row + 1, :]
        send_ref[DISC, 0:1, :] = jnp.sum(acc_scr[...], axis=0, keepdims=True)


def before_exchange(rates, populations, precursor, cols, turb):
    return pl.pallas_call(
        first_kernel,
        grid=(XW // K1_PLANES,),
        in_specs=[
            pl.BlockSpec(memory_space=pltpu.SMEM),
            pl.BlockSpec((27, K1_PLANES, YW, Z), lambda x: (0, x, 0, 0)),
            pl.BlockSpec((27, 2, YW, Z), lambda x: (0, 0, 0, 0)),
            pl.BlockSpec((1, SLOTS), lambda x: (0, 0)),
            pl.BlockSpec((1, SLOTS), lambda x: (0, 0)),
        ],
        out_specs=[
            pl.BlockSpec((NDEV, 8, Z), lambda x: (0, 0, 0)),
            pl.BlockSpec((W_ROWS, 128), lambda x: (0, 0)),
        ],
        out_shape=[jax.ShapeDtypeStruct((NDEV, 8, Z), F32), jax.ShapeDtypeStruct((W_ROWS, 128), F32)],
        scratch_shapes=[pltpu.VMEM((27, 8, Z), F32), pltpu.VMEM((8, 128), F32)],
        name="before_exchange",
    )(rates, populations, precursor, cols, turb)


def collide_kernel(rates_ref, pop_ref, out_ref, xm_ref, xp_ref, ym_ref, yp_ref):
    x = pl.program_id(0)
    lane = lax.broadcasted_iota(jnp.int32, (8, Z), 1)
    for q in range(4):
        rows = slice(8 * q, 8 * q + 8)
        post = collide([pop_ref[i, 0, rows, :] for i in range(27)], lambda i: rates_ref[i])
        post = z_stream(post, lane)
        for i in range(27):
            out_ref[i, 0, rows, :] = post[i]
        for cx in (-1, 0, 1):
            for cz in (-1, 0, 1):
                k = 3 * (cx + 1) + cz + 1
                if q == 0:
                    ym_ref[k, pl.ds(x, 1), :] = post[slot(cx, -1, cz)][0:1, :]
                if q == 3:
                    yp_ref[k, pl.ds(x, 1), :] = post[slot(cx, 1, cz)][7:8, :]

    @pl.when(x == 0)
    def _():
        for k in range(9):
            xm_ref[k, :, :] = out_ref[k, 0, :, :]

    @pl.when(x == XW - 1)
    def _():
        for k in range(9):
            xp_ref[k, :, :] = out_ref[18 + k, 0, :, :]


def collision(rates, populations):
    whole = lambda x: (0, 0, 0)
    return pl.pallas_call(
        collide_kernel,
        grid=(XW,),
        in_specs=[
            pl.BlockSpec(memory_space=pltpu.SMEM),
            pl.BlockSpec((27, 1, YW, Z), lambda x: (0, x, 0, 0)),
        ],
        out_specs=[
            pl.BlockSpec((27, 1, YW, Z), lambda x: (0, x, 0, 0)),
            pl.BlockSpec((9, YW, Z), whole),
            pl.BlockSpec((9, YW, Z), whole),
            pl.BlockSpec((9, XW, Z), whole),
            pl.BlockSpec((9, XW, Z), whole),
        ],
        out_shape=[
            jax.ShapeDtypeStruct((27, XW, YW, Z), F32),
            jax.ShapeDtypeStruct((9, YW, Z), F32),
            jax.ShapeDtypeStruct((9, YW, Z), F32),
            jax.ShapeDtypeStruct((9, XW, Z), F32),
            jax.ShapeDtypeStruct((9, XW, Z), F32),
        ],
        name="collision",
    )(rates, populations)


def route_kernel(pairing_ref, got_ref, send_ref):
    me = lax.axis_index("gx") * GY + lax.axis_index("gy")
    is_next = ((me >= NEXT) & (me < LO_OWN)) | (me == LO_NEXT) | (me == HI_NEXT)
    corner = me - CORNER
    is_corner = (corner >= 0) & (corner < 4)
    low = ((me >= LO_OWN) & (me < HI_OWN)) | (me == LO_NEXT)
    high = ((me >= HI_OWN) & (me < LO_NEXT)) | (me == HI_NEXT)
    from_x = jnp.where(corner < 2, 1, -1)
    from_y = jnp.where(is_corner, jnp.where((corner & 1) == 0, 1, -1), jnp.where(low, -1, jnp.where(high, 1, 0)))
    ahead = jnp.where(is_next, 1, 0)
    lanes = [(t + from_y) & (GY - 1) for t in range(GY)]

    @pl.when(me != DISC)
    def _():
        for d in range(GX):
            tile = pairing_ref[(d + ahead) & (GX - 1)]
            tile = jnp.where(is_corner, (d + from_x) & (GX - 1), tile) * GY
            for t in range(GY):
                send_ref[d * GY + t, :, :] = got_ref[tile + lanes[t], :, :]

    @pl.when(me == DISC)
    def _():
        total = got_ref[0, :, :]
        for n in range(1, NDEV):
            total = total + got_ref[n, :, :]
        for n in range(NDEV):
            send_ref[n, :, :] = total


def route(pairing, got):
    return pl.pallas_call(
        route_kernel,
        in_specs=[pl.BlockSpec(memory_space=pltpu.SMEM), pl.BlockSpec(memory_space=pltpu.VMEM)],
        out_specs=pl.BlockSpec(memory_space=pltpu.VMEM),
        out_shape=jax.ShapeDtypeStruct((NDEV, 8, Z), F32),
        name="route",
    )(pairing, got)


def last_kernel(got_ref, w_ref, loading_ref, r_ref, xm_ref, xp_ref, ym_ref, yp_ref, out_ref, speed_ref,
                rp, force, load_scr, lo_scr, hi_scr, yp_scr, ym_scr):
    x = pl.program_id(0)
    lane = lax.broadcasted_iota(jnp.int32, (8, Z), 1)
    profile = profile_row()
    up = jnp.where(lane == 0, -profile, pltpu.roll(profile, 1, 1))
    down = jnp.where(lane == Z - 1, -profile, pltpu.roll(profile, Z - 1, 1))
    along = (3.0 * down, 3.0 * profile, 3.0 * up)

    def pushed(value, i, f):
        cx = i // 9 - 1
        if cx == 0:
            return value
        term = f * along[i % 3]
        return value + term if cx > 0 else value - term

    def pushes(f):
        return [f * a for a in along]

    def push(value, i, fs):
        cx = i // 9 - 1
        return value if cx == 0 else (value + fs[i % 3] if cx > 0 else value - fs[i % 3])

    @pl.when(x == 0)
    def _():
        load_scr[...] = jnp.zeros_like(load_scr)
        load_scr[0:1, 0:TURBINES] = loading_ref[...]
        counts = w_ref[352:360, :]
        totals = jnp.broadcast_to(got_ref[DISC, 0:1, :], (8, 128))
        k = lax.broadcasted_iota(jnp.int32, (8, 128), 1)
        speed = jnp.where(k < TURBINES, totals / (jnp.where(k < TURBINES, counts, 1.0) * PROFILE_SUM), 0.0)
        speed_ref[...] = speed[0:1, 0:TURBINES]
        thrust = (0.5 * jnp.broadcast_to(load_scr[0:1, :], (8, 128))) * speed * jnp.abs(speed)
        force[...] = -lax.dot_general(
            w_ref[0:352, :] * thrust[0:1, :], jnp.ones((128, Z), F32), (((1,), (0,)), ((), ())),
            precision=lax.Precision.HIGHEST, preferred_element_type=F32)
        for scr, tile, nxt, halo, frow, cy, out in (
            (lo_scr, LO_OWN, LO_NEXT, yp_ref, 320, 1, yp_scr),
            (hi_scr, HI_OWN, HI_NEXT, ym_ref, 336, -1, ym_scr),
        ):
            scr[...] = jnp.zeros_like(scr)
            for c in range(10):
                r = 2 * c
                scr[c, 0:2, :] = got_ref[tile + r // 8, r % 8:r % 8 + 2, :]
            built = rebuild([scr[c] for c in range(10)])
            ahead = rebuild_next([got_ref[nxt, c:c + 1, :] for c in range(6)])
            row = lax.broadcasted_iota(jnp.int32, (8, Z), 0)
            blend = jnp.where(row == 0, BLEND[0], jnp.where(row == 1, BLEND[1], 0.0))
            f = force[frow + 1:frow + 9, :]
            fs = pushes(f)
            for cx in (-1, 0, 1):
                for cz in (-1, 0, 1):
                    k = 3 * (cx + 1) + cz + 1
                    i = slot(cx, cy, cz)
                    b = built[i]
                    b = b if cz == 0 else pltpu.roll(b, cz % Z, 1)
                    out[k, 1:9, :] = (1.0 - blend) * push(halo[k], i, fs) + blend * b
            for cz in (-1, 0, 1):
                i = slot(1, cy, cz)
                n = CORNERS.index((1, cy))
                out[6 + cz + 1, 0:1, :] = got_ref[CORNER + n, cz + 1:cz + 2, :] + (
                    force[frow:frow + 1, :] * along[cz + 1][0:1, :])
                n = CORNERS.index((-1, cy))
                value = got_ref[CORNER + n, cz + 1:cz + 2, :] - force[frow + 9:frow + 10, :] * along[cz + 1][0:1, :]
                b = ahead[3 * (cy + 1) + cz + 1]
                b = b if cz == 0 else pltpu.roll(jnp.broadcast_to(b, (8, Z)), cz % Z, 1)[0:1, :]
                out[cz + 1, 9:10, :] = (1.0 - BLEND[0]) * value + BLEND[0] * b
        for q in range(4):
            rows = slice(8 * q, 8 * q + 8)
            into = slice(8 * q + 8, 8 * q + 16)
            fs = pushes(force[rows, :])
            for k in range(9):
                rp[18 + k, 0, into, :] = push(xp_ref[k, rows, :], 18 + k, fs)
            for p in range(2):
                c = [got_ref[OWN + (2 * k + p) * 4 + q, :, :] for k in range(10)]
                built = z_stream(rebuild(c), lane)
                fs = pushes(force[YW * (p + 1) + 8 * q:YW * (p + 1) + 8 * q + 8, :])
                for i in range(27):
                    rp[i, p + 1, into, :] = (1.0 - BLEND[p]) * push(r_ref[i, p, rows, :], i, fs) + BLEND[p] * built[i]

    @pl.when((x >= 1) & (x < XW - 1))
    def _():
        for q in range(4):
            rows = slice(8 * q, 8 * q + 8)
            into = slice(8 * q + 8, 8 * q + 16)
            fs = pushes(force[pl.ds(pl.multiple_of((x + 2) * YW, YW) + 8 * q, 8), :])
            for i in range(27):
                rp[i, x + 2, into, :] = push(r_ref[i, x + 1, rows, :], i, fs)

    @pl.when(x == XW - 1)
    def _():
        for q in range(4):
            rows = slice(8 * q, 8 * q + 8)
            into = slice(8 * q + 8, 8 * q + 16)
            fs = pushes(force[YW * (XW + 1) + 8 * q:YW * (XW + 1) + 8 * q + 8, :])
            built = rebuild_next([got_ref[NEXT + 4 * k + q, :, :] for k in range(6)])
            for k in range(9):
                cz = k % 3 - 1
                b = built[k] if cz == 0 else pltpu.roll(built[k], cz % Z, 1)
                rp[k, XW + 1, into, :] = (1.0 - BLEND[0]) * push(xm_ref[k, rows, :], k, fs) + BLEND[0] * b

    lane = lax.broadcasted_iota(jnp.int32, (YW, Z), 1)
    row = lax.broadcasted_iota(jnp.int32, (YW, Z), 0)
    for i in range(27):
        cx, cy, cz = i // 9 - 1, i // 3 % 3 - 1, i % 3 - 1
        at = x + 1 - cx
        k = 3 * (cx + 1) + cz + 1
        value = rp[i, at, 8 - cy:40 - cy, :]
        if cy == 1:
            value = jnp.where(row == 0, yp_scr[k, pl.ds(at, 1), :], value)
        elif cy == -1:
            value = jnp.where(row == YW - 1, ym_scr[k, pl.ds(at, 1), :], value)
        if cz != 0 and (cx != 0 or cy != 0):
            value = jnp.where(lane == (0 if cz == 1 else Z - 1), rp[i, x + 1, 8:40, :], value)
        out_ref[i, 0, :, :] = value


def after_exchange(got, w, loading, r, xm, xp, ym, yp):
    full = lambda a: pl.BlockSpec(a.shape, lambda x: (0,) * a.ndim)
    return pl.pallas_call(
        last_kernel,
        grid=(XW,),
        in_specs=[full(a) for a in (got, w, loading, r, xm, xp, ym, yp)],
        out_specs=[
            pl.BlockSpec((27, 1, YW, Z), lambda x: (0, x, 0, 0)),
            pl.BlockSpec((1, TURBINES), lambda x: (0, 0)),
        ],
        out_shape=[jax.ShapeDtypeStruct((27, XW, YW, Z), F32), jax.ShapeDtypeStruct((1, TURBINES), F32)],
        scratch_shapes=[
            pltpu.VMEM((27, XW + 2, 48, Z), F32),
            pltpu.VMEM((352, Z), F32),
            pltpu.VMEM((8, 128), F32),
            pltpu.VMEM((10, 8, Z), F32),
            pltpu.VMEM((10, 8, Z), F32),
            pltpu.VMEM((9, 16, Z), F32),
            pltpu.VMEM((9, 16, Z), F32),
        ],
        name="after_exchange",
    )(got, w, loading, r, xm, xp, ym, yp)


def body(populations, precursor, pairing, rates, loading, disc_cols, disc_turb):
    both = ("gx", "gy")
    ring = lambda n, s: [(i, (i + s) % n) for i in range(n)]
    send, w = before_exchange(rates, populations, precursor, disc_cols.reshape(1, SLOTS), disc_turb.reshape(1, SLOTS))
    got = lax.all_to_all(send, both, 0, 0, tiled=True)
    r, xm, xp, ym, yp = collision(rates, populations)
    xm = lax.ppermute(xm, "gx", ring(GX, -1))
    xp = lax.ppermute(xp, "gx", ring(GX, 1))
    ym = lax.ppermute(ym, "gy", ring(GY, -1))
    yp = lax.ppermute(yp, "gy", ring(GY, 1))
    got = lax.all_to_all(route(pairing, got), both, 0, 0, tiled=True)
    read, speed = after_exchange(got, w, loading.reshape(1, TURBINES), r, xm, xp, ym, yp)
    return read, speed.reshape(TURBINES)


def solution(mesh):
    in_specs = (P(None, "gx", "gy", None), P(None, "gx", "gy", None), P(), P(), P(), P(), P())
    out_specs = (P(None, "gx", "gy", None), P())
    return jax.shard_map(body, mesh=mesh, in_specs=in_specs, out_specs=out_specs, check_vma=False)
```

time: 320 us -> 71.9 us (0.22)
  waiting for transfers between devices: 137 us -> 8.92 us
  matrix products: 51.5 us -> 0 us
  blocking collectives: 75.3 us -> 25 us
  Pallas kernels: 0 us -> 20.8 us
  local copies, waits for them, and re-layouts: 20.7 us -> 0.84 us
  between operations: 15.5 us -> 0.68 us
  other arithmetic: 4.99 us -> 0 us
    all_gather x1 -> x0, waiting for transfers between devices: 124 us -> none  [body(): piece = lax.all_gather(precursor, 'gx', axis=1, tiled=True)]
    psum x1 -> x0, blocking collectives: 75.3 us -> none  [body(): totals = lax.psum(partial_totals, ('gx', 'gy'))]
    dot_general x10 -> x0, matrix products: 51.5 us -> none  [the longest x1 31.6 us: body(): jnp.einsum('pr,kryz->kpyz', chosen, piece, precision=FULL_PRECISION)]
    all_to_all x0 -> x1, blocking collectives: none -> 25 us  [body(): got = lax.all_to_all(send, both, 0, 0, tiled=True)]
    pallas_call x0 -> x4, Pallas kernels: none -> 20.8 us  [the longest x1 7.52 us: collision(): pl.pallas_call(collide_kernel, grid=(XW,), in_specs=[pl.BlockSpec(memory_...]
    unnamed x45 -> x10, local copies, waits for them, and re-layouts: 16.8 us -> 0.84 us
    all_to_all x0 -> x1, starting transfers between devices: none -> 4.87 us  [body(): got = lax.all_to_all(route(pairing, got), both, 0, 0, tiled=True)]
    ppermute x4, starting transfers between devices: 14.2 us -> 9.78 us  [the longest x1 8.03 us: body(): xm = lax.ppermute(xm, 'gx', ring(GX, -1))]
  transfers between devices with their start and end apart: 5 -> 5, of which waited for: 4 -> 2; matrix products, arithmetic and copies ran while one was open for 20% -> 0% of each run, Pallas kernels for 0% -> 11%
where the time goes in v1:
time: 71.9 us; the launch traced here: 71 us
  blocking collectives  25 us (35%)
  Pallas kernels  20.8 us (29%)
  starting transfers between devices  14.7 us (20%)
  waiting for transfers between devices  8.92 us (12%)
  local copies, waits for them, and re-layouts  0.84 us (1%)
    all_to_all x1, blocking collectives, body(): got = lax.all_to_all(send, both, 0, 0, tiled=True)  25 us
    ppermute x1, starting transfers between devices, body(): xm = lax.ppermute(xm, 'gx', ring(GX, -1))  8.03 us
    pallas_call x1, Pallas kernels, collision(): pl.pallas_call(collide_kernel, grid=(XW,), in_specs=[pl.BlockSpec(memory_...  7.52 us
    pallas_call x1, Pallas kernels, after_exchange(): pl.pallas_call(last_kernel, grid=(XW,), in_specs=[full(a) for a in (got,...  6.7 us
    ppermute x1, waiting for transfers between devices, body(): xp = lax.ppermute(xp, 'gx', ring(GX, 1))  5.26 us
    all_to_all x1, starting transfers between devices, body(): got = lax.all_to_all(route(pairing, got), both, 0, 0, tiled=True)  4.87 us
    pallas_call x1, Pallas kernels, before_exchange(): pl.pallas_call(first_kernel, grid=(XW // K1_PLANES,), in_specs=[pl.BlockS...  4.56 us
    ppermute x1, waiting for transfers between devices, body(): ym = lax.ppermute(ym, 'gy', ring(GY, -1))  3.66 us
  transfers between devices with their start and end apart: 5, of which 2 were waited for; matrix products, arithmetic and copies ran while one was open for 0% of the time, Pallas kernels for 11%

profile of v1, /device:TPU:1, one launch (start us, length us, event | category | flops | bytes accessed | tf_op | source)
XLA Modules:
  0.0 71.0 jit_solution(1098337499631622915)
XLA Ops:
  0.6 4.6 %before_exchange.1 = (f32[128,8,128]{2,1,0:T(8,128)}, f32[360,128]{1,0:T(8,128)}) custom-call(f32[27]{0:T(128)} %rates_ref.3, f32[27,8,32,128]{3,2,1,0:T(8,128)} %pop_ref.3, f32[27,2,32,128]{3,2,1,0:T(8,128)} %pre_ref.1, s32[1,512]{1,0:T(1,128)} %bitcast.4, s32[1,512]{1,0:T(1,128)} %bitcast.5), custom_call_target="tpu_custom_call" | custom-call | tf_op jit(solution)/shard_map/before_exchange/pallas_call | solution.py:232
  5.2 25.0 %all_to_all.10.got_ref = f32[128,8,128]{2,1,0:T(8,128)} all-to-all(f32[128,8,128]{2,1,0:T(8,128)} %get-tuple-element.11), channel_id=1, replica_groups=mesh['gx'=32,'gy'=4] {'gx','gy'}, dimensions={0} | all-to-all | bytes 1048576 | tf_op jit(solution)/shard_map/all_to_all | solution.py:491
  30.2 2.0 %route.1 = f32[128,8,128]{2,1,0:T(8,128)} custom-call(s32[32]{0:T(128)} %pairing_ref.1, f32[128,8,128]{2,1,0:T(8,128)} %all_to_all.10.got_ref), custom_call_target="tpu_custom_call" | custom-call | tf_op jit(solution)/shard_map/route/pallas_call | solution.py:337
  32.3 4.9 %all-to-all-start.1 = ((f32[128,8,128]{2,1,0:T(8,128)}), f32[128,8,128]{2,1,0:T(8,128)S(1)}, u32[]{:S(2)}, u32[]{:S(2)}) async-start(f32[128,8,128]{2,1,0:T(8,128)} %route.1), calls=%async_computation.1 | async-start | bytes 1048576 | tf_op jit(solution)/shard_map/all_to_all | solution.py:497
  37.1 7.5 %collision.1 = (f32[27,8,32,128]{3,2,1,0:T(8,128)}, f32[9,32,128]{2,1,0:T(8,128)}, f32[9,32,128]{2,1,0:T(8,128)}, f32[9,8,128]{2,1,0:T(8,128)}, f32[9,8,128]{2,1,0:T(8,128)}) custom-call(f32[27]{0:T(128)} %rates_ref.3, f32[27,8,32,128]{3,2,1,0:T(8,128)} %pop_ref.3), custom_call_target="tpu_custom_call" | custom-call | tf_op jit(solution)/shard_map/collision/pallas_call | solution.py:282
  44.7 8.0 %collective-permute-start = (f32[9,32,128]{2,1,0:T(8,128)}, f32[9,32,128]{2,1,0:T(8,128)S(1)}, u32[]{:S(2)}, u32[]{:S(2)}) collective-permute-start(f32[9,32,128]{2,1,0:T(8,128)} %get-tuple-element.14), channel_id=1, source_target_pairs={{0,124},{4,0},{8,4},{12,8},{16,12},{20,16},{24,20},{28,24},{32,28}... | collective-permute-start | bytes 442376 | tf_op jit(solution)/shard_map/ppermute | solution.py:493
  52.7 0.0 collective-permute-start.1
  52.7 0.6 collective-permute-start.2
  53.3 1.1 %collective-permute-start.3 = (f32[9,8,128]{2,1,0:T(8,128)}, f32[9,8,128]{2,1,0:T(8,128)S(1)}, u32[]{:S(2)}, u32[]{:S(2)}) collective-permute-start(f32[9,8,128]{2,1,0:T(8,128)} %get-tuple-element.17), channel_id=1, source_target_pairs={{0,1},{1,2},{2,3},{3,0},{4,5},{5,6},{6,7},{7,4},{8,9},{9,10},{10,1... | collective-permute-start | bytes 110600 | tf_op jit(solution)/shard_map/ppermute | solution.py:496
  54.5 3.7 %collective-permute-done.2.ym_ref = f32[9,8,128]{2,1,0:T(8,128)S(1)} collective-permute-done((f32[9,8,128]{2,1,0:T(8,128)}, f32[9,8,128]{2,1,0:T(8,128)S(1)}, u32[]{:S(2)}, u32[]{:S(2)}) %collective-permute-start.2) | collective-permute-done | bytes 36896 | tf_op jit(solution)/shard_map/ppermute | solution.py:495
  58.1 0.0 copy-start.3
  58.1 0.0 collective-permute-done.3.yp_ref
  58.1 0.0 copy-start.4
  58.1 0.0 collective-permute-done.xm_ref
  58.1 0.0 copy-start.1
  58.1 5.3 %collective-permute-done.1.xp_ref = f32[9,32,128]{2,1,0:T(8,128)S(1)} collective-permute-done((f32[9,32,128]{2,1,0:T(8,128)}, f32[9,32,128]{2,1,0:T(8,128)S(1)}, u32[]{:S(2)}, u32[]{:S(2)}) %collective-permute-start.1) | collective-permute-done | bytes 147488 | tf_op jit(solution)/shard_map/ppermute | solution.py:494
  63.4 0.0 copy-start.2
  63.4 0.0 all-to-all-done.1.got_ref
  63.4 0.0 copy-start
  63.4 0.0 copy-done.3
  63.4 0.0 copy-done.4
  63.4 0.0 copy-done.1
  63.4 0.6 copy-done.2
  64.1 0.2 copy-done
  64.3 6.7 %after_exchange.1 = (f32[27,8,32,128]{3,2,1,0:T(8,128)}, f32[1,32]{1,0:T(1,128)}) custom-call(f32[128,8,128]{2,1,0:T(8,128)} %copy-done, f32[360,128]{1,0:T(8,128)} %get-tuple-element.12.w_ref, f32[1,32]{1,0:T(1,128)} %bitcast.6, f32[27,8,32,128]{3,2,1,0:T(8,128)} %get-tuple-element.13.r_ref, f32[9,32,128]{2,1,0:T(8,128)} %copy-done.1, ...), custom_call_target="tpu_custom_call" | custom-call | tf_op jit(solution)/shard_map/after_exchange/pallas_call | solution.py:465
Async XLA Ops:
  32.3 31.1 %all-to-all-start.1 = ((f32[128,8,128]{2,1,0:T(8,128)}), f32[128,8,128]{2,1,0:T(8,128)S(1)}, u32[]{:S(2)}, u32[]{:S(2)}) async-start(f32[128,8,128]{2,1,0:T(8,128)} %route.1), calls=%async_computation.1 | async-start | bytes 1048576 | tf_op jit(solution)/shard_map/all_to_all | solution.py:497
  44.7 13.4 %collective-permute-start = (f32[9,32,128]{2,1,0:T(8,128)}, f32[9,32,128]{2,1,0:T(8,128)S(1)}, u32[]{:S(2)}, u32[]{:S(2)}) collective-permute-start(f32[9,32,128]{2,1,0:T(8,128)} %get-tuple-element.14), channel_id=1, source_target_pairs={{0,124},{4,0},{8,4},{12,8},{16,12},{20,16},{24,20},{28,24},{32,28}... | collective-permute-start | bytes 442376 | tf_op jit(solution)/shard_map/ppermute | solution.py:493
  52.7 10.7 %collective-permute-start.1 = (f32[9,32,128]{2,1,0:T(8,128)}, f32[9,32,128]{2,1,0:T(8,128)S(1)}, u32[]{:S(2)}, u32[]{:S(2)}) collective-permute-start(f32[9,32,128]{2,1,0:T(8,128)} %get-tuple-element.15), channel_id=1, source_target_pairs={{0,4},{4,8},{8,12},{12,16},{16,20},{20,24},{24,28},{28,32},{32,36}... | collective-permute-start | bytes 442376 | tf_op jit(solution)/shard_map/ppermute | solution.py:494
  52.7 5.4 %collective-permute-start.2 = (f32[9,8,128]{2,1,0:T(8,128)}, f32[9,8,128]{2,1,0:T(8,128)S(1)}, u32[]{:S(2)}, u32[]{:S(2)}) collective-permute-start(f32[9,8,128]{2,1,0:T(8,128)} %get-tuple-element.16), channel_id=1, source_target_pairs={{0,3},{1,0},{2,1},{3,2},{4,7},{5,4},{6,5},{7,6},{8,11},{9,8},{10,9... | collective-permute-start | bytes 110600 | tf_op jit(solution)/shard_map/ppermute | solution.py:495
  53.3 4.8 %collective-permute-start.3 = (f32[9,8,128]{2,1,0:T(8,128)}, f32[9,8,128]{2,1,0:T(8,128)S(1)}, u32[]{:S(2)}, u32[]{:S(2)}) collective-permute-start(f32[9,8,128]{2,1,0:T(8,128)} %get-tuple-element.17), channel_id=1, source_target_pairs={{0,1},{1,2},{2,3},{3,0},{4,5},{5,6},{6,7},{7,4},{8,9},{9,10},{10,1... | collective-permute-start | bytes 110600 | tf_op jit(solution)/shard_map/ppermute | solution.py:496
  58.1 5.3 %copy-start.3 = (f32[9,8,128]{2,1,0:T(8,128)}, f32[9,8,128]{2,1,0:T(8,128)S(1)}, u32[]{:S(2)}) copy-start(f32[9,8,128]{2,1,0:T(8,128)S(1)} %collective-permute-done.2.ym_ref) | copy-start | bytes 110596
  58.1 5.3 %copy-start.4 = (f32[9,8,128]{2,1,0:T(8,128)}, f32[9,8,128]{2,1,0:T(8,128)S(1)}, u32[]{:S(2)}) copy-start(f32[9,8,128]{2,1,0:T(8,128)S(1)} %collective-permute-done.3.yp_ref) | copy-start | bytes 110596
  58.1 5.3 %copy-start.1 = (f32[9,32,128]{2,1,0:T(8,128)}, f32[9,32,128]{2,1,0:T(8,128)S(1)}, u32[]{:S(2)}) copy-start(f32[9,32,128]{2,1,0:T(8,128)S(1)} %collective-permute-done.xm_ref) | copy-start | bytes 442372
  63.4 0.7 copy-start.2
  63.4 0.9 %copy-start = (f32[128,8,128]{2,1,0:T(8,128)}, f32[128,8,128]{2,1,0:T(8,128)S(1)}, u32[]{:S(2)}) copy-start(f32[128,8,128]{2,1,0:T(8,128)S(1)} %all-to-all-done.1.got_ref) | copy-start | bytes 1572868

commit v2 on v1

v2 whole, which is shorter than its diff:
```python
import jax
import jax.numpy as jnp
import numpy as np
from jax import lax
from jax.experimental import pallas as pl
from jax.experimental.pallas import tpu as pltpu
from jax.sharding import PartitionSpec as P

GX, GY = 32, 4
NDEV = GX * GY
XW, YW, Z = 8, 32, 128
NY_ALL, NX_ALL = 128, 256
SLOTS = 512
TURBINES = 32
F32 = jnp.float32

OWN, NEXT, LO_OWN, HI_OWN, LO_NEXT, HI_NEXT, CORNER = 0, 80, 104, 107, 110, 111, 112
PIECE = 9
CORNERS = ((-1, -1), (-1, 1), (1, -1), (1, 1))
W_ROWS = 360
BLEND = (0.5, 0.25)

PROFILE_SUM = float(np.sum(np.exp(-np.square((np.arange(Z) - Z / 3.0) / (Z / 6.0)))))


HBM = pl.BlockSpec(memory_space=pltpu.HBM)
SMEM = pl.BlockSpec(memory_space=pltpu.SMEM)
VMEM = pl.BlockSpec(memory_space=pltpu.VMEM)


def near(array):
    return pltpu.with_memory_space_constraint(array, pltpu.VMEM)


def far(array):
    return pltpu.with_memory_space_constraint(array, pltpu.HBM)


def slot(cx, cy, cz):
    return 9 * (cx + 1) + 3 * (cy + 1) + (cz + 1)


def profile_row():
    heights = lax.broadcasted_iota(jnp.int32, (8, Z), 1).astype(F32)
    return jnp.exp(-jnp.square((heights - Z / 3.0) * (6.0 / Z)))


def forward(g):
    for stride in (1, 3, 9):
        out = list(g)
        for i in range(27):
            if (i // stride) % 3 == 0:
                a, b, c = g[i], g[i + stride], g[i + 2 * stride]
                s = c + a
                out[i] = s + 4.0 * b
                out[i + stride] = c - a
                out[i + 2 * stride] = s
        g = out
    return g


def backward(m):
    for stride in (9, 3, 1):
        out = list(m)
        for i in range(27):
            if (i // stride) % 3 == 0:
                a, b, c = m[i], m[i + stride], m[i + 2 * stride]
                out[i] = c - b
                out[i + stride] = 0.5 * (a - c)
                out[i + 2 * stride] = c + b
        m = out
    return m


def collide(g, rates):
    return relax(forward(g), rates)


def relax(m, rates):
    density = m[0] * (1.0 / 216.0)
    inv = 1.0 / m[0]
    u = (m[9] * inv, m[3] * inv, m[1] * inv)
    j = (m[9] * (1.0 / 216.0), m[3] * (1.0 / 216.0), m[1] * (1.0 / 216.0))
    ju = {}
    for a in range(3):
        for b in range(a, 3):
            ju[(a, b)] = j[a] * u[b]
    out = []
    for i in range(27):
        order = (i // 9, i // 3 % 3, i % 3)
        ones = [d for d in range(3) if order[d] == 1]
        twos = [d for d in range(3) if order[d] == 2]
        if i in (0, 1, 3, 9):
            out.append(m[i] * 0.125)
            continue
        r = rates(i)
        keep = m[i] * ((1.0 - r) * 0.125)
        if len(ones) == 3:
            out.append(keep)
            continue
        scale = r * (27.0 / 3.0 ** len(twos))
        if len(ones) == 0:
            eq = ju[(twos[0], twos[0])]
            for d in twos[1:]:
                eq = eq + ju[(d, d)]
            eq = density + 3.0 * eq
        elif len(ones) == 1:
            eq = j[ones[0]]
        else:
            eq = ju[(ones[0], ones[1])]
        out.append(keep + eq * scale)
    return backward(out)


def z_stream(p, lane):
    out = []
    for i in range(27):
        cz = i % 3 - 1
        if cz == 0:
            out.append(p[i])
        elif cz == 1:
            out.append(jnp.where(lane == 0, p[26 - i], pltpu.roll(p[i], 1, 1)))
        else:
            out.append(jnp.where(lane == Z - 1, p[26 - i], pltpu.roll(p[i], Z - 1, 1)))
    return out


def precursor_coefficients(g):
    m = forward(g)
    rho, jx, jy, jz = m[0], m[9], m[3], m[1]
    xx, yy, zz, xy, xz, yz = m[18], m[6], m[2], m[12], m[10], m[4]
    third = rho * (1.0 / 3.0)
    pxx, pyy, pzz = xx - third, yy - third, zz - third
    s = 1.0 / 216.0
    k0 = (rho - 1.5 * (pxx + pyy + pzz)) * s
    return [k0, jx * (3 * s), jy * (3 * s), jz * (3 * s), pxx * (4.5 * s), pyy * (4.5 * s), pzz * (4.5 * s),
            xy * (9 * s), xz * (9 * s), yz * (9 * s)]


def next_coefficients(c):
    return [c[0] - c[1] + c[4], c[2] - c[7], c[3] - c[8], c[5], c[6], c[9]]


def rebuild_next(c):
    out = []
    for cy in (-1, 0, 1):
        base = c[0] + (cy * c[1] + c[3] if cy else 0.0)
        lin = c[2] + cy * c[5] if cy else c[2]
        for cz in (-1, 0, 1):
            out.append(base + cz * lin + c[4] if cz else base)
    return out


def rebuild(c):
    out = []
    for cx in (-1, 0, 1):
        base = c[0] + cx * c[1] + c[4] if cx else c[0]
        liny = c[2] + cx * c[7] if cx else c[2]
        linz = c[3] + cx * c[8] if cx else c[3]
        out += rebuild_next([base, liny, linz, c[5], c[6], c[9]])
    return out


def first_kernel(rates_hbm, pop_hbm, pre_hbm, send_ref, pre_ref, corner_scr, rates_ref, sems):
    planes = [pltpu.make_async_copy(pre_hbm.at[:, p], pre_ref.at[:, p], sems.at[p]) for p in range(2)]
    columns = []
    for n, (x, y) in enumerate(((0, 0), (0, YW - 8), (XW - 1, 0), (XW - 1, YW - 8))):
        columns.append(pltpu.make_async_copy(pop_hbm.at[:, x, y:y + 8, :], corner_scr.at[n], sems.at[2 + n]))
    columns.append(pltpu.make_async_copy(rates_hbm, rates_ref, sems.at[6]))
    for copy in planes + columns:
        copy.start()
    send_ref[LO_OWN:, :, :] = jnp.zeros((NDEV - LO_OWN, 8, Z), F32)
    for p in range(2):
        planes[p].wait()
        for q in range(4):
            c = precursor_coefficients([pre_ref[i, p, 8 * q:8 * q + 8, :] for i in range(27)])
            for k in range(10):
                send_ref[OWN + (2 * k + p) * 4 + q, :, :] = c[k]
                row = 2 * k + p
                if q == 3:
                    send_ref[LO_OWN + row // 8, row % 8:row % 8 + 1, :] = c[k][7:8, :]
                if q == 0:
                    send_ref[HI_OWN + row // 8, row % 8:row % 8 + 1, :] = c[k][0:1, :]
            if p == 0:
                c = next_coefficients(c)
                for k in range(6):
                    send_ref[NEXT + 4 * k + q, :, :] = c[k]
                    if q == 3:
                        send_ref[LO_NEXT, k:k + 1, :] = c[k][7:8, :]
                    if q == 0:
                        send_ref[HI_NEXT, k:k + 1, :] = c[k][0:1, :]
    for copy in columns:
        copy.wait()
    row = lax.broadcasted_iota(jnp.int32, (8, Z), 0)
    g = []
    for i in range(27):
        rows = [corner_scr[n, i, y:y + 1, :] for n, y in enumerate((0, 7, 0, 7))]
        g.append(jnp.where(row == 0, rows[0], jnp.where(row == 1, rows[1], jnp.where(row == 2, rows[2], rows[3]))))
    lane = lax.broadcasted_iota(jnp.int32, (8, Z), 1)
    post = z_stream(collide(g, lambda i: rates_ref[i]), lane)
    for n, (cx, cy) in enumerate(CORNERS):
        at = 2 * (cx > 0) + (cy > 0)
        for cz in (-1, 0, 1):
            send_ref[CORNER + n, cz + 1:cz + 2, :] = post[slot(cx, cy, cz)][at:at + 1, :]


def before_exchange(rates, populations, precursor):
    return pl.pallas_call(
        first_kernel,
        in_specs=[HBM, HBM, HBM],
        out_specs=VMEM,
        out_shape=pltpu.VMEM((NDEV, 8, Z), F32),
        scratch_shapes=[
            pltpu.VMEM((27, 2, YW, Z), F32),
            pltpu.VMEM((4, 27, 8, Z), F32),
            pltpu.SMEM((27,), F32),
            pltpu.SemaphoreType.DMA((7,)),
        ],
        name="before_exchange",
        compiler_params=pltpu.CompilerParams(vmem_limit_bytes=4 << 20),
    )(far(rates), far(populations), far(precursor))


def collide_kernel(rates_ref, cols_ref, turb_ref, pop_hbm, out_hbm, xa_ref, xb_ref, ya_ref, yb_ref, w_ref, disc_ref,
                   pop_ref, out_ref, ym_ref, yp_ref, in_sems, out_sems):
    def copy_in(x):
        return pltpu.make_async_copy(pop_hbm.at[:, x], pop_ref.at[:, x], in_sems.at[x])

    def copy_out(x):
        return pltpu.make_async_copy(out_ref.at[:, x], out_hbm.at[:, x], out_sems.at[x])

    for x in range(XW):
        copy_in(x).start()
    gx = lax.axis_index("gx")
    gy = lax.axis_index("gy")
    rows = lax.broadcasted_iota(jnp.int32, (W_ROWS, SLOTS), 0)
    lo = rows - 320
    main = rows < 320
    xx = jnp.where(main, rows >> 5, jnp.where(lo < 16, lo, lo - 16))
    yy = jnp.where(main, rows & 31, jnp.where(lo < 16, -1, YW))
    col = ((gx * XW + xx - 1) & (NX_ALL - 1)) * NY_ALL + ((gy * YW + yy) & (NY_ALL - 1))
    valid = main | ((lo & 15) < 10)
    hit = ((col == cols_ref[...]) & valid & (lo < 32)) | (lo >= 32)
    owner = lax.broadcasted_iota(jnp.int32, (128, SLOTS), 0) == turb_ref[...]
    w_ref[...] = lax.dot_general(
        jnp.where(hit, 1.0, 0.0).astype(jnp.bfloat16),
        jnp.where(owner, 1.0, 0.0).astype(jnp.bfloat16),
        (((1,), (1,)), ((), ())), preferred_element_type=F32)
    disc_ref[...] = jnp.zeros_like(disc_ref)
    lane = lax.broadcasted_iota(jnp.int32, (8, Z), 1)
    profile = profile_row()

    def plane(x, carry):
        copy_in(x).wait()
        for q in range(4):
            rows = slice(8 * q, 8 * q + 8)
            m = forward([pop_ref[i, x, rows, :] for i in range(27)])
            sums = jnp.sum(m[9] / m[0] * profile, axis=1, keepdims=True)
            disc_ref[...] += sums * w_ref[pl.ds(pl.multiple_of((x + 1) * YW + 8 * q, 8), 8), :]
            post = z_stream(relax(m, lambda i: rates_ref[i]), lane)
            for i in range(27):
                out_ref[i, x, rows, :] = post[i]
            for cx in (-1, 0, 1):
                for cz in (-1, 0, 1):
                    k = 3 * (cx + 1) + cz + 1
                    if q == 0:
                        ym_ref[k, pl.ds(x, 1), :] = post[slot(cx, -1, cz)][0:1, :]
                    if q == 3:
                        yp_ref[k, pl.ds(x, 1), :] = post[slot(cx, 1, cz)][7:8, :]
        copy_out(x).start()
        return carry

    lax.fori_loop(0, XW, plane, 0)
    odd_x = (gx & 1) == 1
    odd_y = (gy & 1) == 1
    for k in range(9):
        low, high = out_ref[k, 0, :, :], out_ref[18 + k, XW - 1, :, :]
        xa_ref[k, :, :] = jnp.where(odd_x, low, high)
        xb_ref[k, :, :] = jnp.where(odd_x, high, low)
        low, high = ym_ref[k, :, :], yp_ref[k, :, :]
        ya_ref[k, :, :] = jnp.where(odd_y, low, high)
        yb_ref[k, :, :] = jnp.where(odd_y, high, low)
    for x in range(XW):
        copy_out(x).wait()


def collision(rates, cols, turb, populations):
    shapes = ((27, XW, YW, Z), (9, YW, Z), (9, YW, Z), (9, XW, Z), (9, XW, Z), (W_ROWS, 128), (8, 128))
    return pl.pallas_call(
        collide_kernel,
        in_specs=[SMEM, VMEM, VMEM, HBM],
        out_specs=[HBM] + [VMEM] * (len(shapes) - 1),
        out_shape=[pltpu.HBM(shapes[0], F32)] + [pltpu.VMEM(shape, F32) for shape in shapes[1:]],
        scratch_shapes=[
            pltpu.VMEM(shapes[0], F32),
            pltpu.VMEM(shapes[0], F32),
            pltpu.VMEM((9, XW, Z), F32),
            pltpu.VMEM((9, XW, Z), F32),
            pltpu.SemaphoreType.DMA((XW,)),
            pltpu.SemaphoreType.DMA((XW,)),
        ],
        name="collision",
        compiler_params=pltpu.CompilerParams(vmem_limit_bytes=12 << 20),
    )(rates, cols, turb, far(populations))


def route_kernel(pairing_ref, got_ref, disc_ref, send_ref):
    me = lax.axis_index("gx") * GY + lax.axis_index("gy")
    is_next = ((me >= NEXT) & (me < LO_OWN)) | (me == LO_NEXT) | (me == HI_NEXT)
    corner = me - CORNER
    is_corner = (corner >= 0) & (corner < 4)
    low = ((me >= LO_OWN) & (me < HI_OWN)) | (me == LO_NEXT)
    high = ((me >= HI_OWN) & (me < LO_NEXT)) | (me == HI_NEXT)
    from_x = jnp.where(corner < 2, 1, -1)
    from_y = jnp.where(is_corner, jnp.where((corner & 1) == 0, 1, -1), jnp.where(low, -1, jnp.where(high, 1, 0)))
    ahead = jnp.where(is_next, 1, 0)
    lanes = [(t + from_y) & (GY - 1) for t in range(GY)]
    part = jnp.sum(disc_ref[...], axis=0, keepdims=True)
    for d in range(GX):
        tile = pairing_ref[(d + ahead) & (GX - 1)]
        tile = jnp.where(is_corner, (d + from_x) & (GX - 1), tile) * GY
        for t in range(GY):
            at = (d * GY + t) * PIECE
            send_ref[at:at + 8, :] = got_ref[tile + lanes[t], :, :]
            send_ref[at + 8:at + 9, :] = part


def route(pairing, got, disc):
    return pl.pallas_call(
        route_kernel,
        in_specs=[SMEM, VMEM, VMEM],
        out_specs=VMEM,
        out_shape=pltpu.VMEM((NDEV * PIECE, Z), F32),
        name="route",
        compiler_params=pltpu.CompilerParams(vmem_limit_bytes=3 << 20),
    )(pairing, near(got), near(disc))


def last_kernel(got_ref, w_ref, loading_ref, r_hbm, xa_ref, xb_ref, ya_ref, yb_ref, out_hbm, speed_ref,
                rp, force, load_scr, lo_scr, hi_scr, yp_scr, ym_scr, r_ref, out_scr, in_sems, sems):
    def copy_in(x):
        return pltpu.make_async_copy(r_hbm.at[:, x], r_ref.at[:, x], in_sems.at[x])

    for x in range(XW):
        copy_in(x).start()
    lane = lax.broadcasted_iota(jnp.int32, (8, Z), 1)
    profile = profile_row()
    up = jnp.where(lane == 0, -profile, pltpu.roll(profile, 1, 1))
    down = jnp.where(lane == Z - 1, -profile, pltpu.roll(profile, Z - 1, 1))
    along = (3.0 * down, 3.0 * profile, 3.0 * up)

    odd_x = (lax.axis_index("gx") & 1) == 1
    odd_y = (lax.axis_index("gy") & 1) == 1

    def got(tile, a=0, b=8):
        return got_ref[PIECE * tile + a:PIECE * tile + b, :]

    def pushes(f):
        return [f * a for a in along]

    def push(value, i, fs):
        cx = i // 9 - 1
        return value if cx == 0 else (value + fs[i % 3] if cx > 0 else value - fs[i % 3])

    load_scr[...] = jnp.zeros_like(load_scr)
    load_scr[0:1, 0:TURBINES] = loading_ref[...]
    counts = w_ref[352:360, :]
    totals = jnp.broadcast_to(jnp.sum(got_ref[pl.ds(8, NDEV, stride=PIECE), :], axis=0, keepdims=True), (8, 128))
    k = lax.broadcasted_iota(jnp.int32, (8, 128), 1)
    speed = jnp.where(k < TURBINES, totals / (jnp.where(k < TURBINES, counts, 1.0) * PROFILE_SUM), 0.0)
    speed_ref[...] = speed[0:1, 0:TURBINES]
    thrust = (0.5 * jnp.broadcast_to(load_scr[0:1, :], (8, 128))) * speed * jnp.abs(speed)
    force[...] = -lax.dot_general(
        w_ref[0:352, :] * thrust[0:1, :], jnp.ones((128, Z), F32), (((1,), (0,)), ((), ())),
        precision=lax.Precision.HIGHEST, preferred_element_type=F32)
    for scr, tile, nxt, halo, frow, cy, out in (
        (lo_scr, LO_OWN, LO_NEXT, (ya_ref, yb_ref), 320, 1, yp_scr),
        (hi_scr, HI_OWN, HI_NEXT, (yb_ref, ya_ref), 336, -1, ym_scr),
    ):
        scr[...] = jnp.zeros_like(scr)
        for c in range(10):
            r = 2 * c
            scr[c, 0:2, :] = got(tile + r // 8, r % 8, r % 8 + 2)
        built = rebuild([scr[c] for c in range(10)])
        ahead = rebuild_next([got(nxt, c, c + 1) for c in range(6)])
        row = lax.broadcasted_iota(jnp.int32, (8, Z), 0)
        blend = jnp.where(row == 0, BLEND[0], jnp.where(row == 1, BLEND[1], 0.0))
        fs = pushes(force[frow + 1:frow + 9, :])
        for cx in (-1, 0, 1):
            for cz in (-1, 0, 1):
                k = 3 * (cx + 1) + cz + 1
                i = slot(cx, cy, cz)
                b = built[i]
                b = b if cz == 0 else pltpu.roll(b, cz % Z, 1)
                out[k, 1:9, :] = (1.0 - blend) * push(jnp.where(odd_y, halo[0][k], halo[1][k]), i, fs) + blend * b
        for cz in (-1, 0, 1):
            n = CORNERS.index((1, cy))
            out[6 + cz + 1, 0:1, :] = got(CORNER + n, cz + 1, cz + 2) + (
                force[frow:frow + 1, :] * along[cz + 1][0:1, :])
            n = CORNERS.index((-1, cy))
            value = got(CORNER + n, cz + 1, cz + 2) - force[frow + 9:frow + 10, :] * along[cz + 1][0:1, :]
            b = ahead[3 * (cy + 1) + cz + 1]
            b = b if cz == 0 else pltpu.roll(jnp.broadcast_to(b, (8, Z)), cz % Z, 1)[0:1, :]
            out[cz + 1, 9:10, :] = (1.0 - BLEND[0]) * value + BLEND[0] * b

    copy_in(0).wait()
    copy_in(1).wait()
    for q in range(4):
        rows = slice(8 * q, 8 * q + 8)
        into = slice(8 * q + 8, 8 * q + 16)
        fs = pushes(force[rows, :])
        for k in range(9):
            rp[18 + k, 0, into, :] = push(jnp.where(odd_x, xa_ref[k, rows, :], xb_ref[k, rows, :]), 18 + k, fs)
        for p in range(2):
            built = z_stream(rebuild([got(OWN + (2 * k + p) * 4 + q) for k in range(10)]), lane)
            fs = pushes(force[YW * (p + 1) + 8 * q:YW * (p + 1) + 8 * q + 8, :])
            for i in range(27):
                rp[i, p + 1, into, :] = (1.0 - BLEND[p]) * push(r_ref[i, p, rows, :], i, fs) + BLEND[p] * built[i]
        fs = pushes(force[YW * (XW + 1) + 8 * q:YW * (XW + 1) + 8 * q + 8, :])
        built = rebuild_next([got(NEXT + 4 * k + q) for k in range(6)])
        for k in range(9):
            cz = k % 3 - 1
            b = built[k] if cz == 0 else pltpu.roll(built[k], cz % Z, 1)
            rp[k, XW + 1, into, :] = (1.0 - BLEND[0]) * push(jnp.where(odd_x, xb_ref[k, rows, :], xa_ref[k, rows, :]), k, fs) + BLEND[0] * b

    wide_lane = lax.broadcasted_iota(jnp.int32, (YW, Z), 1)
    wide_row = lax.broadcasted_iota(jnp.int32, (YW, Z), 0)

    def copy_out(x):
        return pltpu.make_async_copy(out_scr.at[:, x], out_hbm.at[:, x], sems.at[x])

    def plane(x, carry):
        @pl.when(x < XW - 2)
        def _():
            copy_in(x + 2).wait()
            for q in range(4):
                rows = slice(8 * q, 8 * q + 8)
                into = slice(8 * q + 8, 8 * q + 16)
                fs = pushes(force[pl.ds(pl.multiple_of((x + 3) * YW + 8 * q, 8), 8), :])
                for i in range(27):
                    rp[i, x + 3, into, :] = push(r_ref[i, x + 2, rows, :], i, fs)

        for i in range(27):
            cx, cy, cz = i // 9 - 1, i // 3 % 3 - 1, i % 3 - 1
            at = x + 1 - cx
            k = 3 * (cx + 1) + cz + 1
            value = rp[i, at, 8 - cy:40 - cy, :]
            if cy == 1:
                value = jnp.where(wide_row == 0, yp_scr[k, pl.ds(at, 1), :], value)
            elif cy == -1:
                value = jnp.where(wide_row == YW - 1, ym_scr[k, pl.ds(at, 1), :], value)
            if cz != 0 and (cx != 0 or cy != 0):
                value = jnp.where(wide_lane == (0 if cz == 1 else Z - 1), rp[i, x + 1, 8:40, :], value)
            out_scr[i, x, :, :] = value
        copy_out(x).start()
        return carry

    lax.fori_loop(0, XW, plane, 0)
    for x in range(XW):
        copy_out(x).wait()


def after_exchange(*args):
    return pl.pallas_call(
        last_kernel,
        in_specs=[HBM if n == 3 else VMEM for n in range(len(args))],
        out_specs=[HBM, VMEM],
        out_shape=[pltpu.HBM((27, XW, YW, Z), F32), jax.ShapeDtypeStruct((1, TURBINES), F32)],
        scratch_shapes=[
            pltpu.VMEM((27, XW + 2, 48, Z), F32),
            pltpu.VMEM((352, Z), F32),
            pltpu.VMEM((8, 128), F32),
            pltpu.VMEM((10, 8, Z), F32),
            pltpu.VMEM((10, 8, Z), F32),
            pltpu.VMEM((9, 16, Z), F32),
            pltpu.VMEM((9, 16, Z), F32),
            pltpu.VMEM((27, XW, YW, Z), F32),
            pltpu.VMEM((27, XW, YW, Z), F32),
            pltpu.SemaphoreType.DMA((XW,)),
            pltpu.SemaphoreType.DMA((XW,)),
        ],
        name="after_exchange",
        compiler_params=pltpu.CompilerParams(vmem_limit_bytes=24 << 20),
    )(*[far(a) if n == 3 else near(a) for n, a in enumerate(args)])


def body(populations, precursor, pairing, rates, loading, disc_cols, disc_turb):
    both = ("gx", "gy")
    inner = lambda n: [(i, i ^ 1) for i in range(n)]
    outer = lambda n: [(i, (i + (1 if i % 2 else -1)) % n) for i in range(n)]
    send = before_exchange(rates, populations, precursor)
    got = lax.all_to_all(send, both, 0, 0, tiled=True)
    r, xa, xb, ya, yb, w, disc = collision(
        rates, disc_cols.reshape(1, SLOTS), disc_turb.reshape(1, SLOTS), populations)
    xb = lax.ppermute(xb, "gx", outer(GX))
    xa = lax.ppermute(xa, "gx", inner(GX))
    yb = lax.ppermute(yb, "gy", outer(GY))
    ya = lax.ppermute(ya, "gy", inner(GY))
    send = route(pairing, got, disc).reshape(NDEV, PIECE, 1, Z)
    got = lax.all_to_all(send, both, 0, 0, tiled=True).reshape(NDEV * PIECE, Z)
    read, speed = after_exchange(got, w, loading.reshape(1, TURBINES), r, xa, xb, ya, yb)
    return read, speed.reshape(TURBINES)


def solution(mesh):
    in_specs = (P(None, "gx", "gy", None), P(None, "gx", "gy", None), P(), P(), P(), P(), P())
    out_specs = (P(None, "gx", "gy", None), P())
    return jax.shard_map(body, mesh=mesh, in_specs=in_specs, out_specs=out_specs, check_vma=False)
```

time: 71.9 us -> 56.2 us (0.78)
  blocking collectives: 25 us -> 0 us
  starting transfers between devices: 14.7 us -> 26.1 us
  Pallas kernels: 20.8 us -> 12.8 us
  waiting for transfers between devices: 8.92 us -> 16.3 us
  local copies, waits for them, and re-layouts: 0.84 us -> 0.02 us
    all_to_all x1 -> x0, blocking collectives: 25 us -> none  [body(): got = lax.all_to_all(send, both, 0, 0, tiled=True)]
    all_to_all x1 -> x2, starting transfers between devices: 4.87 us -> 16.4 us  [the longest x1 11.5 us: body(): got = lax.all_to_all(send, both, 0, 0, tiled=True)]
    all_to_all x1 -> x2, waiting for transfers between devices: 0.01 us -> 8.4 us  [the longest x1 8.4 us: body(): got = lax.all_to_all(send, both, 0, 0, tiled=True)]
    pallas_call x4, Pallas kernels: 20.8 us -> 12.8 us  [the longest x1 5 us: collision(): pl.pallas_call(collide_kernel, in_specs=[SMEM, VMEM, VMEM, HBM], out_spec...]
    ppermute x4, waiting for transfers between devices: 8.92 us -> 7.88 us  [the longest x1 3.71 us: body(): yb = lax.ppermute(yb, 'gy', outer(GY))]
    unnamed x10, local copies, waits for them, and re-layouts: 0.84 us -> 0.02 us
  transfers between devices with their start and end apart: 5 -> 6, of which waited for: 2 -> 4; matrix products, arithmetic and copies ran while one was open for 0% -> 0% of each run, Pallas kernels for 11% -> 9%
where the time goes in v2:
time: 56.2 us; the launch traced here: 55.9 us
  starting transfers between devices  26.1 us (46%)
  waiting for transfers between devices  16.3 us (29%)
  Pallas kernels  12.8 us (23%)
  between operations  0.73 us (1%)
    all_to_all x1, starting transfers between devices, body(): got = lax.all_to_all(send, both, 0, 0, tiled=True)  11.5 us
    all_to_all x1, waiting for transfers between devices, body(): got = lax.all_to_all(send, both, 0, 0, tiled=True)  8.4 us
    ppermute x1, starting transfers between devices, body(): xb = lax.ppermute(xb, 'gx', outer(GX))  7.13 us
    pallas_call x1, Pallas kernels, collision(): pl.pallas_call(collide_kernel, in_specs=[SMEM, VMEM, VMEM, HBM], out_spec...  5 us
    all_to_all x1, starting transfers between devices, body(): got = lax.all_to_all(send, both, 0, 0, tiled=True).reshape(NDEV * PIECE, Z)  4.87 us
    pallas_call x1, Pallas kernels, after_exchange(): pl.pallas_call(last_kernel, in_specs=[HBM if n == 3 else VMEM for n in ra...  4.02 us
    ppermute x1, waiting for transfers between devices, body(): yb = lax.ppermute(yb, 'gy', outer(GY))  3.71 us
    ppermute x1, waiting for transfers between devices, body(): xb = lax.ppermute(xb, 'gx', outer(GX))  3.5 us
  transfers between devices with their start and end apart: 6, of which 4 were waited for; matrix products, arithmetic and copies ran while one was open for 0% of the time, Pallas kernels for 9%

profile of v2, /device:TPU:1, one launch (start us, length us, event | category | flops | bytes accessed | tf_op | source)
XLA Modules:
  0.0 55.9 jit_solution(1689792101988837351)
XLA Ops:
  0.6 0.0 copy-start.2
  0.6 0.0 copy-start.1
  0.7 0.0 copy-start
  0.7 0.0 copy-start.3
  0.7 2.3 %before_exchange.1 = f32[128,8,128]{2,1,0:T(8,128)} custom-call(f32[27]{0:T(128)} %rates_ref.1, f32[27,8,32,128]{3,2,1,0:T(8,128)} %pop_hbm.3, f32[27,2,32,128]{3,2,1,0:T(8,128)} %pre_hbm.1), custom_call_target="tpu_custom_call" | custom-call | tf_op jit(solution)/shard_map/before_exchange/pallas_call | solution.py:208
  3.0 0.0 copy-start.4
  3.0 11.5 %all-to-all-start = ((f32[128,8,128]{2,1,0:T(8,128)}), f32[128,8,128]{2,1,0:T(8,128)S(1)}, u32[]{:S(2)}, u32[]{:S(2)}) async-start(f32[128,8,128]{2,1,0:T(8,128)} %before_exchange.1), calls=%async_computation | async-start | bytes 1048576 | tf_op jit(solution)/shard_map/all_to_all | solution.py:492
  14.5 0.0 copy-done.2
  14.5 0.0 copy-done.1
  14.5 0.0 copy-done
  14.5 5.0 %collision.1 = (f32[27,8,32,128]{3,2,1,0:T(8,128)}, f32[9,32,128]{2,1,0:T(8,128)S(1)}, f32[9,32,128]{2,1,0:T(8,128)S(1)}, f32[9,8,128]{2,1,0:T(8,128)S(1)}, f32[...) custom-call(f32[27]{0:T(128)S(1)} %copy-done.2, s32[1,512]{1,0:T(1,128)S(1)} %bitcast.7, ...), custom_call_target="tpu_custom_call" | custom-call | tf_op jit(solution)/shard_map/collision/pallas_call | solution.py:289
  19.5 8.4 %all-to-all-done.got_ref = f32[128,8,128]{2,1,0:T(8,128)S(1)} async-done(((f32[128,8,128]{2,1,0:T(8,128)}), f32[128,8,128]{2,1,0:T(8,128)S(1)}, u32[]{:S(2)}, u32[]{:S(2)}) %all-to-all-start) | async-done | bytes 524320 | tf_op jit(solution)/shard_map/all_to_all | solution.py:492
  27.9 0.0 copy-done.3
  27.9 1.5 %route.1 = f32[1152,128]{1,0:T(8,128)} custom-call(s32[32]{0:T(128)S(1)} %copy-done.3, f32[128,8,128]{2,1,0:T(8,128)S(1)} %all-to-all-done.got_ref, f32[8,128]{1,0:T(8,128)S(1)} %get-tuple-element.11.disc_ref), custom_call_target="tpu_custom_call" | custom-call | tf_op jit(solution)/shard_map/route/pallas_call | solution.py:329
  29.5 4.9 %all-to-all-start.1 = ((f32[128,9,1,128]{3,2,1,0:T(1,128)}), f32[128,9,1,128]{3,2,1,0:T(1,128)S(1)}, u32[]{:S(2)}, u32[]{:S(2)}) async-start(f32[128,9,1,128]{3,2,1,0:T(1,128)} %bitcast.2), calls=%async_computation.1 | async-start | bytes 1179648 | tf_op jit(solution)/shard_map/all_to_all | solution.py:500
  34.3 1.5 %collective-permute-start = (f32[9,32,128]{2,1,0:T(8,128)S(1)}, f32[9,32,128]{2,1,0:T(8,128)S(1)}, u32[]{:S(2)}, u32[]{:S(2)}) collective-permute-start(f32[9,32,128]{2,1,0:T(8,128)S(1)} %get-tuple-element.14), channel_id=1, source_target_pairs={{0,4},{4,0},{8,12},{12,8},{16,20},{20,16},{24,28},{28,24},{32,36},... | collective-permute-start | bytes 442376 | tf_op jit(solution)/shard_map/ppermute | solution.py:496
  35.8 7.1 %collective-permute-start.1 = (f32[9,32,128]{2,1,0:T(8,128)S(1)}, f32[9,32,128]{2,1,0:T(8,128)S(1)}, u32[]{:S(2)}, u32[]{:S(2)}) collective-permute-start(f32[9,32,128]{2,1,0:T(8,128)S(1)} %get-tuple-element.15), channel_id=1, source_target_pairs={{0,124},{4,8},{8,4},{12,16},{16,12},{20,24},{24,20},{28,32},{32,28... | collective-permute-start | bytes 442376 | tf_op jit(solution)/shard_map/ppermute | solution.py:495
  42.9 0.9 %collective-permute-start.2 = (f32[9,8,128]{2,1,0:T(8,128)S(1)}, f32[9,8,128]{2,1,0:T(8,128)S(1)}, u32[]{:S(2)}, u32[]{:S(2)}) collective-permute-start(f32[9,8,128]{2,1,0:T(8,128)S(1)} %get-tuple-element.16), channel_id=1, source_target_pairs={{0,1},{1,0},{2,3},{3,2},{4,5},{5,4},{6,7},{7,6},{8,9},{9,8},{10,11... | collective-permute-start | bytes 110600 | tf_op jit(solution)/shard_map/ppermute | solution.py:498
  43.9 0.2 collective-permute-start.3
  44.0 0.7 %collective-permute-done.2.ya_ref = f32[9,8,128]{2,1,0:T(8,128)S(1)} collective-permute-done((f32[9,8,128]{2,1,0:T(8,128)S(1)}, f32[9,8,128]{2,1,0:T(8,128)S(1)}, u32[]{:S(2)}, u32[]{:S(2)}) %collective-permute-start.2) | collective-permute-done | bytes 36896 | tf_op jit(solution)/shard_map/ppermute | solution.py:498
  44.7 3.7 %collective-permute-done.3.yb_ref = f32[9,8,128]{2,1,0:T(8,128)S(1)} collective-permute-done((f32[9,8,128]{2,1,0:T(8,128)S(1)}, f32[9,8,128]{2,1,0:T(8,128)S(1)}, u32[]{:S(2)}, u32[]{:S(2)}) %collective-permute-start.3) | collective-permute-done | bytes 36896 | tf_op jit(solution)/shard_map/ppermute | solution.py:497
  48.4 0.0 collective-permute-done.xa_ref
  48.4 3.5 %collective-permute-done.1.xb_ref = f32[9,32,128]{2,1,0:T(8,128)S(1)} collective-permute-done((f32[9,32,128]{2,1,0:T(8,128)S(1)}, f32[9,32,128]{2,1,0:T(8,128)S(1)}, u32[]{:S(2)}, u32[]{:S(2)}) %collective-permute-start.1) | collective-permute-done | bytes 147488 | tf_op jit(solution)/shard_map/ppermute | solution.py:495
  51.9 0.0 all-to-all-done.1
  51.9 0.0 copy-done.4
  51.9 4.0 %after_exchange.1 = (f32[27,8,32,128]{3,2,1,0:T(8,128)}, f32[1,32]{1,0:T(1,128)}) custom-call(f32[1152,128]{1,0:T(8,128)S(1)} %bitcast.6, f32[360,128]{1,0:T(8,128)S(1)} %get-tuple-element.12.w_ref, f32[1,32]{1,0:T(1,128)S(1)} %bitcast.9, f32[27,8,32,128]{3,2,1,0:T(8,128)} %get-tuple-element.13.r_hbm, f32[9,32,128]{2,1,0:T(8,128)S(1)} %collective-permute-done.xa_ref, ...), custom_call_target="tpu_custom_call" | custom-call | tf_op jit(solution)/shard_map/after_exchange/pallas_call | solution.py:464
Async XLA Ops:
  0.6 13.8 %copy-start.2 = (f32[27]{0:T(128)S(1)}, f32[27]{0:T(128)}, u32[]{:S(2)}) copy-start(f32[27]{0:T(128)} %rates_ref.1) | copy-start | bytes 328
  0.6 13.8 %copy-start.1 = (s32[512]{0:T(512)S(1)}, s32[512]{0:T(512)}, u32[]{:S(2)}) copy-start(s32[512]{0:T(512)} %param.13) | copy-start | bytes 6148
  0.7 13.8 %copy-start = (s32[512]{0:T(512)S(1)}, s32[512]{0:T(512)}, u32[]{:S(2)}) copy-start(s32[512]{0:T(512)} %param.12) | copy-start | bytes 6148
  0.7 27.3 %copy-start.3 = (s32[32]{0:T(128)S(1)}, s32[32]{0:T(128)}, u32[]{:S(2)}) copy-start(s32[32]{0:T(128)} %pairing_ref.1) | copy-start | bytes 388
  3.0 49.0 %copy-start.4 = (f32[32]{0:T(128)S(1)}, f32[32]{0:T(128)}, u32[]{:S(2)}) copy-start(f32[32]{0:T(128)} %param.11) | copy-start | bytes 388
  3.0 24.9 %all-to-all-start = ((f32[128,8,128]{2,1,0:T(8,128)}), f32[128,8,128]{2,1,0:T(8,128)S(1)}, u32[]{:S(2)}, u32[]{:S(2)}) async-start(f32[128,8,128]{2,1,0:T(8,128)} %before_exchange.1), calls=%async_computation | async-start | bytes 1048576 | tf_op jit(solution)/shard_map/all_to_all | solution.py:492
  29.5 22.5 %all-to-all-start.1 = ((f32[128,9,1,128]{3,2,1,0:T(1,128)}), f32[128,9,1,128]{3,2,1,0:T(1,128)S(1)}, u32[]{:S(2)}, u32[]{:S(2)}) async-start(f32[128,9,1,128]{3,2,1,0:T(1,128)} %bitcast.2), calls=%async_computation.1 | async-start | bytes 1179648 | tf_op jit(solution)/shard_map/all_to_all | solution.py:500
  34.3 14.1 %collective-permute-start = (f32[9,32,128]{2,1,0:T(8,128)S(1)}, f32[9,32,128]{2,1,0:T(8,128)S(1)}, u32[]{:S(2)}, u32[]{:S(2)}) collective-permute-start(f32[9,32,128]{2,1,0:T(8,128)S(1)} %get-tuple-element.14), channel_id=1, source_target_pairs={{0,4},{4,0},{8,12},{12,8},{16,20},{20,16},{24,28},{28,24},{32,36},... | collective-permute-start | bytes 442376 | tf_op jit(solution)/shard_map/ppermute | solution.py:496
  35.8 16.1 %collective-permute-start.1 = (f32[9,32,128]{2,1,0:T(8,128)S(1)}, f32[9,32,128]{2,1,0:T(8,128)S(1)}, u32[]{:S(2)}, u32[]{:S(2)}) collective-permute-start(f32[9,32,128]{2,1,0:T(8,128)S(1)} %get-tuple-element.15), channel_id=1, source_target_pairs={{0,124},{4,8},{8,4},{12,16},{16,12},{20,24},{24,20},{28,32},{32,28... | collective-permute-start | bytes 442376 | tf_op jit(solution)/shard_map/ppermute | solution.py:495
  42.9 1.8 %collective-permute-start.2 = (f32[9,8,128]{2,1,0:T(8,128)S(1)}, f32[9,8,128]{2,1,0:T(8,128)S(1)}, u32[]{:S(2)}, u32[]{:S(2)}) collective-permute-start(f32[9,8,128]{2,1,0:T(8,128)S(1)} %get-tuple-element.16), channel_id=1, source_target_pairs={{0,1},{1,0},{2,3},{3,2},{4,5},{5,4},{6,7},{7,6},{8,9},{9,8},{10,11... | collective-permute-start | bytes 110600 | tf_op jit(solution)/shard_map/ppermute | solution.py:498
  43.9 4.6 %collective-permute-start.3 = (f32[9,8,128]{2,1,0:T(8,128)S(1)}, f32[9,8,128]{2,1,0:T(8,128)S(1)}, u32[]{:S(2)}, u32[]{:S(2)}) collective-permute-start(f32[9,8,128]{2,1,0:T(8,128)S(1)} %get-tuple-element.17), channel_id=1, source_target_pairs={{0,3},{1,2},{2,1},{3,0},{4,7},{5,6},{6,5},{7,4},{8,11},{9,10},{10,... | collective-permute-start | bytes 110600 | tf_op jit(solution)/shard_map/ppermute | solution.py:497

commit v3 on v2

--- a/solution.py
+++ b/solution.py
@@ -161,17 +161,19 @@
     return out
 
 
-def first_kernel(rates_hbm, pop_hbm, pre_hbm, send_ref, pre_ref, corner_scr, rates_ref, sems):
-    planes = [pltpu.make_async_copy(pre_hbm.at[:, p], pre_ref.at[:, p], sems.at[p]) for p in range(2)]
-    columns = []
-    for n, (x, y) in enumerate(((0, 0), (0, YW - 8), (XW - 1, 0), (XW - 1, YW - 8))):
-        columns.append(pltpu.make_async_copy(pop_hbm.at[:, x, y:y + 8, :], corner_scr.at[n], sems.at[2 + n]))
-    columns.append(pltpu.make_async_copy(rates_hbm, rates_ref, sems.at[6]))
-    for copy in planes + columns:
+def first_kernel(rates_hbm, pop_hbm, pre_hbm, send_ref, xa_ref, xb_ref, ya_ref, yb_ref, pre_ref, edge_ref, side_ref,
+                 rates_ref, sems):
+    copies = [pltpu.make_async_copy(pre_hbm.at[:, p], pre_ref.at[:, p], sems.at[p]) for p in range(2)]
+    for n, x in enumerate((0, XW - 1)):
+        copies.append(pltpu.make_async_copy(pop_hbm.at[:, x], edge_ref.at[:, n], sems.at[2 + n]))
+    copies.append(pltpu.make_async_copy(rates_hbm, rates_ref, sems.at[4]))
+    for n, y in enumerate((0, YW - 1)):
+        copies.append(pltpu.make_async_copy(pop_hbm.at[:, :, y, :], side_ref.at[n], sems.at[5 + n]))
+    for copy in copies:
         copy.start()
     send_ref[LO_OWN:, :, :] = jnp.zeros((NDEV - LO_OWN, 8, Z), F32)
     for p in range(2):
-        planes[p].wait()
+        copies[p].wait()
         for q in range(4):
             c = precursor_coefficients([pre_ref[i, p, 8 * q:8 * q + 8, :] for i in range(27)])
             for k in range(10):
@@ -189,30 +191,51 @@
                         send_ref[LO_NEXT, k:k + 1, :] = c[k][7:8, :]
                     if q == 0:
                         send_ref[HI_NEXT, k:k + 1, :] = c[k][0:1, :]
-    for copy in columns:
-        copy.wait()
-    row = lax.broadcasted_iota(jnp.int32, (8, Z), 0)
-    g = []
-    for i in range(27):
-        rows = [corner_scr[n, i, y:y + 1, :] for n, y in enumerate((0, 7, 0, 7))]
-        g.append(jnp.where(row == 0, rows[0], jnp.where(row == 1, rows[1], jnp.where(row == 2, rows[2], rows[3]))))
+    copies[4].wait()
     lane = lax.broadcasted_iota(jnp.int32, (8, Z), 1)
-    post = z_stream(collide(g, lambda i: rates_ref[i]), lane)
-    for n, (cx, cy) in enumerate(CORNERS):
-        at = 2 * (cx > 0) + (cy > 0)
-        for cz in (-1, 0, 1):
-            send_ref[CORNER + n, cz + 1:cz + 2, :] = post[slot(cx, cy, cz)][at:at + 1, :]
+    odd_x = (lax.axis_index("gx") & 1) == 1
+    for n, cx in enumerate((-1, 1)):
+        copies[2 + n].wait()
+        for q in range(4):
+            rows = slice(8 * q, 8 * q + 8)
+            post = z_stream(collide([edge_ref[i, n, rows, :] for i in range(27)], lambda i: rates_ref[i]), lane)
+            for k in range(9):
+                value = post[9 * (cx + 1) + k]
+                if cx < 0:
+                    xa_ref[k, rows, :] = value
+                else:
+                    keep = xa_ref[k, rows, :]
+                    xa_ref[k, rows, :] = jnp.where(odd_x, keep, value)
+                    xb_ref[k, rows, :] = jnp.where(odd_x, value, keep)
+    odd_y = (lax.axis_index("gy") & 1) == 1
+    for n, cy in enumerate((-1, 1)):
+        copies[5 + n].wait()
+        post = z_stream(collide([side_ref[n, i] for i in range(27)], lambda i: rates_ref[i]), lane)
+        for cx in (-1, 0, 1):
+            for cz in (-1, 0, 1):
+                k = 3 * (cx + 1) + cz + 1
+                value = post[slot(cx, cy, cz)]
+                if cy < 0:
+                    ya_ref[k, :, :] = value
+                else:
+                    keep = ya_ref[k, :, :]
+                    ya_ref[k, :, :] = jnp.where(odd_y, keep, value)
+                    yb_ref[k, :, :] = jnp.where(odd_y, value, keep)
+                if cx:
+                    at = 0 if cx < 0 else XW - 1
+                    send_ref[CORNER + CORNERS.index((cx, cy)), cz + 1:cz + 2, :] = value[at:at + 1, :]
 
 
 def before_exchange(rates, populations, precursor):
     return pl.pallas_call(
         first_kernel,
         in_specs=[HBM, HBM, HBM],
-        out_specs=VMEM,
-        out_shape=pltpu.VMEM((NDEV, 8, Z), F32),
+        out_specs=[VMEM] * 5,
+        out_shape=[pltpu.VMEM((NDEV, 8, Z), F32)] + [pltpu.VMEM((9, n, Z), F32) for n in (YW, YW, XW, XW)],
         scratch_shapes=[
             pltpu.VMEM((27, 2, YW, Z), F32),
-            pltpu.VMEM((4, 27, 8, Z), F32),
+            pltpu.VMEM((27, 2, YW, Z), F32),
+            pltpu.VMEM((2, 27, XW, Z), F32),
             pltpu.SMEM((27,), F32),
             pltpu.SemaphoreType.DMA((7,)),
         ],
@@ -221,8 +244,8 @@
     )(far(rates), far(populations), far(precursor))
 
 
-def collide_kernel(rates_ref, cols_ref, turb_ref, pop_hbm, out_hbm, xa_ref, xb_ref, ya_ref, yb_ref, w_ref, disc_ref,
-                   pop_ref, out_ref, ym_ref, yp_ref, in_sems, out_sems):
+def collide_kernel(rates_ref, cols_ref, turb_ref, pop_hbm, out_hbm, w_ref, disc_ref,
+                   pop_ref, out_ref, in_sems, out_sems):
     def copy_in(x):
         return pltpu.make_async_copy(pop_hbm.at[:, x], pop_ref.at[:, x], in_sems.at[x])
 
@@ -260,32 +283,16 @@
             post = z_stream(relax(m, lambda i: rates_ref[i]), lane)
             for i in range(27):
                 out_ref[i, x, rows, :] = post[i]
-            for cx in (-1, 0, 1):
-                for cz in (-1, 0, 1):
-                    k = 3 * (cx + 1) + cz + 1
-                    if q == 0:
-                        ym_ref[k, pl.ds(x, 1), :] = post[slot(cx, -1, cz)][0:1, :]
-                    if q == 3:
-                        yp_ref[k, pl.ds(x, 1), :] = post[slot(cx, 1, cz)][7:8, :]
         copy_out(x).start()
         return carry
 
     lax.fori_loop(0, XW, plane, 0)
-    odd_x = (gx & 1) == 1
-    odd_y = (gy & 1) == 1
-    for k in range(9):
-        low, high = out_ref[k, 0, :, :], out_ref[18 + k, XW - 1, :, :]
-        xa_ref[k, :, :] = jnp.where(odd_x, low, high)
-        xb_ref[k, :, :] = jnp.where(odd_x, high, low)
-        low, high = ym_ref[k, :, :], yp_ref[k, :, :]
-        ya_ref[k, :, :] = jnp.where(odd_y, low, high)
-        yb_ref[k, :, :] = jnp.where(odd_y, high, low)
     for x in range(XW):
         copy_out(x).wait()
 
 
 def collision(rates, cols, turb, populations):
-    shapes = ((27, XW, YW, Z), (9, YW, Z), (9, YW, Z), (9, XW, Z), (9, XW, Z), (W_ROWS, 128), (8, 128))
+    shapes = ((27, XW, YW, Z), (W_ROWS, 128), (8, 128))
     return pl.pallas_call(
         collide_kernel,
         in_specs=[SMEM, VMEM, VMEM, HBM],
@@ -294,8 +301,6 @@
         scratch_shapes=[
             pltpu.VMEM(shapes[0], F32),
             pltpu.VMEM(shapes[0], F32),
-            pltpu.VMEM((9, XW, Z), F32),
-            pltpu.VMEM((9, XW, Z), F32),
             pltpu.SemaphoreType.DMA((XW,)),
             pltpu.SemaphoreType.DMA((XW,)),
         ],
@@ -488,15 +493,16 @@
     both = ("gx", "gy")
     inner = lambda n: [(i, i ^ 1) for i in range(n)]
     outer = lambda n: [(i, (i + (1 if i % 2 else -1)) % n) for i in range(n)]
-    send = before_exchange(rates, populations, precursor)
+    send, xa, xb, ya, yb = before_exchange(rates, populations, precursor)
     got = lax.all_to_all(send, both, 0, 0, tiled=True)
-    r, xa, xb, ya, yb, w, disc = collision(
+    r, w, disc = collision(
         rates, disc_cols.reshape(1, SLOTS), disc_turb.reshape(1, SLOTS), populations)
     xb = lax.ppermute(xb, "gx", outer(GX))
     xa = lax.ppermute(xa, "gx", inner(GX))
     yb = lax.ppermute(yb, "gy", outer(GY))
     ya = lax.ppermute(ya, "gy", inner(GY))
-    send = route(pairing, got, disc).reshape(NDEV, PIECE, 1, Z)
+    send, xa, xb, ya, yb = lax.optimization_barrier((route(pairing, got, disc), xa, xb, ya, yb))
+    send = send.reshape(NDEV, PIECE, 1, Z)
     got = lax.all_to_all(send, both, 0, 0, tiled=True).reshape(NDEV * PIECE, Z)
     read, speed = after_exchange(got, w, loading.reshape(1, TURBINES), r, xa, xb, ya, yb)
     return read, speed.reshape(TURBINES)

time: 56.2 us -> 55.3 us (0.984)
  blocking collectives: 0 us -> 19.2 us
  waiting for transfers between devices: 16.3 us -> 1.49 us
  starting transfers between devices: 26.1 us -> 21.2 us
    all_to_all x0 -> x1, blocking collectives: none -> 19.2 us  [body(): got = lax.all_to_all(send, both, 0, 0, tiled=True).reshape(NDEV * PIECE, Z)]
    all_to_all x1, waiting for transfers between devices: 8.4 us -> 0.01 us  [body(): got = lax.all_to_all(send, both, 0, 0, tiled=True)]
    all_to_all x1 -> x0, starting transfers between devices: 4.87 us -> none  [body(): got = lax.all_to_all(send, both, 0, 0, tiled=True).reshape(NDEV * PIECE, Z)]
    ppermute x1, waiting for transfers between devices: 3.71 us -> 0.01 us  [body(): yb = lax.ppermute(yb, 'gy', outer(GY))]
    ppermute x1, waiting for transfers between devices: 3.5 us -> 1.48 us  [body(): xb = lax.ppermute(xb, 'gx', outer(GX))]
    pallas_call x1, Pallas kernels: 1.54 us -> 0.73 us  [route(): pl.pallas_call(route_kernel, in_specs=[SMEM, VMEM, VMEM], out_specs=VMEM,...]
    ppermute x1, waiting for transfers between devices: 0.68 us -> 0.01 us  [body(): ya = lax.ppermute(ya, 'gy', inner(GY))]
  transfers between devices with their start and end apart: 6 -> 5, of which waited for: 4 -> 1; matrix products, arithmetic and copies ran while one was open for 0% -> 0% of each run, Pallas kernels for 9% -> 10%
where the time goes in v3:
time: 55.3 us; the launch traced here: 55.1 us
  starting transfers between devices  21.2 us (38%)
  blocking collectives  19.2 us (35%)
  Pallas kernels  12.4 us (22%)
  waiting for transfers between devices  1.49 us (3%)
  between operations  0.75 us (1%)
    all_to_all x1, blocking collectives, body(): got = lax.all_to_all(send, both, 0, 0, tiled=True).reshape(NDEV * PIECE, Z)  19.2 us
    all_to_all x1, starting transfers between devices, body(): got = lax.all_to_all(send, both, 0, 0, tiled=True)  11.5 us
    ppermute x1, starting transfers between devices, body(): xb = lax.ppermute(xb, 'gx', outer(GX))  7.13 us
    pallas_call x1, Pallas kernels, collision(): pl.pallas_call(collide_kernel, in_specs=[SMEM, VMEM, VMEM, HBM], out_spec...  4.9 us
    pallas_call x1, Pallas kernels, after_exchange(): pl.pallas_call(last_kernel, in_specs=[HBM if n == 3 else VMEM for n in ra...  4.02 us
    pallas_call x1, Pallas kernels, before_exchange(): pl.pallas_call(first_kernel, in_specs=[HBM, HBM, HBM], out_specs=[VMEM] *...  2.79 us
    ppermute x1, waiting for transfers between devices, body(): xb = lax.ppermute(xb, 'gx', outer(GX))  1.48 us
    ppermute x1, starting transfers between devices, body(): xa = lax.ppermute(xa, 'gx', inner(GX))  1.47 us
  transfers between devices with their start and end apart: 5, of which 1 were waited for; matrix products, arithmetic and copies ran while one was open for 0% of the time, Pallas kernels for 10%

profile of v3, /device:TPU:1, one launch (start us, length us, event | category | flops | bytes accessed | tf_op | source)
XLA Modules:
  0.0 55.1 jit_solution(8978458512180248796)
XLA Ops:
  0.6 0.0 copy-start.2
  0.6 0.0 copy-start.1
  0.7 0.0 copy-start
  0.7 0.0 copy-start.3
  0.7 2.8 %before_exchange.1 = (f32[128,8,128]{2,1,0:T(8,128)}, f32[9,32,128]{2,1,0:T(8,128)S(1)}, f32[9,32,128]{2,1,0:T(8,128)S(1)}, f32[9,8,128]{2,1,0:T(8,128)S(1)}, f32[9,8,128]{2,1,0:T(8,128)S(1)}) custom-call(f32[27]{0:T(128)} %rates_ref.1, f32[27,8,32,128]{3,2,1,0:T(8,128)} %pop_hbm.3, f32[27,2,32,128]{3,2,1,0:T(8,128)} %pre_hbm.1), custom_call_target="tpu_custom_call" | custom-call | tf_op jit(solution)/shard_map/before_exchange/pallas_call | solution.py:230
  3.5 0.0 copy-start.4
  3.5 11.5 %all-to-all-start = ((f32[128,8,128]{2,1,0:T(8,128)}), f32[128,8,128]{2,1,0:T(8,128)S(1)}, u32[]{:S(2)}, u32[]{:S(2)}) async-start(f32[128,8,128]{2,1,0:T(8,128)} %get-tuple-element.17), calls=%async_computation | async-start | bytes 1048576 | tf_op jit(solution)/shard_map/all_to_all | solution.py:497
  15.0 1.5 %collective-permute-start = (f32[9,32,128]{2,1,0:T(8,128)S(1)}, f32[9,32,128]{2,1,0:T(8,128)S(1)}, u32[]{:S(2)}, u32[]{:S(2)}) collective-permute-start(f32[9,32,128]{2,1,0:T(8,128)S(1)} %get-tuple-element.19), channel_id=1, source_target_pairs={{0,4},{4,0},{8,12},{12,8},{16,20},{20,16},{24,28},{28,24},{32,36},... | collective-permute-start | bytes 442376 | tf_op jit(solution)/shard_map/ppermute | solution.py:501
  16.5 7.1 %collective-permute-start.1 = (f32[9,32,128]{2,1,0:T(8,128)S(1)}, f32[9,32,128]{2,1,0:T(8,128)S(1)}, u32[]{:S(2)}, u32[]{:S(2)}) collective-permute-start(f32[9,32,128]{2,1,0:T(8,128)S(1)} %get-tuple-element.20), channel_id=1, source_target_pairs={{0,124},{4,8},{8,4},{12,16},{16,12},{20,24},{24,20},{28,32},{32,28... | collective-permute-start | bytes 442376 | tf_op jit(solution)/shard_map/ppermute | solution.py:500
  23.6 0.9 %collective-permute-start.2 = (f32[9,8,128]{2,1,0:T(8,128)S(1)}, f32[9,8,128]{2,1,0:T(8,128)S(1)}, u32[]{:S(2)}, u32[]{:S(2)}) collective-permute-start(f32[9,8,128]{2,1,0:T(8,128)S(1)} %get-tuple-element.21), channel_id=1, source_target_pairs={{0,1},{1,0},{2,3},{3,2},{4,5},{5,4},{6,7},{7,6},{8,9},{9,8},{10,11... | collective-permute-start | bytes 110600 | tf_op jit(solution)/shard_map/ppermute | solution.py:503
  24.5 0.2 collective-permute-start.3
  24.7 0.0 copy-done.2
  24.7 0.0 copy-done.1
  24.7 0.0 copy-done
  24.7 4.9 %collision.1 = (f32[27,8,32,128]{3,2,1,0:T(8,128)}, f32[360,128]{1,0:T(8,128)S(1)}, f32[8,128]{1,0:T(8,128)S(1)}) custom-call(f32[27]{0:T(128)S(1)} %copy-done.2, s32[1,512]{1,0:T(1,128)S(1)} %bitcast.8, s32[1,512]{1,0:T(1,128)S(1)} %bitcast.9, f32[27,8,32,128]{3,2,1,0:T(8,128)} %pop_hbm.3), custom_call_target="tpu_custom_call" | custom-call | tf_op jit(solution)/shard_map/collision/pallas_call | solution.py:296
  29.6 0.0 all-to-all-done.got_ref
  29.6 0.0 copy-done.3
  29.6 0.7 %route.1 = f32[1152,128]{1,0:T(8,128)S(1)} custom-call(s32[32]{0:T(128)S(1)} %copy-done.3, f32[128,8,128]{2,1,0:T(8,128)S(1)} %all-to-all-done.got_ref, f32[8,128]{1,0:T(8,128)S(1)} %get-tuple-element.18.disc_ref), custom_call_target="tpu_custom_call" | custom-call | tf_op jit(solution)/shard_map/route/pallas_call | solution.py:334
  30.4 0.0 collective-permute-done.2.ya_ref
  30.4 0.0 collective-permute-done.3.yb_ref
  30.4 0.0 collective-permute-done.xa_ref
  30.4 1.5 %collective-permute-done.1.xb_ref = f32[9,32,128]{2,1,0:T(8,128)S(1)} collective-permute-done((f32[9,32,128]{2,1,0:T(8,128)S(1)}, f32[9,32,128]{2,1,0:T(8,128)S(1)}, u32[]{:S(2)}, u32[]{:S(2)}) %collective-permute-start.1) | collective-permute-done | bytes 147488 | tf_op jit(solution)/shard_map/ppermute | solution.py:500
  31.9 19.2 %all_to_all.10 = f32[128,9,1,128]{3,2,1,0:T(1,128)S(1)} all-to-all(f32[128,9,1,128]{3,2,1,0:T(1,128)S(1)} %bitcast.6), channel_id=1, replica_groups=mesh['gx'=32,'gy'=4] {'gx','gy'}, dimensions={0} | all-to-all | bytes 1179648 | tf_op jit(solution)/shard_map/all_to_all | solution.py:506
  51.0 0.0 copy-done.4
  51.0 4.0 %after_exchange.1 = (f32[27,8,32,128]{3,2,1,0:T(8,128)}, f32[1,32]{1,0:T(1,128)}) custom-call(f32[1152,128]{1,0:T(8,128)S(1)} %bitcast.7, f32[360,128]{1,0:T(8,128)S(1)} %get-tuple-element.24.w_ref, f32[1,32]{1,0:T(1,128)S(1)} %bitcast.10, f32[27,8,32,128]{3,2,1,0:T(8,128)} %get-tuple-element.25.r_hbm, f32[9,32,128]{2,1,0:T(8,128)S(1)} %collective-permute-done.xa_ref, ...), custom_call_target="tpu_custom_call" | custom-call | tf_op jit(solution)/shard_map/after_exchange/pallas_call | solution.py:469
Async XLA Ops:
  0.6 24.1 %copy-start.2 = (f32[27]{0:T(128)S(1)}, f32[27]{0:T(128)}, u32[]{:S(2)}) copy-start(f32[27]{0:T(128)} %rates_ref.1) | copy-start | bytes 328
  0.6 24.1 %copy-start.1 = (s32[512]{0:T(512)S(1)}, s32[512]{0:T(512)}, u32[]{:S(2)}) copy-start(s32[512]{0:T(512)} %param.13) | copy-start | bytes 6148
  0.7 24.1 %copy-start = (s32[512]{0:T(512)S(1)}, s32[512]{0:T(512)}, u32[]{:S(2)}) copy-start(s32[512]{0:T(512)} %param.12) | copy-start | bytes 6148
  0.7 29.0 %copy-start.3 = (s32[32]{0:T(128)S(1)}, s32[32]{0:T(128)}, u32[]{:S(2)}) copy-start(s32[32]{0:T(128)} %pairing_ref.1) | copy-start | bytes 388
  3.5 47.6 %copy-start.4 = (f32[32]{0:T(128)S(1)}, f32[32]{0:T(128)}, u32[]{:S(2)}) copy-start(f32[32]{0:T(128)} %param.11) | copy-start | bytes 388
  3.5 26.1 %all-to-all-start = ((f32[128,8,128]{2,1,0:T(8,128)}), f32[128,8,128]{2,1,0:T(8,128)S(1)}, u32[]{:S(2)}, u32[]{:S(2)}) async-start(f32[128,8,128]{2,1,0:T(8,128)} %get-tuple-element.17), calls=%async_computation | async-start | bytes 1048576 | tf_op jit(solution)/shard_map/all_to_all | solution.py:497
  15.0 15.4 %collective-permute-start = (f32[9,32,128]{2,1,0:T(8,128)S(1)}, f32[9,32,128]{2,1,0:T(8,128)S(1)}, u32[]{:S(2)}, u32[]{:S(2)}) collective-permute-start(f32[9,32,128]{2,1,0:T(8,128)S(1)} %get-tuple-element.19), channel_id=1, source_target_pairs={{0,4},{4,0},{8,12},{12,8},{16,20},{20,16},{24,28},{28,24},{32,36},... | collective-permute-start | bytes 442376 | tf_op jit(solution)/shard_map/ppermute | solution.py:501
  16.5 15.4 %collective-permute-start.1 = (f32[9,32,128]{2,1,0:T(8,128)S(1)}, f32[9,32,128]{2,1,0:T(8,128)S(1)}, u32[]{:S(2)}, u32[]{:S(2)}) collective-permute-start(f32[9,32,128]{2,1,0:T(8,128)S(1)} %get-tuple-element.20), channel_id=1, source_target_pairs={{0,124},{4,8},{8,4},{12,16},{16,12},{20,24},{24,20},{28,32},{32,28... | collective-permute-start | bytes 442376 | tf_op jit(solution)/shard_map/ppermute | solution.py:500
  23.6 6.8 %collective-permute-start.2 = (f32[9,8,128]{2,1,0:T(8,128)S(1)}, f32[9,8,128]{2,1,0:T(8,128)S(1)}, u32[]{:S(2)}, u32[]{:S(2)}) collective-permute-start(f32[9,8,128]{2,1,0:T(8,128)S(1)} %get-tuple-element.21), channel_id=1, source_target_pairs={{0,1},{1,0},{2,3},{3,2},{4,5},{5,4},{6,7},{7,6},{8,9},{9,8},{10,11... | collective-permute-start | bytes 110600 | tf_op jit(solution)/shard_map/ppermute | solution.py:503
  24.5 5.9 %collective-permute-start.3 = (f32[9,8,128]{2,1,0:T(8,128)S(1)}, f32[9,8,128]{2,1,0:T(8,128)S(1)}, u32[]{:S(2)}, u32[]{:S(2)}) collective-permute-start(f32[9,8,128]{2,1,0:T(8,128)S(1)} %get-tuple-element.22), channel_id=1, source_target_pairs={{0,3},{1,2},{2,1},{3,0},{4,7},{5,6},{6,5},{7,4},{8,11},{9,10},{10,... | collective-permute-start | bytes 110600 | tf_op jit(solution)/shard_map/ppermute | solution.py:502

commit v4 on v3

--- a/solution.py
+++ b/solution.py
@@ -161,8 +161,8 @@
     return out
 
 
-def first_kernel(rates_hbm, pop_hbm, pre_hbm, send_ref, xa_ref, xb_ref, ya_ref, yb_ref, pre_ref, edge_ref, side_ref,
-                 rates_ref, sems):
+def first_kernel(rates_hbm, pop_hbm, pre_hbm, send_hbm, xa_ref, xb_ref, ya_ref, yb_ref, pre_ref, edge_ref, side_ref,
+                 rates_ref, send_ref, sems):
     copies = [pltpu.make_async_copy(pre_hbm.at[:, p], pre_ref.at[:, p], sems.at[p]) for p in range(2)]
     for n, x in enumerate((0, XW - 1)):
         copies.append(pltpu.make_async_copy(pop_hbm.at[:, x], edge_ref.at[:, n], sems.at[2 + n]))
@@ -191,6 +191,9 @@
                         send_ref[LO_NEXT, k:k + 1, :] = c[k][7:8, :]
                     if q == 0:
                         send_ref[HI_NEXT, k:k + 1, :] = c[k][0:1, :]
+    sends = [pltpu.make_async_copy(send_ref.at[0:LO_OWN], send_hbm.at[0:LO_OWN], sems.at[7]),
+             pltpu.make_async_copy(send_ref.at[LO_OWN:NDEV], send_hbm.at[LO_OWN:NDEV], sems.at[8])]
+    sends[0].start()
     copies[4].wait()
     lane = lax.broadcasted_iota(jnp.int32, (8, Z), 1)
     odd_x = (lax.axis_index("gx") & 1) == 1
@@ -224,20 +227,24 @@
                 if cx:
                     at = 0 if cx < 0 else XW - 1
                     send_ref[CORNER + CORNERS.index((cx, cy)), cz + 1:cz + 2, :] = value[at:at + 1, :]
+    sends[1].start()
+    for copy in sends:
+        copy.wait()
 
 
 def before_exchange(rates, populations, precursor):
     return pl.pallas_call(
         first_kernel,
         in_specs=[HBM, HBM, HBM],
-        out_specs=[VMEM] * 5,
-        out_shape=[pltpu.VMEM((NDEV, 8, Z), F32)] + [pltpu.VMEM((9, n, Z), F32) for n in (YW, YW, XW, XW)],
+        out_specs=[HBM] + [VMEM] * 4,
+        out_shape=[pltpu.HBM((NDEV, 8, Z), F32)] + [pltpu.VMEM((9, n, Z), F32) for n in (YW, YW, XW, XW)],
         scratch_shapes=[
             pltpu.VMEM((27, 2, YW, Z), F32),
             pltpu.VMEM((27, 2, YW, Z), F32),
             pltpu.VMEM((2, 27, XW, Z), F32),
             pltpu.SMEM((27,), F32),
-            pltpu.SemaphoreType.DMA((7,)),
+            pltpu.VMEM((NDEV, 8, Z), F32),
+            pltpu.SemaphoreType.DMA((9,)),
         ],
         name="before_exchange",
         compiler_params=pltpu.CompilerParams(vmem_limit_bytes=4 << 20),
@@ -309,7 +316,7 @@
     )(rates, cols, turb, far(populations))
 
 
-def route_kernel(pairing_ref, got_ref, disc_ref, send_ref):
+def route_kernel(pairing_ref, got_ref, disc_ref, send_hbm, send_ref, sems):
     me = lax.axis_index("gx") * GY + lax.axis_index("gy")
     is_next = ((me >= NEXT) & (me < LO_OWN)) | (me == LO_NEXT) | (me == HI_NEXT)
     corner = me - CORNER
@@ -321,6 +328,7 @@
     ahead = jnp.where(is_next, 1, 0)
     lanes = [(t + from_y) & (GY - 1) for t in range(GY)]
     part = jnp.sum(disc_ref[...], axis=0, keepdims=True)
+    copies = []
     for d in range(GX):
         tile = pairing_ref[(d + ahead) & (GX - 1)]
         tile = jnp.where(is_corner, (d + from_x) & (GX - 1), tile) * GY
@@ -328,20 +336,49 @@
             at = (d * GY + t) * PIECE
             send_ref[at:at + 8, :] = got_ref[tile + lanes[t], :, :]
             send_ref[at + 8:at + 9, :] = part
+        if d % 8 == 7:
+            rows = slice((d - 7) * GY * PIECE, (d + 1) * GY * PIECE)
+            copies.append(pltpu.make_async_copy(send_ref.at[rows], send_hbm.at[rows], sems.at[d // 8]))
+            copies[-1].start()
+    for copy in copies:
+        copy.wait()
 
 
 def route(pairing, got, disc):
     return pl.pallas_call(
         route_kernel,
         in_specs=[SMEM, VMEM, VMEM],
-        out_specs=VMEM,
-        out_shape=pltpu.VMEM((NDEV * PIECE, Z), F32),
+        out_specs=HBM,
+        out_shape=pltpu.HBM((NDEV * PIECE, Z), F32),
+        scratch_shapes=[pltpu.VMEM((NDEV * PIECE, Z), F32), pltpu.SemaphoreType.DMA((GX // 8,))],
         name="route",
         compiler_params=pltpu.CompilerParams(vmem_limit_bytes=3 << 20),
     )(pairing, near(got), near(disc))
 
 
-def last_kernel(got_ref, w_ref, loading_ref, r_hbm, xa_ref, xb_ref, ya_ref, yb_ref, out_hbm, speed_ref,
+def side_kernel(xa_ref, xb_ref, ya_ref, yb_ref, xm_ref, xp_ref, ym_ref, yp_ref):
+    odd_x = (lax.axis_index("gx") & 1) == 1
+    odd_y = (lax.axis_index("gy") & 1) == 1
+    for k in range(9):
+        xm_ref[k] = jnp.where(odd_x, xb_ref[k], xa_ref[k])
+        xp_ref[k] = jnp.where(odd_x, xa_ref[k], xb_ref[k])
+        ym_ref[k] = jnp.where(odd_y, yb_ref[k], ya_ref[k])
+        yp_ref[k] = jnp.where(odd_y, ya_ref[k], yb_ref[k])
+
+
+def sides(*borders):
+    return pl.pallas_call(
+        side_kernel,
+        in_specs=[VMEM] * 4,
+        out_specs=[VMEM] * 4,
+        out_shape=[pltpu.VMEM(b.shape, F32) for b in borders],
+        name="sides",
+        compiler_params=pltpu.CompilerParams(vmem_limit_bytes=2 << 20),
+        cost_estimate=pl.CostEstimate(flops=7 * 10**9, transcendentals=0, bytes_accessed=10**6),
+    )(*[near(b) for b in borders])
+
+
+def last_kernel(got_ref, w_ref, loading_ref, r_hbm, xm_ref, xp_ref, ym_ref, yp_ref, out_hbm, speed_ref,
                 rp, force, load_scr, lo_scr, hi_scr, yp_scr, ym_scr, r_ref, out_scr, in_sems, sems):
     def copy_in(x):
         return pltpu.make_async_copy(r_hbm.at[:, x], r_ref.at[:, x], in_sems.at[x])
@@ -353,9 +390,6 @@
     up = jnp.where(lane == 0, -profile, pltpu.roll(profile, 1, 1))
     down = jnp.where(lane == Z - 1, -profile, pltpu.roll(profile, Z - 1, 1))
     along = (3.0 * down, 3.0 * profile, 3.0 * up)
-
-    odd_x = (lax.axis_index("gx") & 1) == 1
-    odd_y = (lax.axis_index("gy") & 1) == 1
 
     def got(tile, a=0, b=8):
         return got_ref[PIECE * tile + a:PIECE * tile + b, :]
@@ -379,8 +413,8 @@
         w_ref[0:352, :] * thrust[0:1, :], jnp.ones((128, Z), F32), (((1,), (0,)), ((), ())),
         precision=lax.Precision.HIGHEST, preferred_element_type=F32)
     for scr, tile, nxt, halo, frow, cy, out in (
-        (lo_scr, LO_OWN, LO_NEXT, (ya_ref, yb_ref), 320, 1, yp_scr),
-        (hi_scr, HI_OWN, HI_NEXT, (yb_ref, ya_ref), 336, -1, ym_scr),
+        (lo_scr, LO_OWN, LO_NEXT, yp_ref, 320, 1, yp_scr),
+        (hi_scr, HI_OWN, HI_NEXT, ym_ref, 336, -1, ym_scr),
     ):
         scr[...] = jnp.zeros_like(scr)
         for c in range(10):
@@ -397,7 +431,7 @@
                 i = slot(cx, cy, cz)
                 b = built[i]
                 b = b if cz == 0 else pltpu.roll(b, cz % Z, 1)
-                out[k, 1:9, :] = (1.0 - blend) * push(jnp.where(odd_y, halo[0][k], halo[1][k]), i, fs) + blend * b
+                out[k, 1:9, :] = (1.0 - blend) * push(halo[k], i, fs) + blend * b
         for cz in (-1, 0, 1):
             n = CORNERS.index((1, cy))
             out[6 + cz + 1, 0:1, :] = got(CORNER + n, cz + 1, cz + 2) + (
@@ -415,7 +449,7 @@
         into = slice(8 * q + 8, 8 * q + 16)
         fs = pushes(force[rows, :])
         for k in range(9):
-            rp[18 + k, 0, into, :] = push(jnp.where(odd_x, xa_ref[k, rows, :], xb_ref[k, rows, :]), 18 + k, fs)
+            rp[18 + k, 0, into, :] = push(xp_ref[k, rows, :], 18 + k, fs)
         for p in range(2):
             built = z_stream(rebuild([got(OWN + (2 * k + p) * 4 + q) for k in range(10)]), lane)
             fs = pushes(force[YW * (p + 1) + 8 * q:YW * (p + 1) + 8 * q + 8, :])
@@ -426,7 +460,7 @@
         for k in range(9):
             cz = k % 3 - 1
             b = built[k] if cz == 0 else pltpu.roll(built[k], cz % Z, 1)
-            rp[k, XW + 1, into, :] = (1.0 - BLEND[0]) * push(jnp.where(odd_x, xb_ref[k, rows, :], xa_ref[k, rows, :]), k, fs) + BLEND[0] * b
+            rp[k, XW + 1, into, :] = (1.0 - BLEND[0]) * push(xm_ref[k, rows, :], k, fs) + BLEND[0] * b
 
     wide_lane = lax.broadcasted_iota(jnp.int32, (YW, Z), 1)
     wide_row = lax.broadcasted_iota(jnp.int32, (YW, Z), 0)
@@ -501,10 +535,9 @@
     xa = lax.ppermute(xa, "gx", inner(GX))
     yb = lax.ppermute(yb, "gy", outer(GY))
     ya = lax.ppermute(ya, "gy", inner(GY))
-    send, xa, xb, ya, yb = lax.optimization_barrier((route(pairing, got, disc), xa, xb, ya, yb))
-    send = send.reshape(NDEV, PIECE, 1, Z)
+    send = route(pairing, got, disc).reshape(NDEV, PIECE, 1, Z)
     got = lax.all_to_all(send, both, 0, 0, tiled=True).reshape(NDEV * PIECE, Z)
-    read, speed = after_exchange(got, w, loading.reshape(1, TURBINES), r, xa, xb, ya, yb)
+    read, speed = after_exchange(got, w, loading.reshape(1, TURBINES), r, *sides(xa, xb, ya, yb))
     return read, speed.reshape(TURBINES)
 
 

time: 55.3 us -> 53.8 us (0.973)
  blocking collectives: 19.2 us -> 0 us
  waiting for transfers between devices: 1.49 us -> 14 us
  starting transfers between devices: 21.2 us -> 25.7 us
  Pallas kernels: 12.4 us -> 13 us
    all_to_all x1 -> x0, blocking collectives: 19.2 us -> none  [body(): got = lax.all_to_all(send, both, 0, 0, tiled=True).reshape(NDEV * PIECE, Z)]
    all_to_all x0 -> x1, waiting for transfers between devices: none -> 14 us  [body(): got = lax.all_to_all(send, both, 0, 0, tiled=True).reshape(NDEV * PIECE, Z)]
    all_to_all x0 -> x1, starting transfers between devices: none -> 4.47 us  [body(): got = lax.all_to_all(send, both, 0, 0, tiled=True).reshape(NDEV * PIECE, Z)]
    ppermute x1, waiting for transfers between devices: 1.48 us -> 0.01 us  [body(): xb = lax.ppermute(xb, 'gx', outer(GX))]
    pallas_call x2 -> x3, Pallas kernels: 3.52 us -> 4.14 us  [the longest x1 2.65 us: before_exchange(): pl.pallas_call(first_kernel, in_specs=[HBM, HBM, HBM], out_specs=[HBM] +...]
  transfers between devices with their start and end apart: 5 -> 6, of which waited for: 1 -> 1; matrix products, arithmetic and copies ran while one was open for 0% -> 0% of each run, Pallas kernels for 10% -> 12%
where the time goes in v4:
time: 53.8 us; the launch traced here: 53.5 us
  starting transfers between devices  25.7 us (48%)
  waiting for transfers between devices  14 us (26%)
  Pallas kernels  13 us (24%)
  between operations  0.77 us (1%)
    all_to_all x1, waiting for transfers between devices, body(): got = lax.all_to_all(send, both, 0, 0, tiled=True).reshape(NDEV * PIECE, Z)  14 us
    all_to_all x1, starting transfers between devices, body(): got = lax.all_to_all(send, both, 0, 0, tiled=True)  11.5 us
    ppermute x1, starting transfers between devices, body(): xb = lax.ppermute(xb, 'gx', outer(GX))  7.13 us
    pallas_call x1, Pallas kernels, collision(): pl.pallas_call(collide_kernel, in_specs=[SMEM, VMEM, VMEM, HBM], out_spec...  4.89 us
    all_to_all x1, starting transfers between devices, body(): got = lax.all_to_all(send, both, 0, 0, tiled=True).reshape(NDEV * PIECE, Z)  4.47 us
    pallas_call x1, Pallas kernels, after_exchange(): pl.pallas_call(last_kernel, in_specs=[HBM if n == 3 else VMEM for n in ra...  3.98 us
    pallas_call x1, Pallas kernels, before_exchange(): pl.pallas_call(first_kernel, in_specs=[HBM, HBM, HBM], out_specs=[HBM] +...  2.65 us
    ppermute x1, starting transfers between devices, body(): xa = lax.ppermute(xa, 'gx', inner(GX))  1.47 us
  transfers between devices with their start and end apart: 6, of which 1 were waited for; matrix products, arithmetic and copies ran while one was open for 0% of the time, Pallas kernels for 12%

profile of v4, /device:TPU:1, one launch (start us, length us, event | category | flops | bytes accessed | tf_op | source)
XLA Modules:
  0.0 53.5 jit_solution(12281214721612741384)
XLA Ops:
  0.6 0.0 copy-start.2
  0.6 0.0 copy-start.1
  0.7 0.0 copy-start
  0.7 0.0 copy-start.3
  0.7 2.7 %before_exchange.1 = (f32[128,8,128]{2,1,0:T(8,128)}, f32[9,32,128]{2,1,0:T(8,128)S(1)}, f32[9,32,128]{2,1,0:T(8,128)S(1)}, f32[9,8,128]{2,1,0:T(8,128)S(1)}, f32[9,8,128]{2,1,0:T(8,128)S(1)}) custom-call(f32[27]{0:T(128)} %rates_ref.1, f32[27,8,32,128]{3,2,1,0:T(8,128)} %pop_hbm.3, f32[27,2,32,128]{3,2,1,0:T(8,128)} %pre_hbm.1), custom_call_target="tpu_custom_call" | custom-call | tf_op jit(solution)/shard_map/before_exchange/pallas_call | solution.py:236
  3.3 11.5 %all-to-all-start = ((f32[128,8,128]{2,1,0:T(8,128)}), f32[128,8,128]{2,1,0:T(8,128)S(1)}, u32[]{:S(2)}, u32[]{:S(2)}) async-start(f32[128,8,128]{2,1,0:T(8,128)} %get-tuple-element.16), calls=%async_computation | async-start | bytes 1048576 | tf_op jit(solution)/shard_map/all_to_all | solution.py:531
  14.8 1.5 %collective-permute-start = (f32[9,32,128]{2,1,0:T(8,128)S(1)}, f32[9,32,128]{2,1,0:T(8,128)S(1)}, u32[]{:S(2)}, u32[]{:S(2)}) collective-permute-start(f32[9,32,128]{2,1,0:T(8,128)S(1)} %get-tuple-element.20), channel_id=1, source_target_pairs={{0,4},{4,0},{8,12},{12,8},{16,20},{20,16},{24,28},{28,24},{32,36},... | collective-permute-start | bytes 442376 | tf_op jit(solution)/shard_map/ppermute | solution.py:535
  16.3 7.1 %collective-permute-start.1 = (f32[9,32,128]{2,1,0:T(8,128)S(1)}, f32[9,32,128]{2,1,0:T(8,128)S(1)}, u32[]{:S(2)}, u32[]{:S(2)}) collective-permute-start(f32[9,32,128]{2,1,0:T(8,128)S(1)} %get-tuple-element.21), channel_id=1, source_target_pairs={{0,124},{4,8},{8,4},{12,16},{16,12},{20,24},{24,20},{28,32},{32,28... | collective-permute-start | bytes 442376 | tf_op jit(solution)/shard_map/ppermute | solution.py:534
  23.4 0.9 %collective-permute-start.2 = (f32[9,8,128]{2,1,0:T(8,128)S(1)}, f32[9,8,128]{2,1,0:T(8,128)S(1)}, u32[]{:S(2)}, u32[]{:S(2)}) collective-permute-start(f32[9,8,128]{2,1,0:T(8,128)S(1)} %get-tuple-element.22), channel_id=1, source_target_pairs={{0,1},{1,0},{2,3},{3,2},{4,5},{5,4},{6,7},{7,6},{8,9},{9,8},{10,11... | collective-permute-start | bytes 110600 | tf_op jit(solution)/shard_map/ppermute | solution.py:537
  24.4 0.2 collective-permute-start.3
  24.5 0.0 copy-done.2
  24.6 0.0 copy-done.1
  24.6 0.0 copy-done
  24.6 4.9 %collision.1 = (f32[27,8,32,128]{3,2,1,0:T(8,128)}, f32[360,128]{1,0:T(8,128)S(1)}, f32[8,128]{1,0:T(8,128)S(1)}) custom-call(f32[27]{0:T(128)S(1)} %copy-done.2, s32[1,512]{1,0:T(1,128)S(1)} %bitcast.7, s32[1,512]{1,0:T(1,128)S(1)} %bitcast.8, f32[27,8,32,128]{3,2,1,0:T(8,128)} %pop_hbm.3), custom_call_target="tpu_custom_call" | custom-call | tf_op jit(solution)/shard_map/collision/pallas_call | solution.py:303
  29.5 0.0 all-to-all-done.got_ref
  29.5 0.0 copy-done.3
  29.5 1.4 %route.1 = f32[1152,128]{1,0:T(8,128)} custom-call(s32[32]{0:T(128)S(1)} %copy-done.3, f32[128,8,128]{2,1,0:T(8,128)S(1)} %all-to-all-done.got_ref, f32[8,128]{1,0:T(8,128)S(1)} %get-tuple-element.17.disc_ref), custom_call_target="tpu_custom_call" | custom-call | tf_op jit(solution)/shard_map/route/pallas_call | solution.py:348
  30.9 4.5 %all-to-all-start.1 = ((f32[128,9,1,128]{3,2,1,0:T(1,128)}), f32[128,9,1,128]{3,2,1,0:T(1,128)S(1)}, u32[]{:S(2)}, u32[]{:S(2)}) async-start(f32[128,9,1,128]{3,2,1,0:T(1,128)} %bitcast.10), calls=%async_computation.1 | async-start | bytes 1179648 | tf_op jit(solution)/shard_map/all_to_all | solution.py:539
  35.4 0.0 copy-start.4
  35.4 0.0 collective-permute-done.2.ya_ref
  35.4 0.0 collective-permute-done.3.yb_ref
  35.4 0.0 collective-permute-done.xa_ref
  35.5 0.0 collective-permute-done.1.xb_ref
  35.5 14.0 %all-to-all-done.1 = f32[128,9,1,128]{3,2,1,0:T(1,128)S(1)} async-done(((f32[128,9,1,128]{3,2,1,0:T(1,128)}), f32[128,9,1,128]{3,2,1,0:T(1,128)S(1)}, u32[]{:S(2)}, u32[]{:S(2)}) %all-to-all-start.1) | async-done | bytes 589856 | tf_op jit(solution)/shard_map/all_to_all | solution.py:539
  49.5 0.0 copy-done.4
  49.5 4.0 %after_exchange.1 = (f32[27,8,32,128]{3,2,1,0:T(8,128)}, f32[1,32]{1,0:T(1,128)}) custom-call(f32[1152,128]{1,0:T(8,128)S(1)} %bitcast.6, f32[360,128]{1,0:T(8,128)S(1)} %get-tuple-element.18.w_ref, f32[1,32]{1,0:T(1,128)S(1)} %bitcast.9, f32[27,8,32,128]{3,2,1,0:T(8,128)} %get-tuple-element.19.r_hbm, f32[9,32,128]{2,1,0:T(8,128)S(1)} %get-tuple-element.24.xm_ref, ...), custom_call_target="tpu_custom_call" | custom-call | tf_op jit(solution)/shard_map/after_exchange/pallas_call | solution.py:503
  (1 shorter events, 0.0 us)
Async XLA Ops:
  0.6 23.9 %copy-start.2 = (f32[27]{0:T(128)S(1)}, f32[27]{0:T(128)}, u32[]{:S(2)}) copy-start(f32[27]{0:T(128)} %rates_ref.1) | copy-start | bytes 328
  0.6 23.9 %copy-start.1 = (s32[512]{0:T(512)S(1)}, s32[512]{0:T(512)}, u32[]{:S(2)}) copy-start(s32[512]{0:T(512)} %param.13) | copy-start | bytes 6148
  0.7 23.9 %copy-start = (s32[512]{0:T(512)S(1)}, s32[512]{0:T(512)}, u32[]{:S(2)}) copy-start(s32[512]{0:T(512)} %param.12) | copy-start | bytes 6148
  0.7 28.8 %copy-start.3 = (s32[32]{0:T(128)S(1)}, s32[32]{0:T(128)}, u32[]{:S(2)}) copy-start(s32[32]{0:T(128)} %pairing_ref.1) | copy-start | bytes 388
  3.3 26.1 %all-to-all-start = ((f32[128,8,128]{2,1,0:T(8,128)}), f32[128,8,128]{2,1,0:T(8,128)S(1)}, u32[]{:S(2)}, u32[]{:S(2)}) async-start(f32[128,8,128]{2,1,0:T(8,128)} %get-tuple-element.16), calls=%async_computation | async-start | bytes 1048576 | tf_op jit(solution)/shard_map/all_to_all | solution.py:531
  14.8 20.6 %collective-permute-start = (f32[9,32,128]{2,1,0:T(8,128)S(1)}, f32[9,32,128]{2,1,0:T(8,128)S(1)}, u32[]{:S(2)}, u32[]{:S(2)}) collective-permute-start(f32[9,32,128]{2,1,0:T(8,128)S(1)} %get-tuple-element.20), channel_id=1, source_target_pairs={{0,4},{4,0},{8,12},{12,8},{16,20},{20,16},{24,28},{28,24},{32,36},... | collective-permute-start | bytes 442376 | tf_op jit(solution)/shard_map/ppermute | solution.py:535
  16.3 19.1 %collective-permute-start.1 = (f32[9,32,128]{2,1,0:T(8,128)S(1)}, f32[9,32,128]{2,1,0:T(8,128)S(1)}, u32[]{:S(2)}, u32[]{:S(2)}) collective-permute-start(f32[9,32,128]{2,1,0:T(8,128)S(1)} %get-tuple-element.21), channel_id=1, source_target_pairs={{0,124},{4,8},{8,4},{12,16},{16,12},{20,24},{24,20},{28,32},{32,28... | collective-permute-start | bytes 442376 | tf_op jit(solution)/shard_map/ppermute | solution.py:534
  23.4 12.0 %collective-permute-start.2 = (f32[9,8,128]{2,1,0:T(8,128)S(1)}, f32[9,8,128]{2,1,0:T(8,128)S(1)}, u32[]{:S(2)}, u32[]{:S(2)}) collective-permute-start(f32[9,8,128]{2,1,0:T(8,128)S(1)} %get-tuple-element.22), channel_id=1, source_target_pairs={{0,1},{1,0},{2,3},{3,2},{4,5},{5,4},{6,7},{7,6},{8,9},{9,8},{10,11... | collective-permute-start | bytes 110600 | tf_op jit(solution)/shard_map/ppermute | solution.py:537
  24.4 11.1 %collective-permute-start.3 = (f32[9,8,128]{2,1,0:T(8,128)S(1)}, f32[9,8,128]{2,1,0:T(8,128)S(1)}, u32[]{:S(2)}, u32[]{:S(2)}) collective-permute-start(f32[9,8,128]{2,1,0:T(8,128)S(1)} %get-tuple-element.23), channel_id=1, source_target_pairs={{0,3},{1,2},{2,1},{3,0},{4,7},{5,6},{6,5},{7,4},{8,11},{9,10},{10,... | collective-permute-start | bytes 110600 | tf_op jit(solution)/shard_map/ppermute | solution.py:536
  30.9 18.6 %all-to-all-start.1 = ((f32[128,9,1,128]{3,2,1,0:T(1,128)}), f32[128,9,1,128]{3,2,1,0:T(1,128)S(1)}, u32[]{:S(2)}, u32[]{:S(2)}) async-start(f32[128,9,1,128]{3,2,1,0:T(1,128)} %bitcast.10), calls=%async_computation.1 | async-start | bytes 1179648 | tf_op jit(solution)/shard_map/all_to_all | solution.py:539
  35.4 14.1 %copy-start.4 = (f32[32]{0:T(128)S(1)}, f32[32]{0:T(128)}, u32[]{:S(2)}) copy-start(f32[32]{0:T(128)} %param.11) | copy-start | bytes 388

commit v5 on v4

--- a/solution.py
+++ b/solution.py
@@ -356,35 +356,128 @@
     )(pairing, near(got), near(disc))
 
 
-def side_kernel(xa_ref, xb_ref, ya_ref, yb_ref, xm_ref, xp_ref, ym_ref, yp_ref):
+def changed(used_ref, p):
+    return (p == 0) | (p == 1) | (p == XW) | (used_ref[p + 1] > 0)
+
+
+def late(used_ref, x, cx):
+    if cx == 0:
+        return x < len(BLEND)
+    return changed(used_ref, x) | changed(used_ref, x - cx)
+
+
+def stream_group(rp, low_scr, high_scr, out_scr, x, cx):
+    lane = lax.broadcasted_iota(jnp.int32, (YW, Z), 1)
+    row = lax.broadcasted_iota(jnp.int32, (YW, Z), 0)
+    at = x + 1 - cx
+    for cy in (-1, 0, 1):
+        for cz in (-1, 0, 1):
+            i = slot(cx, cy, cz)
+            k = 3 * (cx + 1) + cz + 1
+            value = rp[i, at, 8 - cy:40 - cy, :]
+            if cy == 1:
+                value = jnp.where(row == 0, low_scr[k, pl.ds(at, 1), :], value)
+            elif cy == -1:
+                value = jnp.where(row == YW - 1, high_scr[k, pl.ds(at, 1), :], value)
+            if cz != 0 and (cx != 0 or cy != 0):
+                value = jnp.where(lane == (0 if cz == 1 else Z - 1), rp[i, x + 1, 8:40, :], value)
+            out_scr[i, x, :, :] = value
+
+
+def group_copy(out_scr, out_hbm, sems, x, cx):
+    group = slice(9 * (cx + 1), 9 * (cx + 2))
+    return pltpu.make_async_copy(out_scr.at[group, x], out_hbm.at[group, x], sems.at[x, cx + 1])
+
+
+HELD = (0, 1, 2, XW - 1)
+
+
+def early_kernel(w_ref, r_hbm, xa_ref, xb_ref, ya_ref, yb_ref, out_hbm, xm_ref, xp_ref, ym_ref, yp_ref, held_ref,
+                 used_ref, rp, low_scr, high_scr, out_scr, in_sems, held_sems, sems):
+    first = len(BLEND)
+
+    def copy_in(x):
+        return pltpu.make_async_copy(r_hbm.at[:, x], rp.at[:, x + 1, 8:40, :], in_sems.at[x])
+
+    for x in range(first, XW):
+        copy_in(x).start()
+    holds = [pltpu.make_async_copy(r_hbm.at[:, x], held_ref.at[:, n], held_sems.at[n]) for n, x in enumerate(HELD)]
+    for copy in holds:
+        copy.start()
+    for p in range(XW + 2):
+        beside = jnp.max(w_ref[320 + p:321 + p, :] + w_ref[336 + p:337 + p, :])
+        used_ref[p] = jnp.where(jnp.max(w_ref[YW * p:YW * p + YW, :]) + beside > 0.0, 1, 0)
     odd_x = (lax.axis_index("gx") & 1) == 1
     odd_y = (lax.axis_index("gy") & 1) == 1
     for k in range(9):
         xm_ref[k] = jnp.where(odd_x, xb_ref[k], xa_ref[k])
         xp_ref[k] = jnp.where(odd_x, xa_ref[k], xb_ref[k])
-        ym_ref[k] = jnp.where(odd_y, yb_ref[k], ya_ref[k])
-        yp_ref[k] = jnp.where(odd_y, ya_ref[k], yb_ref[k])
-
-
-def sides(*borders):
+        high = jnp.where(odd_y, yb_ref[k], ya_ref[k])
+        low = jnp.where(odd_y, ya_ref[k], yb_ref[k])
+        ym_ref[k] = high
+        yp_ref[k] = low
+        high_scr[k, 1:9, :] = high
+        low_scr[k, 1:9, :] = low
+    copy_in(first).wait()
+
+    def plane(x, carry):
+        @pl.when(x + 1 < XW)
+        def _():
+            copy_in(jnp.minimum(x + 1, XW - 1)).wait()
+
+        for cx in (-1, 0, 1):
+            @pl.when(jnp.logical_not(late(used_ref, x, cx)))
+            def _():
+                stream_group(rp, low_scr, high_scr, out_scr, x, cx)
+                group_copy(out_scr, out_hbm, sems, x, cx).start()
+        return carry
+
+    lax.fori_loop(first, XW, plane, 0)
+    for copy in holds:
+        copy.wait()
+    for x in range(first, XW):
+        for cx in (-1, 0, 1):
+            @pl.when(jnp.logical_not(late(used_ref, x, cx)))
+            def _():
+                group_copy(out_scr, out_hbm, sems, x, cx).wait()
+
+
+def stream_early(w, r, *borders):
     return pl.pallas_call(
-        side_kernel,
-        in_specs=[VMEM] * 4,
-        out_specs=[VMEM] * 4,
-        out_shape=[pltpu.VMEM(b.shape, F32) for b in borders],
-        name="sides",
-        compiler_params=pltpu.CompilerParams(vmem_limit_bytes=2 << 20),
+        early_kernel,
+        in_specs=[VMEM, HBM] + [VMEM] * 4,
+        out_specs=[HBM] + [VMEM] * 5 + [SMEM],
+        out_shape=[pltpu.HBM((27, XW, YW, Z), F32)] + [pltpu.VMEM(b.shape, F32) for b in borders]
+        + [pltpu.VMEM((27, len(HELD), YW, Z), F32), jax.ShapeDtypeStruct((XW + 2,), jnp.int32)],
+        scratch_shapes=[
+            pltpu.VMEM((27, XW + 2, 48, Z), F32),
+            pltpu.VMEM((9, 16, Z), F32),
+            pltpu.VMEM((9, 16, Z), F32),
+            pltpu.VMEM((27, XW, YW, Z), F32),
+            pltpu.SemaphoreType.DMA((XW,)),
+            pltpu.SemaphoreType.DMA((len(HELD),)),
+            pltpu.SemaphoreType.DMA((XW, 3)),
+        ],
+        name="stream_early",
+        compiler_params=pltpu.CompilerParams(vmem_limit_bytes=16 << 20),
         cost_estimate=pl.CostEstimate(flops=7 * 10**9, transcendentals=0, bytes_accessed=10**6),
-    )(*[near(b) for b in borders])
-
-
-def last_kernel(got_ref, w_ref, loading_ref, r_hbm, xm_ref, xp_ref, ym_ref, yp_ref, out_hbm, speed_ref,
+    )(near(w), far(r), *[near(b) for b in borders])
+
+
+def last_kernel(got_ref, w_ref, loading_ref, r_hbm, xm_ref, xp_ref, ym_ref, yp_ref, held_ref, used_ref, early_hbm,
+                out_hbm, speed_ref,
                 rp, force, load_scr, lo_scr, hi_scr, yp_scr, ym_scr, r_ref, out_scr, in_sems, sems):
     def copy_in(x):
         return pltpu.make_async_copy(r_hbm.at[:, x], r_ref.at[:, x], in_sems.at[x])
 
-    for x in range(XW):
-        copy_in(x).start()
+    def needed(p):
+        return changed(used_ref, p - 1) | changed(used_ref, p) | changed(used_ref, p + 1)
+
+    for x in range(3, XW - 1):
+        @pl.when(needed(x))
+        def _():
+            copy_in(x).start()
+
     lane = lax.broadcasted_iota(jnp.int32, (8, Z), 1)
     profile = profile_row()
     up = jnp.where(lane == 0, -profile, pltpu.roll(profile, 1, 1))
@@ -442,8 +535,6 @@
             b = b if cz == 0 else pltpu.roll(jnp.broadcast_to(b, (8, Z)), cz % Z, 1)[0:1, :]
             out[cz + 1, 9:10, :] = (1.0 - BLEND[0]) * value + BLEND[0] * b
 
-    copy_in(0).wait()
-    copy_in(1).wait()
     for q in range(4):
         rows = slice(8 * q, 8 * q + 8)
         into = slice(8 * q + 8, 8 * q + 16)
@@ -454,7 +545,12 @@
             built = z_stream(rebuild([got(OWN + (2 * k + p) * 4 + q) for k in range(10)]), lane)
             fs = pushes(force[YW * (p + 1) + 8 * q:YW * (p + 1) + 8 * q + 8, :])
             for i in range(27):
-                rp[i, p + 1, into, :] = (1.0 - BLEND[p]) * push(r_ref[i, p, rows, :], i, fs) + BLEND[p] * built[i]
+                rp[i, p + 1, into, :] = (1.0 - BLEND[p]) * push(held_ref[i, p, rows, :], i, fs) + BLEND[p] * built[i]
+        for n in range(2, len(HELD)):
+            x = HELD[n]
+            fs = pushes(force[YW * (x + 1) + 8 * q:YW * (x + 1) + 8 * q + 8, :])
+            for i in range(27):
+                rp[i, x + 1, into, :] = push(held_ref[i, n, rows, :], i, fs)
         fs = pushes(force[YW * (XW + 1) + 8 * q:YW * (XW + 1) + 8 * q + 8, :])
         built = rebuild_next([got(NEXT + 4 * k + q) for k in range(6)])
         for k in range(9):
@@ -462,47 +558,38 @@
             b = built[k] if cz == 0 else pltpu.roll(built[k], cz % Z, 1)
             rp[k, XW + 1, into, :] = (1.0 - BLEND[0]) * push(xm_ref[k, rows, :], k, fs) + BLEND[0] * b
 
-    wide_lane = lax.broadcasted_iota(jnp.int32, (YW, Z), 1)
-    wide_row = lax.broadcasted_iota(jnp.int32, (YW, Z), 0)
-
-    def copy_out(x):
-        return pltpu.make_async_copy(out_scr.at[:, x], out_hbm.at[:, x], sems.at[x])
-
-    def plane(x, carry):
-        @pl.when(x < XW - 2)
+    for x in range(3, XW - 1):
+        @pl.when(needed(x))
         def _():
-            copy_in(x + 2).wait()
+            copy_in(x).wait()
             for q in range(4):
                 rows = slice(8 * q, 8 * q + 8)
                 into = slice(8 * q + 8, 8 * q + 16)
-                fs = pushes(force[pl.ds(pl.multiple_of((x + 3) * YW + 8 * q, 8), 8), :])
+                fs = pushes(force[YW * (x + 1) + 8 * q:YW * (x + 1) + 8 * q + 8, :])
                 for i in range(27):
-                    rp[i, x + 3, into, :] = push(r_ref[i, x + 2, rows, :], i, fs)
-
-        for i in range(27):
-            cx, cy, cz = i // 9 - 1, i // 3 % 3 - 1, i % 3 - 1
-            at = x + 1 - cx
-            k = 3 * (cx + 1) + cz + 1
-            value = rp[i, at, 8 - cy:40 - cy, :]
-            if cy == 1:
-                value = jnp.where(wide_row == 0, yp_scr[k, pl.ds(at, 1), :], value)
-            elif cy == -1:
-                value = jnp.where(wide_row == YW - 1, ym_scr[k, pl.ds(at, 1), :], value)
-            if cz != 0 and (cx != 0 or cy != 0):
-                value = jnp.where(wide_lane == (0 if cz == 1 else Z - 1), rp[i, x + 1, 8:40, :], value)
-            out_scr[i, x, :, :] = value
-        copy_out(x).start()
+                    rp[i, x + 1, into, :] = push(r_ref[i, x, rows, :], i, fs)
+
+    def plane(x, carry):
+        for cx in (-1, 0, 1):
+            @pl.when(late(used_ref, x, cx))
+            def _():
+                stream_group(rp, yp_scr, ym_scr, out_scr, x, cx)
+                group_copy(out_scr, out_hbm, sems, x, cx).start()
         return carry
 
     lax.fori_loop(0, XW, plane, 0)
     for x in range(XW):
-        copy_out(x).wait()
+        for cx in (-1, 0, 1):
+            @pl.when(late(used_ref, x, cx))
+            def _():
+                group_copy(out_scr, out_hbm, sems, x, cx).wait()
 
 
 def after_exchange(*args):
     return pl.pallas_call(
         last_kernel,
-        in_specs=[HBM if n == 3 else VMEM for n in range(len(args))],
+        in_specs=[HBM if n in (3, 10) else SMEM if n == 9 else VMEM for n in range(len(args))],
+        input_output_aliases={10: 0},
         out_specs=[HBM, VMEM],
         out_shape=[pltpu.HBM((27, XW, YW, Z), F32), jax.ShapeDtypeStruct((1, TURBINES), F32)],
         scratch_shapes=[
@@ -516,11 +603,11 @@
             pltpu.VMEM((27, XW, YW, Z), F32),
             pltpu.VMEM((27, XW, YW, Z), F32),
             pltpu.SemaphoreType.DMA((XW,)),
-            pltpu.SemaphoreType.DMA((XW,)),
+            pltpu.SemaphoreType.DMA((XW, 3)),
         ],
         name="after_exchange",
         compiler_params=pltpu.CompilerParams(vmem_limit_bytes=24 << 20),
-    )(*[far(a) if n == 3 else near(a) for n, a in enumerate(args)])
+    )(*[far(a) if n in (3, 10) else a if n == 9 else near(a) for n, a in enumerate(args)])
 
 
 def body(populations, precursor, pairing, rates, loading, disc_cols, disc_turb):
@@ -537,7 +624,8 @@
     ya = lax.ppermute(ya, "gy", inner(GY))
     send = route(pairing, got, disc).reshape(NDEV, PIECE, 1, Z)
     got = lax.all_to_all(send, both, 0, 0, tiled=True).reshape(NDEV * PIECE, Z)
-    read, speed = after_exchange(got, w, loading.reshape(1, TURBINES), r, *sides(xa, xb, ya, yb))
+    read, *rest = stream_early(w, r, xa, xb, ya, yb)
+    read, speed = after_exchange(got, w, loading.reshape(1, TURBINES), r, *rest, read)
     return read, speed.reshape(TURBINES)
 
 

time: 53.8 us -> 53.3 us (level)
  waiting for transfers between devices: 14 us -> 10.1 us
  Pallas kernels: 13 us -> 16 us
    all_to_all x1, waiting for transfers between devices: 14 us -> 10.1 us  [body(): got = lax.all_to_all(send, both, 0, 0, tiled=True).reshape(NDEV * PIECE, Z)]
    pallas_call x2, Pallas kernels: 4.02 us -> 6.98 us  [the longest x1 3.97 us: stream_early(): pl.pallas_call(early_kernel, in_specs=[VMEM, HBM] + [VMEM] * 4, out_specs...]
  transfers between devices with their start and end apart: 6 -> 6, of which waited for: 1 -> 1; matrix products, arithmetic and copies ran while one was open for 0% -> 0% of each run, Pallas kernels for 12% -> 20%
where the time goes in v5:
time: 53.3 us; the launch traced here: 52.6 us
  starting transfers between devices  25.7 us (48%)
  Pallas kernels  16 us (30%)
  waiting for transfers between devices  10.1 us (19%)
  between operations  0.77 us (1%)
    all_to_all x1, starting transfers between devices, body(): got = lax.all_to_all(send, both, 0, 0, tiled=True)  11.5 us
    all_to_all x1, waiting for transfers between devices, body(): got = lax.all_to_all(send, both, 0, 0, tiled=True).reshape(NDEV * PIECE, Z)  10.1 us
    ppermute x1, starting transfers between devices, body(): xb = lax.ppermute(xb, 'gx', outer(GX))  7.13 us
    pallas_call x1, Pallas kernels, collision(): pl.pallas_call(collide_kernel, in_specs=[SMEM, VMEM, VMEM, HBM], out_spec...  4.89 us
    all_to_all x1, starting transfers between devices, body(): got = lax.all_to_all(send, both, 0, 0, tiled=True).reshape(NDEV * PIECE, Z)  4.47 us
    pallas_call x1, Pallas kernels, stream_early(): pl.pallas_call(early_kernel, in_specs=[VMEM, HBM] + [VMEM] * 4, out_specs...  3.97 us
    pallas_call x1, Pallas kernels, after_exchange(): pl.pallas_call(last_kernel, in_specs=[HBM if n in (3, 10) else SMEM if n...  3 us
    pallas_call x1, Pallas kernels, before_exchange(): pl.pallas_call(first_kernel, in_specs=[HBM, HBM, HBM], out_specs=[HBM] +...  2.66 us
  transfers between devices with their start and end apart: 6, of which 1 were waited for; matrix products, arithmetic and copies ran while one was open for 0% of the time, Pallas kernels for 20%

profile of v5, /device:TPU:1, one launch (start us, length us, event | category | flops | bytes accessed | tf_op | source)
XLA Modules:
  0.0 52.6 jit_solution(5689271749469806070)
XLA Ops:
  0.6 0.0 copy-start.2
  0.6 0.0 copy-start.1
  0.7 0.0 copy-start
  0.7 0.0 copy-start.3
  0.7 2.7 %before_exchange.1 = (f32[128,8,128]{2,1,0:T(8,128)}, f32[9,32,128]{2,1,0:T(8,128)S(1)}, f32[9,32,128]{2,1,0:T(8,128)S(1)}, f32[9,8,128]{2,1,0:T(8,128)S(1)}, f32[9,8,128]{2,1,0:T(8,128)S(1)}) custom-call(f32[27]{0:T(128)} %rates_ref.1, f32[27,8,32,128]{3,2,1,0:T(8,128)} %pop_hbm.3, f32[27,2,32,128]{3,2,1,0:T(8,128)} %pre_hbm.1), custom_call_target="tpu_custom_call" | custom-call | tf_op jit(solution)/shard_map/before_exchange/pallas_call | solution.py:236
  3.3 11.5 %all-to-all-start = ((f32[128,8,128]{2,1,0:T(8,128)}), f32[128,8,128]{2,1,0:T(8,128)S(1)}, u32[]{:S(2)}, u32[]{:S(2)}) async-start(f32[128,8,128]{2,1,0:T(8,128)} %get-tuple-element.19), calls=%async_computation | async-start | bytes 1048576 | tf_op jit(solution)/shard_map/all_to_all | solution.py:618
  14.8 1.5 %collective-permute-start = (f32[9,32,128]{2,1,0:T(8,128)S(1)}, f32[9,32,128]{2,1,0:T(8,128)S(1)}, u32[]{:S(2)}, u32[]{:S(2)}) collective-permute-start(f32[9,32,128]{2,1,0:T(8,128)S(1)} %get-tuple-element.23), channel_id=1, source_target_pairs={{0,4},{4,0},{8,12},{12,8},{16,20},{20,16},{24,28},{28,24},{32,36},... | collective-permute-start | bytes 442376 | tf_op jit(solution)/shard_map/ppermute | solution.py:622
  16.3 7.1 %collective-permute-start.1 = (f32[9,32,128]{2,1,0:T(8,128)S(1)}, f32[9,32,128]{2,1,0:T(8,128)S(1)}, u32[]{:S(2)}, u32[]{:S(2)}) collective-permute-start(f32[9,32,128]{2,1,0:T(8,128)S(1)} %get-tuple-element.24), channel_id=1, source_target_pairs={{0,124},{4,8},{8,4},{12,16},{16,12},{20,24},{24,20},{28,32},{32,28... | collective-permute-start | bytes 442376 | tf_op jit(solution)/shard_map/ppermute | solution.py:621
  23.4 0.9 %collective-permute-start.2 = (f32[9,8,128]{2,1,0:T(8,128)S(1)}, f32[9,8,128]{2,1,0:T(8,128)S(1)}, u32[]{:S(2)}, u32[]{:S(2)}) collective-permute-start(f32[9,8,128]{2,1,0:T(8,128)S(1)} %get-tuple-element.25), channel_id=1, source_target_pairs={{0,1},{1,0},{2,3},{3,2},{4,5},{5,4},{6,7},{7,6},{8,9},{9,8},{10,11... | collective-permute-start | bytes 110600 | tf_op jit(solution)/shard_map/ppermute | solution.py:624
  24.4 0.2 collective-permute-start.3
  24.6 0.0 copy-done.2
  24.6 0.0 copy-done.1
  24.6 0.0 copy-done
  24.6 4.9 %collision.1 = (f32[27,8,32,128]{3,2,1,0:T(8,128)}, f32[360,128]{1,0:T(8,128)S(1)}, f32[8,128]{1,0:T(8,128)S(1)}) custom-call(f32[27]{0:T(128)S(1)} %copy-done.2, s32[1,512]{1,0:T(1,128)S(1)} %bitcast.7, s32[1,512]{1,0:T(1,128)S(1)} %bitcast.8, f32[27,8,32,128]{3,2,1,0:T(8,128)} %pop_hbm.3), custom_call_target="tpu_custom_call" | custom-call | tf_op jit(solution)/shard_map/collision/pallas_call | solution.py:303
  29.5 0.0 all-to-all-done.got_ref
  29.5 0.0 copy-done.3
  29.5 1.5 %route.1 = f32[1152,128]{1,0:T(8,128)} custom-call(s32[32]{0:T(128)S(1)} %copy-done.3, f32[128,8,128]{2,1,0:T(8,128)S(1)} %all-to-all-done.got_ref, f32[8,128]{1,0:T(8,128)S(1)} %get-tuple-element.20.disc_ref), custom_call_target="tpu_custom_call" | custom-call | tf_op jit(solution)/shard_map/route/pallas_call | solution.py:348
  30.9 4.5 %all-to-all-start.1 = ((f32[128,9,1,128]{3,2,1,0:T(1,128)}), f32[128,9,1,128]{3,2,1,0:T(1,128)S(1)}, u32[]{:S(2)}, u32[]{:S(2)}) async-start(f32[128,9,1,128]{3,2,1,0:T(1,128)} %bitcast.10), calls=%async_computation.1 | async-start | bytes 1179648 | tf_op jit(solution)/shard_map/all_to_all | solution.py:626
  35.4 0.0 collective-permute-done.2.ya_ref
  35.4 0.0 collective-permute-done.3.yb_ref
  35.4 0.0 collective-permute-done.xa_ref
  35.4 0.0 collective-permute-done.1.xb_ref
  35.5 0.0 copy-start.4
  35.5 4.0 %stream_early.1 = (f32[27,8,32,128]{3,2,1,0:T(8,128)}, f32[9,32,128]{2,1,0:T(8,128)S(1)}, f32[9,32,128]{2,1,0:T(8,128)S(1)}, f32[9,8,128]{2,1,0:T(8,128)S(1)}, f...) custom-call(f32[360,128]{1,0:T(8,128)S(1)} %get-tuple-element.21.w_ref, ...), custom_call_target="tpu_custom_call" | custom-call | flops 7000000000 | bytes 1000000 | tf_op jit(solution)/shard_map/stream_early/pallas_call | solution.py:446
  39.5 10.1 %all-to-all-done.1 = f32[128,9,1,128]{3,2,1,0:T(1,128)S(1)} async-done(((f32[128,9,1,128]{3,2,1,0:T(1,128)}), f32[128,9,1,128]{3,2,1,0:T(1,128)S(1)}, u32[]{:S(2)}, u32[]{:S(2)}) %all-to-all-start.1) | async-done | bytes 589856 | tf_op jit(solution)/shard_map/all_to_all | solution.py:626
  49.5 0.0 copy-done.4
  49.6 3.0 %after_exchange.1 = (f32[27,8,32,128]{3,2,1,0:T(8,128)}, f32[1,32]{1,0:T(1,128)}) custom-call(f32[1152,128]{1,0:T(8,128)S(1)} %bitcast.6, f32[360,128]{1,0:T(8,128)S(1)} %get-tuple-element.21.w_ref, f32[1,32]{1,0:T(1,128)S(1)} %bitcast.9, f32[27,8,32,128]{3,2,1,0:T(8,128)} %get-tuple-element.22.r_hbm, ...), custom_call_target="tpu_custom_call", output_to_operand_aliasing={{0}: (10, {})} | custom-call | tf_op jit(solution)/shard_map/after_exchange/pallas_call | solution.py:589
Async XLA Ops:
  0.6 23.9 %copy-start.2 = (f32[27]{0:T(128)S(1)}, f32[27]{0:T(128)}, u32[]{:S(2)}) copy-start(f32[27]{0:T(128)} %rates_ref.1) | copy-start | bytes 328
  0.6 23.9 %copy-start.1 = (s32[512]{0:T(512)S(1)}, s32[512]{0:T(512)}, u32[]{:S(2)}) copy-start(s32[512]{0:T(512)} %param.13) | copy-start | bytes 6148
  0.7 23.9 %copy-start = (s32[512]{0:T(512)S(1)}, s32[512]{0:T(512)}, u32[]{:S(2)}) copy-start(s32[512]{0:T(512)} %param.12) | copy-start | bytes 6148
  0.7 28.8 %copy-start.3 = (s32[32]{0:T(128)S(1)}, s32[32]{0:T(128)}, u32[]{:S(2)}) copy-start(s32[32]{0:T(128)} %pairing_ref.1) | copy-start | bytes 388
  3.3 26.1 %all-to-all-start = ((f32[128,8,128]{2,1,0:T(8,128)}), f32[128,8,128]{2,1,0:T(8,128)S(1)}, u32[]{:S(2)}, u32[]{:S(2)}) async-start(f32[128,8,128]{2,1,0:T(8,128)} %get-tuple-element.19), calls=%async_computation | async-start | bytes 1048576 | tf_op jit(solution)/shard_map/all_to_all | solution.py:618
  14.8 20.6 %collective-permute-start = (f32[9,32,128]{2,1,0:T(8,128)S(1)}, f32[9,32,128]{2,1,0:T(8,128)S(1)}, u32[]{:S(2)}, u32[]{:S(2)}) collective-permute-start(f32[9,32,128]{2,1,0:T(8,128)S(1)} %get-tuple-element.23), channel_id=1, source_target_pairs={{0,4},{4,0},{8,12},{12,8},{16,20},{20,16},{24,28},{28,24},{32,36},... | collective-permute-start | bytes 442376 | tf_op jit(solution)/shard_map/ppermute | solution.py:622
  16.3 19.1 %collective-permute-start.1 = (f32[9,32,128]{2,1,0:T(8,128)S(1)}, f32[9,32,128]{2,1,0:T(8,128)S(1)}, u32[]{:S(2)}, u32[]{:S(2)}) collective-permute-start(f32[9,32,128]{2,1,0:T(8,128)S(1)} %get-tuple-element.24), channel_id=1, source_target_pairs={{0,124},{4,8},{8,4},{12,16},{16,12},{20,24},{24,20},{28,32},{32,28... | collective-permute-start | bytes 442376 | tf_op jit(solution)/shard_map/ppermute | solution.py:621
  23.4 12.0 %collective-permute-start.2 = (f32[9,8,128]{2,1,0:T(8,128)S(1)}, f32[9,8,128]{2,1,0:T(8,128)S(1)}, u32[]{:S(2)}, u32[]{:S(2)}) collective-permute-start(f32[9,8,128]{2,1,0:T(8,128)S(1)} %get-tuple-element.25), channel_id=1, source_target_pairs={{0,1},{1,0},{2,3},{3,2},{4,5},{5,4},{6,7},{7,6},{8,9},{9,8},{10,11... | collective-permute-start | bytes 110600 | tf_op jit(solution)/shard_map/ppermute | solution.py:624
  24.4 11.1 %collective-permute-start.3 = (f32[9,8,128]{2,1,0:T(8,128)S(1)}, f32[9,8,128]{2,1,0:T(8,128)S(1)}, u32[]{:S(2)}, u32[]{:S(2)}) collective-permute-start(f32[9,8,128]{2,1,0:T(8,128)S(1)} %get-tuple-element.26), channel_id=1, source_target_pairs={{0,3},{1,2},{2,1},{3,0},{4,7},{5,6},{6,5},{7,4},{8,11},{9,10},{10,... | collective-permute-start | bytes 110600 | tf_op jit(solution)/shard_map/ppermute | solution.py:623
  30.9 18.6 %all-to-all-start.1 = ((f32[128,9,1,128]{3,2,1,0:T(1,128)}), f32[128,9,1,128]{3,2,1,0:T(1,128)S(1)}, u32[]{:S(2)}, u32[]{:S(2)}) async-start(f32[128,9,1,128]{3,2,1,0:T(1,128)} %bitcast.10), calls=%async_computation.1 | async-start | bytes 1179648 | tf_op jit(solution)/shard_map/all_to_all | solution.py:626
  35.5 14.1 %copy-start.4 = (f32[32]{0:T(128)S(1)}, f32[32]{0:T(128)}, u32[]{:S(2)}) copy-start(f32[32]{0:T(128)} %param.11) | copy-start | bytes 388

commit v6 on v5

--- a/solution.py
+++ b/solution.py
@@ -251,13 +251,9 @@
     )(far(rates), far(populations), far(precursor))
 
 
-def collide_kernel(rates_ref, cols_ref, turb_ref, pop_hbm, out_hbm, w_ref, disc_ref,
-                   pop_ref, out_ref, in_sems, out_sems):
+def sums_kernel(cols_ref, turb_ref, pop_hbm, w_ref, disc_ref, pop_ref, in_sems):
     def copy_in(x):
         return pltpu.make_async_copy(pop_hbm.at[:, x], pop_ref.at[:, x], in_sems.at[x])
-
-    def copy_out(x):
-        return pltpu.make_async_copy(out_ref.at[:, x], out_hbm.at[:, x], out_sems.at[x])
 
     for x in range(XW):
         copy_in(x).start()
@@ -277,43 +273,40 @@
         jnp.where(owner, 1.0, 0.0).astype(jnp.bfloat16),
         (((1,), (1,)), ((), ())), preferred_element_type=F32)
     disc_ref[...] = jnp.zeros_like(disc_ref)
-    lane = lax.broadcasted_iota(jnp.int32, (8, Z), 1)
     profile = profile_row()
 
     def plane(x, carry):
         copy_in(x).wait()
         for q in range(4):
             rows = slice(8 * q, 8 * q + 8)
-            m = forward([pop_ref[i, x, rows, :] for i in range(27)])
-            sums = jnp.sum(m[9] / m[0] * profile, axis=1, keepdims=True)
+            part = []
+            for cx in range(3):
+                total = None
+                for cy in range(3):
+                    b = 9 * cx + 3 * cy
+                    t = pop_ref[b, x, rows, :] + pop_ref[b + 2, x, rows, :] + 4.0 * pop_ref[b + 1, x, rows, :]
+                    t = 4.0 * t if cy == 1 else t
+                    total = t if total is None else total + t
+                part.append(total)
+            ends = part[0] + part[2]
+            ux = (part[2] - part[0]) / (ends + 4.0 * part[1])
+            sums = jnp.sum(ux * profile, axis=1, keepdims=True)
             disc_ref[...] += sums * w_ref[pl.ds(pl.multiple_of((x + 1) * YW + 8 * q, 8), 8), :]
-            post = z_stream(relax(m, lambda i: rates_ref[i]), lane)
-            for i in range(27):
-                out_ref[i, x, rows, :] = post[i]
-        copy_out(x).start()
         return carry
 
     lax.fori_loop(0, XW, plane, 0)
-    for x in range(XW):
-        copy_out(x).wait()
-
-
-def collision(rates, cols, turb, populations):
-    shapes = ((27, XW, YW, Z), (W_ROWS, 128), (8, 128))
+
+
+def disc_sums(cols, turb, populations):
     return pl.pallas_call(
-        collide_kernel,
-        in_specs=[SMEM, VMEM, VMEM, HBM],
-        out_specs=[HBM] + [VMEM] * (len(shapes) - 1),
-        out_shape=[pltpu.HBM(shapes[0], F32)] + [pltpu.VMEM(shape, F32) for shape in shapes[1:]],
-        scratch_shapes=[
-            pltpu.VMEM(shapes[0], F32),
-            pltpu.VMEM(shapes[0], F32),
-            pltpu.SemaphoreType.DMA((XW,)),
-            pltpu.SemaphoreType.DMA((XW,)),
-        ],
-        name="collision",
-        compiler_params=pltpu.CompilerParams(vmem_limit_bytes=12 << 20),
-    )(rates, cols, turb, far(populations))
+        sums_kernel,
+        in_specs=[VMEM, VMEM, HBM],
+        out_specs=[VMEM] * 2,
+        out_shape=[pltpu.VMEM((W_ROWS, 128), F32), pltpu.VMEM((8, 128), F32)],
+        scratch_shapes=[pltpu.VMEM((27, XW, YW, Z), F32), pltpu.SemaphoreType.DMA((XW,))],
+        name="disc_sums",
+        compiler_params=pltpu.CompilerParams(vmem_limit_bytes=8 << 20),
+    )(cols, turb, far(populations))
 
 
 def route_kernel(pairing_ref, got_ref, disc_ref, send_hbm, send_ref, sems):
@@ -392,18 +385,28 @@
 HELD = (0, 1, 2, XW - 1)
 
 
-def early_kernel(w_ref, r_hbm, xa_ref, xb_ref, ya_ref, yb_ref, out_hbm, xm_ref, xp_ref, ym_ref, yp_ref, held_ref,
-                 used_ref, rp, low_scr, high_scr, out_scr, in_sems, held_sems, sems):
+def early_kernel(rates_ref, pop_hbm, w_ref, xa_ref, xb_ref, ya_ref, yb_ref, out_hbm, r_hbm, xm_ref, xp_ref, ym_ref,
+                 yp_ref, held_ref, used_ref, rp, low_scr, high_scr, out_scr, pop_ref, in_sems, r_sems, sems):
     first = len(BLEND)
 
     def copy_in(x):
-        return pltpu.make_async_copy(r_hbm.at[:, x], rp.at[:, x + 1, 8:40, :], in_sems.at[x])
-
-    for x in range(first, XW):
+        return pltpu.make_async_copy(pop_hbm.at[:, x], pop_ref.at[:, x], in_sems.at[x])
+
+    def copy_r(x):
+        return pltpu.make_async_copy(rp.at[:, x + 1, 8:40, :], r_hbm.at[:, x], r_sems.at[x])
+
+    for x in range(XW):
         copy_in(x).start()
-    holds = [pltpu.make_async_copy(r_hbm.at[:, x], held_ref.at[:, n], held_sems.at[n]) for n, x in enumerate(HELD)]
-    for copy in holds:
-        copy.start()
+    lane = lax.broadcasted_iota(jnp.int32, (8, Z), 1)
+
+    def collide_plane(x):
+        copy_in(x).wait()
+        for q in range(4):
+            rows = slice(8 * q, 8 * q + 8)
+            post = z_stream(collide([pop_ref[i, x, rows, :] for i in range(27)], lambda i: rates_ref[i]), lane)
+            for i in range(27):
+                rp[i, x + 1, 8 * q + 8:8 * q + 16, :] = post[i]
+
     for p in range(XW + 2):
         beside = jnp.max(w_ref[320 + p:321 + p, :] + w_ref[336 + p:337 + p, :])
         used_ref[p] = jnp.where(jnp.max(w_ref[YW * p:YW * p + YW, :]) + beside > 0.0, 1, 0)
@@ -418,12 +421,16 @@
         yp_ref[k] = low
         high_scr[k, 1:9, :] = high
         low_scr[k, 1:9, :] = low
-    copy_in(first).wait()
+    def prepare(x, carry):
+        collide_plane(x)
+        return carry
+
+    lax.fori_loop(0, first + 1, prepare, 0)
 
     def plane(x, carry):
         @pl.when(x + 1 < XW)
         def _():
-            copy_in(jnp.minimum(x + 1, XW - 1)).wait()
+            collide_plane(jnp.minimum(x + 1, XW - 1))
 
         for cx in (-1, 0, 1):
             @pl.when(jnp.logical_not(late(used_ref, x, cx)))
@@ -433,8 +440,12 @@
         return carry
 
     lax.fori_loop(first, XW, plane, 0)
-    for copy in holds:
-        copy.wait()
+    for x in range(3, XW - 1):
+        copy_r(x).start()
+    for n, x in enumerate(HELD):
+        held_ref[:, n, :, :] = rp[:, x + 1, 8:40, :]
+    for x in range(3, XW - 1):
+        copy_r(x).wait()
     for x in range(first, XW):
         for cx in (-1, 0, 1):
             @pl.when(jnp.logical_not(late(used_ref, x, cx)))
@@ -442,26 +453,27 @@
                 group_copy(out_scr, out_hbm, sems, x, cx).wait()
 
 
-def stream_early(w, r, *borders):
+def stream_early(rates, populations, w, *borders):
     return pl.pallas_call(
         early_kernel,
-        in_specs=[VMEM, HBM] + [VMEM] * 4,
-        out_specs=[HBM] + [VMEM] * 5 + [SMEM],
-        out_shape=[pltpu.HBM((27, XW, YW, Z), F32)] + [pltpu.VMEM(b.shape, F32) for b in borders]
+        in_specs=[SMEM, HBM, VMEM] + [VMEM] * 4,
+        out_specs=[HBM, HBM] + [VMEM] * 5 + [SMEM],
+        out_shape=[pltpu.HBM((27, XW, YW, Z), F32)] * 2 + [pltpu.VMEM(b.shape, F32) for b in borders]
         + [pltpu.VMEM((27, len(HELD), YW, Z), F32), jax.ShapeDtypeStruct((XW + 2,), jnp.int32)],
         scratch_shapes=[
             pltpu.VMEM((27, XW + 2, 48, Z), F32),
             pltpu.VMEM((9, 16, Z), F32),
             pltpu.VMEM((9, 16, Z), F32),
             pltpu.VMEM((27, XW, YW, Z), F32),
+            pltpu.VMEM((27, XW, YW, Z), F32),
             pltpu.SemaphoreType.DMA((XW,)),
-            pltpu.SemaphoreType.DMA((len(HELD),)),
+            pltpu.SemaphoreType.DMA((XW,)),
             pltpu.SemaphoreType.DMA((XW, 3)),
         ],
         name="stream_early",
-        compiler_params=pltpu.CompilerParams(vmem_limit_bytes=16 << 20),
+        compiler_params=pltpu.CompilerParams(vmem_limit_bytes=20 << 20),
         cost_estimate=pl.CostEstimate(flops=7 * 10**9, transcendentals=0, bytes_accessed=10**6),
-    )(near(w), far(r), *[near(b) for b in borders])
+    )(rates, far(populations), near(w), *[near(b) for b in borders])
 
 
 def last_kernel(got_ref, w_ref, loading_ref, r_hbm, xm_ref, xp_ref, ym_ref, yp_ref, held_ref, used_ref, early_hbm,
@@ -616,15 +628,15 @@
     outer = lambda n: [(i, (i + (1 if i % 2 else -1)) % n) for i in range(n)]
     send, xa, xb, ya, yb = before_exchange(rates, populations, precursor)
     got = lax.all_to_all(send, both, 0, 0, tiled=True)
-    r, w, disc = collision(
-        rates, disc_cols.reshape(1, SLOTS), disc_turb.reshape(1, SLOTS), populations)
+    w, disc = disc_sums(disc_cols.reshape(1, SLOTS), disc_turb.reshape(1, SLOTS), populations)
     xb = lax.ppermute(xb, "gx", outer(GX))
     xa = lax.ppermute(xa, "gx", inner(GX))
     yb = lax.ppermute(yb, "gy", outer(GY))
     ya = lax.ppermute(ya, "gy", inner(GY))
-    send = route(pairing, got, disc).reshape(NDEV, PIECE, 1, Z)
+    send = route(pairing, got, disc)
+    send = send.reshape(NDEV, PIECE, 1, Z)
     got = lax.all_to_all(send, both, 0, 0, tiled=True).reshape(NDEV * PIECE, Z)
-    read, *rest = stream_early(w, r, xa, xb, ya, yb)
+    read, r, *rest = stream_early(rates, populations, w, xa, xb, ya, yb)
     read, speed = after_exchange(got, w, loading.reshape(1, TURBINES), r, *rest, read)
     return read, speed.reshape(TURBINES)
 

time: 53.3 us -> 53.4 us (level); the launches traced: 52.6 us -> 53.7 us
  starting transfers between devices: 25.7 us -> 26.9 us
  waiting for transfers between devices: 10.1 us -> 9.03 us
  Pallas kernels: 16 us -> 17 us
    all_to_all x1, waiting for transfers between devices: 10.1 us -> 7.48 us  [body(): got = lax.all_to_all(send, both, 0, 0, tiled=True).reshape(NDEV * PIECE, Z)]
    all_to_all x1, waiting for transfers between devices: 0.01 us -> 1.54 us  [body(): got = lax.all_to_all(send, both, 0, 0, tiled=True)]
    all_to_all x1, starting transfers between devices: 4.47 us -> 5.66 us  [body(): got = lax.all_to_all(send, both, 0, 0, tiled=True).reshape(NDEV * PIECE, Z)]
    pallas_call x1, Pallas kernels: 3 us -> 4.14 us  [after_exchange(): pl.pallas_call(last_kernel, in_specs=[HBM if n in (3, 10) else SMEM if n...]
  transfers between devices with their start and end apart: 6 -> 6, of which waited for: 1 -> 2; matrix products, arithmetic and copies ran while one was open for 0% -> 0% of each run, Pallas kernels for 20% -> 19%
where the time goes in v6:
time: 53.4 us; the launch traced here: 53.7 us
  starting transfers between devices  26.9 us (50%)
  Pallas kernels  17 us (32%)
  waiting for transfers between devices  9.03 us (17%)
  between operations  0.76 us (1%)
    all_to_all x1, starting transfers between devices, body(): got = lax.all_to_all(send, both, 0, 0, tiled=True)  11.5 us
    all_to_all x1, waiting for transfers between devices, body(): got = lax.all_to_all(send, both, 0, 0, tiled=True).reshape(NDEV * PIECE, Z)  7.48 us
    ppermute x1, starting transfers between devices, body(): xb = lax.ppermute(xb, 'gx', outer(GX))  7.13 us
    pallas_call x1, Pallas kernels, stream_early(): pl.pallas_call(early_kernel, in_specs=[SMEM, HBM, VMEM] + [VMEM] * 4, out...  6.58 us
    all_to_all x1, starting transfers between devices, body(): got = lax.all_to_all(send, both, 0, 0, tiled=True).reshape(NDEV * PIECE, Z)  5.66 us
    pallas_call x1, Pallas kernels, after_exchange(): pl.pallas_call(last_kernel, in_specs=[HBM if n in (3, 10) else SMEM if n...  4.14 us
    pallas_call x1, Pallas kernels, before_exchange(): pl.pallas_call(first_kernel, in_specs=[HBM, HBM, HBM], out_specs=[HBM] +...  2.65 us
    pallas_call x1, Pallas kernels, disc_sums(): pl.pallas_call(sums_kernel, in_specs=[VMEM, VMEM, HBM], out_specs=[VMEM]...  2.18 us
  transfers between devices with their start and end apart: 6, of which 2 were waited for; matrix products, arithmetic and copies ran while one was open for 0% of the time, Pallas kernels for 19%

profile of v6, /device:TPU:1, one launch (start us, length us, event | category | flops | bytes accessed | tf_op | source)
XLA Modules:
  0.0 53.7 jit_solution(17310433167415069798)
XLA Ops:
  0.6 0.0 copy-start.1
  0.6 0.0 copy-start
  0.7 0.0 copy-start.2
  0.7 2.6 %before_exchange.1 = (f32[128,8,128]{2,1,0:T(8,128)}, f32[9,32,128]{2,1,0:T(8,128)S(1)}, f32[9,32,128]{2,1,0:T(8,128)S(1)}, f32[9,8,128]{2,1,0:T(8,128)S(1)}, f32[9,8,128]{2,1,0:T(8,128)S(1)}) custom-call(f32[27]{0:T(128)} %rates_ref.1, f32[27,8,32,128]{3,2,1,0:T(8,128)} %pop_hbm.5, f32[27,2,32,128]{3,2,1,0:T(8,128)} %pre_hbm.1), custom_call_target="tpu_custom_call" | custom-call | tf_op jit(solution)/shard_map/before_exchange/pallas_call | solution.py:236
  3.3 0.0 copy-start.3
  3.3 11.5 %all-to-all-start = ((f32[128,8,128]{2,1,0:T(8,128)}), f32[128,8,128]{2,1,0:T(8,128)S(1)}, u32[]{:S(2)}, u32[]{:S(2)}) async-start(f32[128,8,128]{2,1,0:T(8,128)} %get-tuple-element.19), calls=%async_computation | async-start | bytes 1048576 | tf_op jit(solution)/shard_map/all_to_all | solution.py:630
  14.8 1.5 %collective-permute-start = (f32[9,32,128]{2,1,0:T(8,128)S(1)}, f32[9,32,128]{2,1,0:T(8,128)S(1)}, u32[]{:S(2)}, u32[]{:S(2)}) collective-permute-start(f32[9,32,128]{2,1,0:T(8,128)S(1)} %get-tuple-element.22), channel_id=1, source_target_pairs={{0,4},{4,0},{8,12},{12,8},{16,20},{20,16},{24,28},{28,24},{32,36},... | collective-permute-start | bytes 442376 | tf_op jit(solution)/shard_map/ppermute | solution.py:633
  16.3 7.1 %collective-permute-start.1 = (f32[9,32,128]{2,1,0:T(8,128)S(1)}, f32[9,32,128]{2,1,0:T(8,128)S(1)}, u32[]{:S(2)}, u32[]{:S(2)}) collective-permute-start(f32[9,32,128]{2,1,0:T(8,128)S(1)} %get-tuple-element.23), channel_id=1, source_target_pairs={{0,124},{4,8},{8,4},{12,16},{16,12},{20,24},{24,20},{28,32},{32,28... | collective-permute-start | bytes 442376 | tf_op jit(solution)/shard_map/ppermute | solution.py:632
  23.4 0.9 %collective-permute-start.2 = (f32[9,8,128]{2,1,0:T(8,128)S(1)}, f32[9,8,128]{2,1,0:T(8,128)S(1)}, u32[]{:S(2)}, u32[]{:S(2)}) collective-permute-start(f32[9,8,128]{2,1,0:T(8,128)S(1)} %get-tuple-element.24), channel_id=1, source_target_pairs={{0,1},{1,0},{2,3},{3,2},{4,5},{5,4},{6,7},{7,6},{8,9},{9,8},{10,11... | collective-permute-start | bytes 110600 | tf_op jit(solution)/shard_map/ppermute | solution.py:635
  24.4 0.2 collective-permute-start.3
  24.5 0.0 copy-done.1
  24.5 0.0 copy-done
  24.6 2.2 %disc_sums.1 = (f32[360,128]{1,0:T(8,128)S(1)}, f32[8,128]{1,0:T(8,128)S(1)}) custom-call(s32[1,512]{1,0:T(1,128)S(1)} %bitcast.7, s32[1,512]{1,0:T(1,128)S(1)} %bitcast.8, f32[27,8,32,128]{3,2,1,0:T(8,128)} %pop_hbm.5), custom_call_target="tpu_custom_call" | custom-call | tf_op jit(solution)/shard_map/disc_sums/pallas_call | solution.py:301
  26.7 1.5 %all-to-all-done.got_ref = f32[128,8,128]{2,1,0:T(8,128)S(1)} async-done(((f32[128,8,128]{2,1,0:T(8,128)}), f32[128,8,128]{2,1,0:T(8,128)S(1)}, u32[]{:S(2)}, u32[]{:S(2)}) %all-to-all-start) | async-done | bytes 524320 | tf_op jit(solution)/shard_map/all_to_all | solution.py:630
  28.3 0.0 copy-done.2
  28.3 1.4 %route.1 = f32[1152,128]{1,0:T(8,128)} custom-call(s32[32]{0:T(128)S(1)} %copy-done.2, f32[128,8,128]{2,1,0:T(8,128)S(1)} %all-to-all-done.got_ref, f32[8,128]{1,0:T(8,128)S(1)} %get-tuple-element.20.disc_ref), custom_call_target="tpu_custom_call" | custom-call | tf_op jit(solution)/shard_map/route/pallas_call | solution.py:341
  29.7 5.7 %all-to-all-start.1 = ((f32[128,9,1,128]{3,2,1,0:T(1,128)}), f32[128,9,1,128]{3,2,1,0:T(1,128)S(1)}, u32[]{:S(2)}, u32[]{:S(2)}) async-start(f32[128,9,1,128]{3,2,1,0:T(1,128)} %bitcast.10), calls=%async_computation.1 | async-start | bytes 1179648 | tf_op jit(solution)/shard_map/all_to_all | solution.py:638
  35.4 0.0 collective-permute-done.2.ya_ref
  35.4 0.0 collective-permute-done.3.yb_ref
  35.4 0.0 collective-permute-done.xa_ref
  35.4 0.0 collective-permute-done.1.xb_ref
  35.5 0.0 copy-done.3
  35.5 0.0 copy-start.4
  35.5 6.6 %stream_early.1 = (f32[27,8,32,128]{3,2,1,0:T(8,128)}, f32[27,8,32,128]{3,2,1,0:T(8,128)}, f32[9,32,128]{2,1,0:T(8,128)S(1)}, f32[9,32,128]{2,1,0:T(8,128)S(1)},...) custom-call(f32[27]{0:T(128)S(1)} %copy-done.3, ...), custom_call_target="tpu_custom_call" | custom-call | flops 7000000000 | bytes 1000000 | tf_op jit(solution)/shard_map/stream_early/pallas_call | solution.py:457
  42.1 7.5 %all-to-all-done.1 = f32[128,9,1,128]{3,2,1,0:T(1,128)S(1)} async-done(((f32[128,9,1,128]{3,2,1,0:T(1,128)}), f32[128,9,1,128]{3,2,1,0:T(1,128)S(1)}, u32[]{:S(2)}, u32[]{:S(2)}) %all-to-all-start.1) | async-done | bytes 589856 | tf_op jit(solution)/shard_map/all_to_all | solution.py:638
  49.5 0.0 copy-done.4
  49.5 4.1 %after_exchange.1 = (f32[27,8,32,128]{3,2,1,0:T(8,128)}, f32[1,32]{1,0:T(1,128)}) custom-call(f32[1152,128]{1,0:T(8,128)S(1)} %bitcast.6, f32[360,128]{1,0:T(8,128)S(1)} %get-tuple-element.21.w_ref, f32[1,32]{1,0:T(1,128)S(1)} %bitcast.9, f32[27,8,32,128]{3,2,1,0:T(8,128)} %get-tuple-element.26.r_hbm, ...), custom_call_target="tpu_custom_call", output_to_operand_aliasing={{0}: (10, {})} | custom-call | tf_op jit(solution)/shard_map/after_exchange/pallas_call | solution.py:601
Async XLA Ops:
  0.6 23.9 %copy-start.1 = (s32[512]{0:T(512)S(1)}, s32[512]{0:T(512)}, u32[]{:S(2)}) copy-start(s32[512]{0:T(512)} %param.13) | copy-start | bytes 6148
  0.6 23.9 %copy-start = (s32[512]{0:T(512)S(1)}, s32[512]{0:T(512)}, u32[]{:S(2)}) copy-start(s32[512]{0:T(512)} %param.12) | copy-start | bytes 6148
  0.7 27.6 %copy-start.2 = (s32[32]{0:T(128)S(1)}, s32[32]{0:T(128)}, u32[]{:S(2)}) copy-start(s32[32]{0:T(128)} %pairing_ref.1) | copy-start | bytes 388
  3.3 32.1 %copy-start.3 = (f32[27]{0:T(128)S(1)}, f32[27]{0:T(128)}, u32[]{:S(2)}) copy-start(f32[27]{0:T(128)} %rates_ref.1) | copy-start | bytes 328
  3.3 24.9 %all-to-all-start = ((f32[128,8,128]{2,1,0:T(8,128)}), f32[128,8,128]{2,1,0:T(8,128)S(1)}, u32[]{:S(2)}, u32[]{:S(2)}) async-start(f32[128,8,128]{2,1,0:T(8,128)} %get-tuple-element.19), calls=%async_computation | async-start | bytes 1048576 | tf_op jit(solution)/shard_map/all_to_all | solution.py:630
  14.8 20.6 %collective-permute-start = (f32[9,32,128]{2,1,0:T(8,128)S(1)}, f32[9,32,128]{2,1,0:T(8,128)S(1)}, u32[]{:S(2)}, u32[]{:S(2)}) collective-permute-start(f32[9,32,128]{2,1,0:T(8,128)S(1)} %get-tuple-element.22), channel_id=1, source_target_pairs={{0,4},{4,0},{8,12},{12,8},{16,20},{20,16},{24,28},{28,24},{32,36},... | collective-permute-start | bytes 442376 | tf_op jit(solution)/shard_map/ppermute | solution.py:633
  16.3 19.1 %collective-permute-start.1 = (f32[9,32,128]{2,1,0:T(8,128)S(1)}, f32[9,32,128]{2,1,0:T(8,128)S(1)}, u32[]{:S(2)}, u32[]{:S(2)}) collective-permute-start(f32[9,32,128]{2,1,0:T(8,128)S(1)} %get-tuple-element.23), channel_id=1, source_target_pairs={{0,124},{4,8},{8,4},{12,16},{16,12},{20,24},{24,20},{28,32},{32,28... | collective-permute-start | bytes 442376 | tf_op jit(solution)/shard_map/ppermute | solution.py:632
  23.4 12.0 %collective-permute-start.2 = (f32[9,8,128]{2,1,0:T(8,128)S(1)}, f32[9,8,128]{2,1,0:T(8,128)S(1)}, u32[]{:S(2)}, u32[]{:S(2)}) collective-permute-start(f32[9,8,128]{2,1,0:T(8,128)S(1)} %get-tuple-element.24), channel_id=1, source_target_pairs={{0,1},{1,0},{2,3},{3,2},{4,5},{5,4},{6,7},{7,6},{8,9},{9,8},{10,11... | collective-permute-start | bytes 110600 | tf_op jit(solution)/shard_map/ppermute | solution.py:635
  24.4 11.1 %collective-permute-start.3 = (f32[9,8,128]{2,1,0:T(8,128)S(1)}, f32[9,8,128]{2,1,0:T(8,128)S(1)}, u32[]{:S(2)}, u32[]{:S(2)}) collective-permute-start(f32[9,8,128]{2,1,0:T(8,128)S(1)} %get-tuple-element.25), channel_id=1, source_target_pairs={{0,3},{1,2},{2,1},{3,0},{4,7},{5,6},{6,5},{7,4},{8,11},{9,10},{10,... | collective-permute-start | bytes 110600 | tf_op jit(solution)/shard_map/ppermute | solution.py:634
  29.7 19.8 %all-to-all-start.1 = ((f32[128,9,1,128]{3,2,1,0:T(1,128)}), f32[128,9,1,128]{3,2,1,0:T(1,128)S(1)}, u32[]{:S(2)}, u32[]{:S(2)}) async-start(f32[128,9,1,128]{3,2,1,0:T(1,128)} %bitcast.10), calls=%async_computation.1 | async-start | bytes 1179648 | tf_op jit(solution)/shard_map/all_to_all | solution.py:638
  35.5 14.1 %copy-start.4 = (f32[32]{0:T(128)S(1)}, f32[32]{0:T(128)}, u32[]{:S(2)}) copy-start(f32[32]{0:T(128)} %param.11) | copy-start | bytes 388

commit v7 on v5

--- a/solution.py
+++ b/solution.py
@@ -619,6 +619,7 @@
     r, w, disc = collision(
         rates, disc_cols.reshape(1, SLOTS), disc_turb.reshape(1, SLOTS), populations)
     xb = lax.ppermute(xb, "gx", outer(GX))
+    disc, xa = lax.optimization_barrier((disc, xa))
     xa = lax.ppermute(xa, "gx", inner(GX))
     yb = lax.ppermute(yb, "gy", outer(GY))
     ya = lax.ppermute(ya, "gy", inner(GY))

time: 53.3 us -> 52.8 us (level)
    ppermute x1, starting transfers between devices: 1.47 us -> 0.09 us  [body(): xa = lax.ppermute(xa, 'gx', inner(GX))]
    ppermute x1, starting transfers between devices: 7.13 us -> 8.08 us  [body(): xb = lax.ppermute(xb, 'gx', outer(GX))]
    all_to_all x1, starting transfers between devices: 4.47 us -> 5.04 us  [body(): got = lax.all_to_all(send, both, 0, 0, tiled=True).reshape(NDEV * PIECE, Z)]
where the time goes in v7:
time: 52.8 us; the launch traced here: 52.6 us
  starting transfers between devices  25.7 us (49%)
  Pallas kernels  16 us (30%)
  waiting for transfers between devices  10.1 us (19%)
  between operations  0.76 us (1%)
    all_to_all x1, starting transfers between devices, body(): got = lax.all_to_all(send, both, 0, 0, tiled=True)  11.5 us
    all_to_all x1, waiting for transfers between devices, body(): got = lax.all_to_all(send, both, 0, 0, tiled=True).reshape(NDEV * PIECE, Z)  10.1 us
    ppermute x1, starting transfers between devices, body(): xb = lax.ppermute(xb, 'gx', outer(GX))  8.08 us
    all_to_all x1, starting transfers between devices, body(): got = lax.all_to_all(send, both, 0, 0, tiled=True).reshape(NDEV * PIECE, Z)  5.04 us
    pallas_call x1, Pallas kernels, collision(): pl.pallas_call(collide_kernel, in_specs=[SMEM, VMEM, VMEM, HBM], out_spec...  4.89 us
    pallas_call x1, Pallas kernels, stream_early(): pl.pallas_call(early_kernel, in_specs=[VMEM, HBM] + [VMEM] * 4, out_specs...  3.97 us
    pallas_call x1, Pallas kernels, after_exchange(): pl.pallas_call(last_kernel, in_specs=[HBM if n in (3, 10) else SMEM if n...  3 us
    pallas_call x1, Pallas kernels, before_exchange(): pl.pallas_call(first_kernel, in_specs=[HBM, HBM, HBM], out_specs=[HBM] +...  2.66 us
  transfers between devices with their start and end apart: 6, of which 1 were waited for; matrix products, arithmetic and copies ran while one was open for 0% of the time, Pallas kernels for 20%

profile of v7, /device:TPU:1, one launch (start us, length us, event | category | flops | bytes accessed | tf_op | source)
XLA Modules:
  0.0 52.6 jit_solution(14447552120130005947)
XLA Ops:
  0.6 0.0 copy-start.2
  0.6 0.0 copy-start.1
  0.7 0.0 copy-start
  0.7 0.0 copy-start.3
  0.7 2.7 %before_exchange.1 = (f32[128,8,128]{2,1,0:T(8,128)}, f32[9,32,128]{2,1,0:T(8,128)S(1)}, f32[9,32,128]{2,1,0:T(8,128)S(1)}, f32[9,8,128]{2,1,0:T(8,128)S(1)}, f32[9,8,128]{2,1,0:T(8,128)S(1)}) custom-call(f32[27]{0:T(128)} %rates_ref.1, f32[27,8,32,128]{3,2,1,0:T(8,128)} %pop_hbm.3, f32[27,2,32,128]{3,2,1,0:T(8,128)} %pre_hbm.1), custom_call_target="tpu_custom_call" | custom-call | tf_op jit(solution)/shard_map/before_exchange/pallas_call | solution.py:236
  3.3 11.5 %all-to-all-start = ((f32[128,8,128]{2,1,0:T(8,128)}), f32[128,8,128]{2,1,0:T(8,128)S(1)}, u32[]{:S(2)}, u32[]{:S(2)}) async-start(f32[128,8,128]{2,1,0:T(8,128)} %get-tuple-element.21), calls=%async_computation | async-start | bytes 1048576 | tf_op jit(solution)/shard_map/all_to_all | solution.py:618
  14.8 8.1 %collective-permute-start.1 = (f32[9,32,128]{2,1,0:T(8,128)S(1)}, f32[9,32,128]{2,1,0:T(8,128)S(1)}, u32[]{:S(2)}, u32[]{:S(2)}) collective-permute-start(f32[9,32,128]{2,1,0:T(8,128)S(1)} %get-tuple-element.28), channel_id=1, source_target_pairs={{0,124},{4,8},{8,4},{12,16},{16,12},{20,24},{24,20},{28,32},{32,28... | collective-permute-start | bytes 442376 | tf_op jit(solution)/shard_map/ppermute | solution.py:621
  22.9 0.0 copy-done.2
  22.9 0.0 copy-done.1
  22.9 0.0 copy-done
  22.9 4.9 %collision.1 = (f32[27,8,32,128]{3,2,1,0:T(8,128)}, f32[360,128]{1,0:T(8,128)S(1)}, f32[8,128]{1,0:T(8,128)S(1)}) custom-call(f32[27]{0:T(128)S(1)} %copy-done.2, s32[1,512]{1,0:T(1,128)S(1)} %bitcast.7, s32[1,512]{1,0:T(1,128)S(1)} %bitcast.8, f32[27,8,32,128]{3,2,1,0:T(8,128)} %pop_hbm.3), custom_call_target="tpu_custom_call" | custom-call | tf_op jit(solution)/shard_map/collision/pallas_call | solution.py:303
  27.8 0.1 collective-permute-start
  27.9 0.7 %collective-permute-start.2 = (f32[9,8,128]{2,1,0:T(8,128)S(1)}, f32[9,8,128]{2,1,0:T(8,128)S(1)}, u32[]{:S(2)}, u32[]{:S(2)}) collective-permute-start(f32[9,8,128]{2,1,0:T(8,128)S(1)} %get-tuple-element.29), channel_id=1, source_target_pairs={{0,1},{1,0},{2,3},{3,2},{4,5},{5,4},{6,7},{7,6},{8,9},{9,8},{10,11... | collective-permute-start | bytes 110600 | tf_op jit(solution)/shard_map/ppermute | solution.py:625
  28.7 0.3 collective-permute-start.3
  28.9 0.0 all-to-all-done.got_ref
  28.9 0.0 copy-done.3
  28.9 1.5 %route.1 = f32[1152,128]{1,0:T(8,128)} custom-call(s32[32]{0:T(128)S(1)} %copy-done.3, f32[128,8,128]{2,1,0:T(8,128)S(1)} %all-to-all-done.got_ref, f32[8,128]{1,0:T(8,128)S(1)} %get-tuple-element.24.disc_ref), custom_call_target="tpu_custom_call" | custom-call | tf_op jit(solution)/shard_map/route/pallas_call | solution.py:348
  30.4 5.0 %all-to-all-start.1 = ((f32[128,9,1,128]{3,2,1,0:T(1,128)}), f32[128,9,1,128]{3,2,1,0:T(1,128)S(1)}, u32[]{:S(2)}, u32[]{:S(2)}) async-start(f32[128,9,1,128]{3,2,1,0:T(1,128)} %bitcast.10), calls=%async_computation.1 | async-start | bytes 1179648 | tf_op jit(solution)/shard_map/all_to_all | solution.py:627
  35.4 0.0 collective-permute-done.2.ya_ref
  35.5 0.0 collective-permute-done.3.yb_ref
  35.5 0.0 collective-permute-done.1.xb_ref
  35.5 0.0 collective-permute-done.xa_ref
  35.5 0.0 copy-start.4
  35.5 4.0 %stream_early.1 = (f32[27,8,32,128]{3,2,1,0:T(8,128)}, f32[9,32,128]{2,1,0:T(8,128)S(1)}, f32[9,32,128]{2,1,0:T(8,128)S(1)}, f32[9,8,128]{2,1,0:T(8,128)S(1)}, f...) custom-call(f32[360,128]{1,0:T(8,128)S(1)} %get-tuple-element.25.w_ref, ...), custom_call_target="tpu_custom_call" | custom-call | flops 7000000000 | bytes 1000000 | tf_op jit(solution)/shard_map/stream_early/pallas_call | solution.py:446
  39.5 10.1 %all-to-all-done.1 = f32[128,9,1,128]{3,2,1,0:T(1,128)S(1)} async-done(((f32[128,9,1,128]{3,2,1,0:T(1,128)}), f32[128,9,1,128]{3,2,1,0:T(1,128)S(1)}, u32[]{:S(2)}, u32[]{:S(2)}) %all-to-all-start.1) | async-done | bytes 589856 | tf_op jit(solution)/shard_map/all_to_all | solution.py:627
  49.6 0.0 copy-done.4
  49.6 3.0 %after_exchange.1 = (f32[27,8,32,128]{3,2,1,0:T(8,128)}, f32[1,32]{1,0:T(1,128)}) custom-call(f32[1152,128]{1,0:T(8,128)S(1)} %bitcast.6, f32[360,128]{1,0:T(8,128)S(1)} %get-tuple-element.25.w_ref, f32[1,32]{1,0:T(1,128)S(1)} %bitcast.9, f32[27,8,32,128]{3,2,1,0:T(8,128)} %get-tuple-element.26.r_hbm, ...), custom_call_target="tpu_custom_call", output_to_operand_aliasing={{0}: (10, {})} | custom-call | tf_op jit(solution)/shard_map/after_exchange/pallas_call | solution.py:589
Async XLA Ops:
  0.6 22.3 %copy-start.2 = (f32[27]{0:T(128)S(1)}, f32[27]{0:T(128)}, u32[]{:S(2)}) copy-start(f32[27]{0:T(128)} %rates_ref.1) | copy-start | bytes 328
  0.6 22.3 %copy-start.1 = (s32[512]{0:T(512)S(1)}, s32[512]{0:T(512)}, u32[]{:S(2)}) copy-start(s32[512]{0:T(512)} %param.13) | copy-start | bytes 6148
  0.7 22.3 %copy-start = (s32[512]{0:T(512)S(1)}, s32[512]{0:T(512)}, u32[]{:S(2)}) copy-start(s32[512]{0:T(512)} %param.12) | copy-start | bytes 6148
  0.7 28.3 %copy-start.3 = (s32[32]{0:T(128)S(1)}, s32[32]{0:T(128)}, u32[]{:S(2)}) copy-start(s32[32]{0:T(128)} %pairing_ref.1) | copy-start | bytes 388
  3.3 25.6 %all-to-all-start = ((f32[128,8,128]{2,1,0:T(8,128)}), f32[128,8,128]{2,1,0:T(8,128)S(1)}, u32[]{:S(2)}, u32[]{:S(2)}) async-start(f32[128,8,128]{2,1,0:T(8,128)} %get-tuple-element.21), calls=%async_computation | async-start | bytes 1048576 | tf_op jit(solution)/shard_map/all_to_all | solution.py:618
  14.8 20.6 %collective-permute-start.1 = (f32[9,32,128]{2,1,0:T(8,128)S(1)}, f32[9,32,128]{2,1,0:T(8,128)S(1)}, u32[]{:S(2)}, u32[]{:S(2)}) collective-permute-start(f32[9,32,128]{2,1,0:T(8,128)S(1)} %get-tuple-element.28), channel_id=1, source_target_pairs={{0,124},{4,8},{8,4},{12,16},{16,12},{20,24},{24,20},{28,32},{32,28... | collective-permute-start | bytes 442376 | tf_op jit(solution)/shard_map/ppermute | solution.py:621
  27.8 7.6 %collective-permute-start = (f32[9,32,128]{2,1,0:T(8,128)S(1)}, f32[9,32,128]{2,1,0:T(8,128)S(1)}, u32[]{:S(2)}, u32[]{:S(2)}) collective-permute-start(f32[9,32,128]{2,1,0:T(8,128)S(1)} %get-tuple-element.27), channel_id=1, source_target_pairs={{0,4},{4,0},{8,12},{12,8},{16,20},{20,16},{24,28},{28,24},{32,36},... | collective-permute-start | bytes 442376 | tf_op jit(solution)/shard_map/ppermute | solution.py:623
  27.9 7.5 %collective-permute-start.2 = (f32[9,8,128]{2,1,0:T(8,128)S(1)}, f32[9,8,128]{2,1,0:T(8,128)S(1)}, u32[]{:S(2)}, u32[]{:S(2)}) collective-permute-start(f32[9,8,128]{2,1,0:T(8,128)S(1)} %get-tuple-element.29), channel_id=1, source_target_pairs={{0,1},{1,0},{2,3},{3,2},{4,5},{5,4},{6,7},{7,6},{8,9},{9,8},{10,11... | collective-permute-start | bytes 110600 | tf_op jit(solution)/shard_map/ppermute | solution.py:625
  28.7 6.8 %collective-permute-start.3 = (f32[9,8,128]{2,1,0:T(8,128)S(1)}, f32[9,8,128]{2,1,0:T(8,128)S(1)}, u32[]{:S(2)}, u32[]{:S(2)}) collective-permute-start(f32[9,8,128]{2,1,0:T(8,128)S(1)} %get-tuple-element.30), channel_id=1, source_target_pairs={{0,3},{1,2},{2,1},{3,0},{4,7},{5,6},{6,5},{7,4},{8,11},{9,10},{10,... | collective-permute-start | bytes 110600 | tf_op jit(solution)/shard_map/ppermute | solution.py:624
  30.4 19.2 %all-to-all-start.1 = ((f32[128,9,1,128]{3,2,1,0:T(1,128)}), f32[128,9,1,128]{3,2,1,0:T(1,128)S(1)}, u32[]{:S(2)}, u32[]{:S(2)}) async-start(f32[128,9,1,128]{3,2,1,0:T(1,128)} %bitcast.10), calls=%async_computation.1 | async-start | bytes 1179648 | tf_op jit(solution)/shard_map/all_to_all | solution.py:627
  35.5 14.1 %copy-start.4 = (f32[32]{0:T(128)S(1)}, f32[32]{0:T(128)}, u32[]{:S(2)}) copy-start(f32[32]{0:T(128)} %param.11) | copy-start | bytes 388
